TPU v7x, 32 devices: a whole 2x2x4 slice. The times are simulated.
32 devices in a mesh: dp: 16 (over z, y, x), tensor: 2 (over core).
Axes of the slice: x: 2, y: 2, z: 4, core: 2. Of those that a mesh axis runs over, the one named last changes fastest.
Arguments:
- tokens: bfloat16 [4096, 1024], P('dp'), may hold values from -6 to 6
- encoder_states: bfloat16 [4096, 1024], P('dp'), may hold values from -6 to 6
- cotangent: bfloat16 [4096, 1024], P('dp'), may hold values from -6 to 6
- lengths: int32 [16], replicated, may hold values from 1 to 256, 3686 in all
- deal_order: int32 [16], replicated, may hold values from 0 to 15, each once
- bucket_index: int32 [256], replicated, may hold values from 0 to 31, as said below
- rel_table: float32 [32, 16], P(None, 'tensor'), may hold values from -4 to 4
- gain_self: float32 [1024], replicated, may hold values from 0.5 to 1.5
- self_query: bfloat16 [1024, 1024], P('dp', 'tensor'), may hold values from -0.046875 to 0.046875
- self_key: bfloat16 [1024, 1024], P('dp', 'tensor'), may hold values from -0.1875 to 0.1875
- self_value: bfloat16 [1024, 1024], P('dp', 'tensor'), may hold values from -0.1875 to 0.1875
- self_output: bfloat16 [1024, 1024], P('dp', 'tensor'), may hold values from -0.75 to 0.75
- gain_cross: float32 [1024], replicated, may hold values from 0.5 to 1.5
- cross_query: bfloat16 [1024, 1024], P('dp', 'tensor'), may hold values from -0.046875 to 0.046875
- cross_key: bfloat16 [1024, 1024], P('dp', 'tensor'), may hold values from -0.1875 to 0.1875
- cross_value: bfloat16 [1024, 1024], P('dp', 'tensor'), may hold values from -0.1875 to 0.1875
- cross_output: bfloat16 [1024, 1024], P('dp', 'tensor'), may hold values from -0.75 to 0.75
- gain_feed: float32 [1024], replicated, may hold values from 0.5 to 1.5
- feed_gate: bfloat16 [1024, 2816], P('dp', 'tensor'), may hold values from -0.1875 to 0.1875
- feed_value: bfloat16 [1024, 2816], P('dp', 'tensor'), may hold values from -0.1875 to 0.1875
- feed_output: bfloat16 [1024, 2816], P('dp', 'tensor'), may hold values from -0.109375 to 0.109375
Outputs:
- layer_out: bfloat16 [4096, 1024], P('dp')
- tokens_grad: bfloat16 [4096, 1024], P('dp')
- encoder_grad: bfloat16 [4096, 1024], P(('dp', 'tensor'))
- rel_table_grad: float32 [32, 16], P(None, 'tensor')
- gain_self_grad: float32 [1024], replicated
- self_query_grad: float32 [1024, 1024], P('dp', 'tensor')
- self_key_grad: float32 [1024, 1024], P('dp', 'tensor')
- self_value_grad: float32 [1024, 1024], P('dp', 'tensor')
- self_output_grad: float32 [1024, 1024], P('dp', 'tensor')
- gain_cross_grad: float32 [1024], replicated
- cross_query_grad: float32 [1024, 1024], P('dp', 'tensor')
- cross_key_grad: float32 [1024, 1024], P('dp', 'tensor')
- cross_value_grad: float32 [1024, 1024], P('dp', 'tensor')
- cross_output_grad: float32 [1024, 1024], P('dp', 'tensor')
- gain_feed_grad: float32 [1024], replicated
- feed_gate_grad: float32 [1024, 2816], P('dp', 'tensor')
- feed_value_grad: float32 [1024, 2816], P('dp', 'tensor')
- feed_output_grad: float32 [1024, 2816], P('dp', 'tensor')
Inputs may be any that keep to these rules, and one draw needn't show every extreme that they name: `lengths`: one sequence has exactly 256 tokens. `deal_order`: each dp index receives exactly one sequence. `bucket_index`: never falls as the distance grows; distance 0 has bucket 0 and distance 256 - 1 has bucket 32 - 1.
All inputs are finite; a program needn't handle non-finite values.
Results may differ from a plain program's by a relative error of at most 0.04.
Values may be sent and summed in bfloat16 or wider, within the bound.
No kernel may reach another device: no remote copies, remote signals or barrier semaphores. Data moves between devices by JAX's collectives and lax.ppermute only.
A program may use at most 192 MiB of HBM per device.

v0:
```python
import functools

import jax
import jax.numpy as jnp
import numpy as np
from jax import lax
from jax.experimental import pallas as pl
from jax.experimental.pallas import tpu as pltpu
from jax.sharding import PartitionSpec as P

EPSILON = 1e-06
MASKED = -1e30
HIGHEST = lax.Precision.HIGHEST
HEAD = 64
PAIR = 2 * HEAD
LOW = jnp.bfloat16
FULL = jnp.float32


def upper_masks(devices):
    if devices == 16:
        return [12, 4]
    return [1 << bit for bit in range(devices.bit_length() - 2, 1, -1)]


def block_offsets(masks):
    offsets = [0]
    for mask in masks:
        offsets = offsets + [offset ^ mask for offset in offsets]
    return offsets


def swap_dp(value, mask, devices):
    return lax.ppermute(value, "dp", [(one, one ^ mask) for one in range(devices)])


def swap_tensor(value):
    return lax.ppermute(value, "tensor", [(0, 1), (1, 0)])


def total_small(value, devices):
    mask = 1
    while mask < devices:
        value = value + swap_dp(value, mask, devices)
        mask = 2 * mask
    return value


def product_plain(left, right):
    return jnp.dot(left, right, preferred_element_type=FULL)


def product_right(left, right):
    return lax.dot_general(left, right, (((1,), (1,)), ((), ())), preferred_element_type=FULL)


def product_left(left, right):
    return lax.dot_general(left, right, (((0,), (0,)), ((), ())), preferred_element_type=FULL)


def quarter(ref, number):
    width = ref.shape[1] // 4
    return ref[:, number * width : (number + 1) * width]


def sides(refs):
    own, x_part, y_part, left, right = refs
    rows = left.shape[0]
    return (
        [own.at[:rows], x_part.at[:rows], y_part.at[:rows], left],
        [own.at[rows:], x_part.at[rows:], y_part.at[rows:], right],
    )


def after(value, *earlier):
    return lax.optimization_barrier((value, *earlier))[0]


def project_in(value_ref, pieces, columns):
    total = None
    for number, piece in enumerate(pieces):
        part = product_plain(quarter(value_ref, number), piece[:, columns])
        total = part if total is None else total + part
    return total


def inverse_root(value):
    return lax.rsqrt(jnp.mean(value * value, axis=-1, keepdims=True) + EPSILON)


def norm_backward(value, gain, upstream):
    root = inverse_root(value)
    weighted = upstream * gain
    inner_mean = jnp.mean(weighted * value, axis=-1, keepdims=True)
    grad = root * weighted - value * (root * root * root) * inner_mean
    return grad, jnp.sum(upstream * value * root, axis=0, keepdims=True)


def both(mine_ref, other_ref):
    return mine_ref[...].astype(FULL) + other_ref[...].astype(FULL)


def valid_column(length_ref, rows):
    return (lax.broadcasted_iota(jnp.int32, (rows, 1), 0) < length_ref[0]).astype(FULL)


def toeplitz_bias(row, rows):
    wide = jnp.broadcast_to(row, (rows, row.shape[1]))
    return pltpu.roll(wide, 0, 1, stride=1, stride_axis=0)[:, :rows]


def head_half(value, side, lanes):
    keep = lanes < HEAD if side == 0 else lanes >= HEAD
    return jnp.where(keep, value, jnp.zeros_like(value))


def masked_scores(query, key, length_ref, bias_ref, head):
    scores = product_right(query, key)
    if bias_ref is None:
        return scores
    rows, columns = scores.shape
    scores = scores + toeplitz_bias(bias_ref[pl.ds(head, 1), :], rows)
    at_row = lax.broadcasted_iota(jnp.int32, (rows, columns), 0)
    at_column = lax.broadcasted_iota(jnp.int32, (rows, columns), 1)
    allowed = (at_column <= at_row) & (at_column < length_ref[0])
    return jnp.where(allowed, scores, MASKED)


def softmax_rows(scores):
    exponent = jnp.exp(scores - jnp.max(scores, axis=-1, keepdims=True))
    return exponent / jnp.sum(exponent, axis=-1, keepdims=True)


def attention_forward(query_ref, key_ref, value_ref, out_ref, length_ref=None, bias_ref=None):
    rows, width = query_ref.shape
    lanes = lax.broadcasted_iota(jnp.int32, (rows, PAIR), 1)

    def one_pair(pair, carry):
        columns = pl.ds(pl.multiple_of(pair * PAIR, PAIR), PAIR)
        query, key, value = query_ref[:, columns], key_ref[:, columns], value_ref[:, columns]
        mixed = []
        for side in range(2):
            scores = masked_scores(
                head_half(query, side, lanes), key, length_ref, bias_ref, 2 * pair + side
            )
            mixed.append(product_plain(softmax_rows(scores).astype(LOW), value))
        out_ref[:, columns] = jnp.where(lanes < HEAD, mixed[0], mixed[1]).astype(LOW)
        return carry

    lax.fori_loop(0, width // PAIR, one_pair, 0)


def attention_backward(
    query_ref,
    key_ref,
    value_ref,
    grad_ref,
    dquery_ref,
    dkey_ref,
    dvalue_ref,
    length_ref=None,
    bias_ref=None,
    diagonal_ref=None,
):
    rows, width = query_ref.shape
    lanes = lax.broadcasted_iota(jnp.int32, (rows, PAIR), 1)
    if bias_ref is not None:
        flip = (
            lax.broadcasted_iota(jnp.int32, (rows, rows), 0)
            + lax.broadcasted_iota(jnp.int32, (rows, rows), 1)
            == rows - 1
        ).astype(LOW)

    def one_pair(pair, carry):
        columns = pl.ds(pl.multiple_of(pair * PAIR, PAIR), PAIR)
        query, key, value = query_ref[:, columns], key_ref[:, columns], value_ref[:, columns]
        grad = grad_ref[:, columns]
        dquery, dkey, dvalue = [], [], []
        for side in range(2):
            head = 2 * pair + side
            scores = masked_scores(head_half(query, side, lanes), key, length_ref, bias_ref, head)
            chance = softmax_rows(scores)
            chance_grad = product_right(head_half(grad, side, lanes), value)
            delta = jnp.sum(chance * chance_grad, axis=-1, keepdims=True)
            score_grad = (chance * (chance_grad - delta)).astype(LOW)
            dquery.append(product_plain(score_grad, key))
            dkey.append(product_left(score_grad, query))
            dvalue.append(product_left(chance.astype(LOW), grad))
            if bias_ref is not None:
                flipped = product_plain(flip, score_grad)
                wide = jnp.concatenate([flipped, jnp.zeros_like(flipped)], axis=1)
                skewed = pltpu.roll(wide, rows + 1, 1, stride=1, stride_axis=0)
                diagonal_ref[pl.ds(head, 1), :] = jnp.sum(skewed, axis=0, keepdims=True)
        left = lanes < HEAD
        dquery_ref[:, columns] = jnp.where(left, dquery[0], dquery[1]).astype(LOW)
        dkey_ref[:, columns] = jnp.where(left, dkey[0], dkey[1]).astype(LOW)
        dvalue_ref[:, columns] = jnp.where(left, dvalue[0], dvalue[1]).astype(LOW)
        return carry

    lax.fori_loop(0, width // PAIR, one_pair, 0)


def low_shape(*shape):
    return jax.ShapeDtypeStruct(shape, LOW)


def full_shape(*shape):
    return jax.ShapeDtypeStruct(shape, FULL)


def call(body, out_shape, scalars, arrays, scratch=(), flops=0):
    vmem = pl.BlockSpec(memory_space=pltpu.VMEM)
    smem = pl.BlockSpec(memory_space=pltpu.SMEM)
    return pl.pallas_call(
        body,
        out_shape=list(out_shape),
        in_specs=[smem] * len(scalars) + [vmem] * len(arrays),
        out_specs=[vmem] * len(out_shape),
        scratch_shapes=list(scratch),
        name=getattr(body, "func", body).__name__,
        cost_estimate=pl.CostEstimate(
            flops=int(flops * 1), transcendentals=0, bytes_accessed=1024
        ),
        compiler_params=pltpu.CompilerParams(vmem_limit_bytes=44 << 20),
    )(*scalars, *arrays)


def prepare_body(
    length_ref,
    tokens_ref,
    cotangent_ref,
    gains_ref,
    source_ref,
    permute_ref,
    input_ref,
    grad_ref,
    gains_out_ref,
    normed_ref,
):
    rows, width = tokens_ref.shape
    at_row = lax.broadcasted_iota(jnp.int32, (width, width), 0)
    permute_ref[...] = (at_row == source_ref[...]).astype(FULL).astype(LOW)
    permute = permute_ref[...]
    valid = valid_column(length_ref, rows)
    masked = product_plain(tokens_ref[...], permute) * valid
    input_ref[...] = masked.astype(LOW)
    grad_ref[...] = (product_plain(cotangent_ref[...], permute) * valid).astype(LOW)
    gains = gains_ref[...]
    high = gains.astype(LOW)
    middle = (gains - high.astype(FULL)).astype(LOW)
    low = (gains - high.astype(FULL) - middle.astype(FULL)).astype(LOW)
    gains_out_ref[...] = (
        product_plain(high, permute) + product_plain(middle, permute)
    ) + product_plain(low, permute)
    normed_ref[...] = (masked * inverse_root(masked) * gains_out_ref[0:1, :]).astype(LOW)


def self_forward_body(
    length_ref, bias_ref, normed_ref, *refs
):
    qk, vo = sides(refs[:5])
    query_ref, key_ref, value_ref, mixed_ref, partial_ref = refs[5:]
    inner = query_ref.shape[1]
    query_ref[...] = project_in(normed_ref, qk, slice(0, inner)).astype(LOW)
    key_ref[...] = project_in(normed_ref, qk, slice(inner, 2 * inner)).astype(LOW)
    value_ref[...] = project_in(normed_ref, vo, slice(0, inner)).astype(LOW)
    attention_forward(query_ref, key_ref, value_ref, mixed_ref, length_ref, bias_ref)
    width = partial_ref.shape[1] // 4
    for number in range(4):
        partial_ref[:, number * width : (number + 1) * width] = product_right(
            mixed_ref[...], vo[number][:, inner:]
        ).astype(LOW)


def memory_body(half_ref, other_ref, permute_ref, *refs):
    kv, _ = sides(refs[:5])
    memory_ref, key_ref, value_ref = refs[5:]
    inner = key_ref.shape[1]
    half = half_ref.shape[0]
    memory_ref[:half, :] = product_plain(half_ref[...], permute_ref[...]).astype(LOW)
    memory_ref[half:, :] = product_plain(other_ref[...], permute_ref[...]).astype(LOW)
    key_ref[...] = project_in(memory_ref, kv, slice(0, inner)).astype(LOW)
    value_ref[...] = project_in(memory_ref, kv, slice(inner, 2 * inner)).astype(LOW)


def cross_forward_body(input_ref, mine_ref, other_ref, gains_ref, key_ref, value_ref, *refs):
    _, qo = sides(refs[:5])
    hidden_ref, normed_ref, query_ref, mixed_ref, partial_ref = refs[5:]
    inner = query_ref.shape[1]
    hidden = input_ref[...].astype(FULL) + both(mine_ref, other_ref)
    hidden_ref[...] = hidden
    normed_ref[...] = (hidden * inverse_root(hidden) * gains_ref[1:2, :]).astype(LOW)
    query_ref[...] = project_in(normed_ref, qo, slice(0, inner)).astype(LOW)
    attention_forward(query_ref, key_ref, value_ref, mixed_ref)
    width = partial_ref.shape[1] // 4
    for number in range(4):
        partial_ref[:, number * width : (number + 1) * width] = product_right(
            mixed_ref[...], qo[number][:, inner:]
        ).astype(LOW)


GELU_SCALE = float(np.sqrt(2.0 / np.pi))
GELU_CUBE = 0.044715
CHUNK = 256


def feed_body(transposed, hidden_in_ref, mine_ref, other_ref, gains_ref, grad_ref, *refs):
    gate_w, lift_w = sides(refs[:5])
    down_w = refs[5:9]
    hidden_ref, partial_ref, dnormed_ref = refs[9:12]
    dgate_w, dlift_w = sides(refs[12:17])
    ddown_w = refs[17:21]
    normed_ref, normed_t_ref, grad_t_ref, down_ref, total_ref, dtotal_ref = refs[21:]
    rows, model = hidden_ref.shape
    width = model // 4
    block = width // 4
    feed = gate_w[0].shape[1]
    hidden = hidden_in_ref[...] + both(mine_ref, other_ref)
    hidden_ref[...] = hidden
    normed_ref[...] = (hidden * inverse_root(hidden) * gains_ref[2:3, :]).astype(LOW)
    normed_t_ref[...] = normed_ref[...].T
    grad_t_ref[...] = grad_ref[...].T
    for number in range(4):
        if transposed:
            for other in range(4):
                place = number * width + other * block
                down_ref[place : place + block, :] = down_w[other][
                    number * block : (number + 1) * block, :
                ]
        else:
            down_ref[number * width : (number + 1) * width, :] = down_w[number][...]
    total_ref[...] = jnp.zeros_like(total_ref)
    dtotal_ref[...] = jnp.zeros_like(dtotal_ref)

    def some_columns(columns):
        gate = project_in(normed_ref, gate_w, columns)
        lift = project_in(normed_ref, lift_w, columns)
        squared = gate * gate
        curve = jnp.tanh(GELU_SCALE * (gate + GELU_CUBE * squared * gate))
        half_up = 0.5 * (1.0 + curve)
        activated = gate * half_up
        product = (activated * lift).astype(LOW)
        down = down_ref[:, columns]
        dproduct = product_plain(grad_ref[...], down).astype(LOW).astype(FULL)
        slope = half_up + 0.5 * gate * (1.0 - curve * curve) * (
            GELU_SCALE * (1.0 + 3.0 * GELU_CUBE * squared)
        )
        dgate = (dproduct * lift * slope).astype(LOW)
        dlift = (dproduct * activated).astype(LOW)
        total_ref[...] += product_right(product, down)
        for number in range(4):
            part = slice(number * width, (number + 1) * width)
            normed_t = normed_t_ref[part, :]
            dgate_w[number][:, columns] = product_plain(normed_t, dgate).astype(LOW)
            dlift_w[number][:, columns] = product_plain(normed_t, dlift).astype(LOW)
            ddown = product_plain(grad_t_ref[part, :], product).astype(LOW)
            if transposed:
                for other in range(4):
                    ddown_w[other][number * block : (number + 1) * block, columns] = ddown[
                        other * block : (other + 1) * block, :
                    ]
            else:
                ddown_w[number][:, columns] = ddown
            dtotal_ref[:, part] += product_right(
                dgate, gate_w[number][:, columns]
            ) + product_right(dlift, lift_w[number][:, columns])

    def one_chunk(chunk, carry):
        some_columns(pl.ds(pl.multiple_of(chunk * CHUNK, CHUNK), CHUNK))
        return carry

    whole = feed // CHUNK
    lax.fori_loop(0, whole, one_chunk, 0)
    if feed % CHUNK:
        some_columns(pl.ds(whole * CHUNK, feed % CHUNK))
    partial_ref[...] = total_ref[...].astype(LOW)
    dnormed_ref[...] = dtotal_ref[...].astype(LOW)


def cross_backward_body(
    hidden_ref,
    mine_ref,
    other_ref,
    gains_ref,
    grad_ref,
    normed_ref,
    memory_ref,
    query_ref,
    key_ref,
    value_ref,
    mixed_ref,
    *refs,
):
    kv, qo = sides(refs[:5])
    grad_out_ref, dgain_ref, dnormed_ref, keep_ref, away_ref = refs[5:10]
    dkv, dqo = sides(refs[10:15])
    low_ref, transposed_ref, dmixed_ref, dquery_ref, dkey_ref, dvalue_ref = refs[15:]
    rows, model = hidden_ref.shape
    width = model // 4
    inner = query_ref.shape[1]
    half = rows // 2
    back, dgain_ref[...] = norm_backward(
        hidden_ref[...], gains_ref[2:3, :], both(mine_ref, other_ref)
    )
    grad = grad_ref[...].astype(FULL) + back
    grad_out_ref[...] = grad
    low_ref[...] = grad.astype(LOW)
    dmixed_ref[...] = project_in(low_ref, qo, slice(inner, 2 * inner)).astype(LOW)
    attention_backward(
        query_ref, key_ref, value_ref, dmixed_ref, dquery_ref, dkey_ref, dvalue_ref
    )
    for number in range(4):
        part = slice(number * width, (number + 1) * width)
        dnormed_ref[:, part] = product_right(dquery_ref[...], qo[number][:, :inner]).astype(LOW)
        partial = (
            product_right(dkey_ref[...], kv[number][:, :inner])
            + product_right(dvalue_ref[...], kv[number][:, inner:])
        ).astype(LOW)
        keep_ref[:, part] = partial[:half]
        away_ref[:, part] = partial[half:]
    transposed_ref[...] = memory_ref[...].T
    for number in range(4):
        part = slice(number * width, (number + 1) * width)
        dkv[number][:, :inner] = product_plain(transposed_ref[part, :], dkey_ref[...]).astype(LOW)
        dkv[number][:, inner:] = product_plain(transposed_ref[part, :], dvalue_ref[...]).astype(
            LOW
        )
    transposed_ref[...] = normed_ref[...].T
    for number in range(4):
        part = slice(number * width, (number + 1) * width)
        dqo[number][:, :inner] = product_plain(transposed_ref[part, :], dquery_ref[...]).astype(
            LOW
        )
    transposed_ref[...] = low_ref[...].T
    for number in range(4):
        part = slice(number * width, (number + 1) * width)
        dqo[number][:, inner:] = product_plain(transposed_ref[part, :], mixed_ref[...]).astype(LOW)


def self_backward_body(
    length_ref,
    bias_ref,
    hidden_ref,
    mine_ref,
    other_ref,
    gains_ref,
    grad_ref,
    normed_ref,
    query_ref,
    key_ref,
    value_ref,
    mixed_ref,
    *refs,
):
    qk, vo = sides(refs[:5])
    grad_out_ref, dgain_ref, dnormed_ref, diagonal_ref = refs[5:9]
    dqk, dvo = sides(refs[9:14])
    low_ref, transposed_ref, dmixed_ref, dquery_ref, dkey_ref, dvalue_ref = refs[14:]
    rows, model = hidden_ref.shape
    width = model // 4
    inner = query_ref.shape[1]
    back, dgain_ref[...] = norm_backward(
        hidden_ref[...], gains_ref[1:2, :], both(mine_ref, other_ref)
    )
    grad = grad_ref[...] + back
    grad_out_ref[...] = grad
    low_ref[...] = grad.astype(LOW)
    dmixed_ref[...] = project_in(low_ref, vo, slice(inner, 2 * inner)).astype(LOW)
    attention_backward(
        query_ref,
        key_ref,
        value_ref,
        dmixed_ref,
        dquery_ref,
        dkey_ref,
        dvalue_ref,
        length_ref,
        bias_ref,
        diagonal_ref,
    )
    for number in range(4):
        part = slice(number * width, (number + 1) * width)
        dnormed_ref[:, part] = (
            product_right(dquery_ref[...], qk[number][:, :inner])
            + product_right(dkey_ref[...], qk[number][:, inner:])
            + product_right(dvalue_ref[...], vo[number][:, :inner])
        ).astype(LOW)
    transposed_ref[...] = normed_ref[...].T
    for number in range(4):
        part = slice(number * width, (number + 1) * width)
        dqk[number][:, :inner] = product_plain(transposed_ref[part, :], dquery_ref[...]).astype(
            LOW
        )
        dqk[number][:, inner:] = product_plain(transposed_ref[part, :], dkey_ref[...]).astype(LOW)
        dvo[number][:, :inner] = product_plain(transposed_ref[part, :], dvalue_ref[...]).astype(
            LOW
        )
    transposed_ref[...] = low_ref[...].T
    for number in range(4):
        part = slice(number * width, (number + 1) * width)
        dvo[number][:, inner:] = product_plain(transposed_ref[part, :], mixed_ref[...]).astype(LOW)


def finish_body(
    length_ref,
    permute_ref,
    input_ref,
    mine_ref,
    other_ref,
    gains_ref,
    grad_ref,
    dgain_cross_ref,
    dgain_feed_ref,
    onehot_ref,
    diagonal_ref,
    out_ref,
    dgains_ref,
    table_ref,
):
    rows = input_ref.shape[0]
    permute = permute_ref[...]
    back, dgain = norm_backward(
        input_ref[...].astype(FULL), gains_ref[0:1, :], both(mine_ref, other_ref)
    )
    total = ((grad_ref[...] + back) * valid_column(length_ref, rows)).astype(LOW)
    out_ref[...] = product_right(total, permute).astype(LOW)
    dgains = jnp.concatenate([dgain, dgain_cross_ref[...], dgain_feed_ref[...]], axis=0)
    high = dgains.astype(LOW)
    middle = (dgains - high.astype(FULL)).astype(LOW)
    low = (dgains - high.astype(FULL) - middle.astype(FULL)).astype(LOW)
    dgains_ref[...] = (
        product_right(high, permute) + product_right(middle, permute)
    ) + product_right(low, permute)
    table_ref[...] = lax.dot_general(
        onehot_ref[...],
        diagonal_ref[...],
        (((1,), (1,)), ((), ())),
        precision=HIGHEST,
        preferred_element_type=FULL,
    )


def output_body(length_ref, permute_ref, hidden_ref, mine_ref, other_ref, out_ref):
    rows = hidden_ref.shape[0]
    total = (hidden_ref[...] + both(mine_ref, other_ref)) * valid_column(length_ref, rows)
    out_ref[...] = product_right(total.astype(LOW), permute_ref[...]).astype(LOW)


def encoder_body(permute_ref, mine_ref, other_ref, out_ref):
    total = both(mine_ref, other_ref).astype(LOW)
    out_ref[...] = product_right(total, permute_ref[...]).astype(LOW)


def fold_body(*refs):
    own, one, two = refs[:3]
    outs = refs[3:]
    width = own.shape[1]
    sides_held = outs[0].shape[1] // width
    block = outs[0].shape[0]
    for side in range(sides_held):
        for place in range(4):
            first = (4 * side + place) * block
            rows = slice(first, first + block)
            total = (
                own[rows, :].astype(FULL) + one[rows, :].astype(FULL) + two[rows, :].astype(FULL)
            )
            outs[place][:, side * width : (side + 1) * width] = total.astype(outs[place].dtype)


def fold_quarter(terms, sides_held):
    rows = terms[0].shape[0] // (4 * sides_held)
    width = terms[0].shape[1] * sides_held
    kinds = [full_shape, full_shape, low_shape, low_shape]
    return call(fold_body, [kind(rows, width) for kind in kinds], (), terms)


def stack_body(*refs):
    parts, outs = refs[:4], refs[4:]
    block = parts[0].shape[0]
    first = 0
    for out in outs:
        width = out.shape[1]
        for side in range(out.shape[0] // (4 * block)):
            for place in range(4):
                row = (4 * side + place) * block
                out[row : row + block, :] = parts[place][:, first : first + width]
            first += width


def stack_quarter(parts, shapes):
    return call(stack_body, [low_shape(*shape) for shape in shapes], (), parts)


def merge_body(x_in, y_in, left, right, x_out, y_out):
    x_out[...] = (x_in[...].astype(FULL) + left[...].astype(FULL)).astype(LOW)
    y_out[...] = (y_in[...].astype(FULL) + right[...].astype(FULL)).astype(LOW)


def merge_quarters(x_part, y_part, left, right):
    rows, width = left.shape
    at = [
        pl.BlockSpec((rows, width), lambda one: (0, 0)),
        pl.BlockSpec((rows, width), lambda one: (1, 0)),
    ]
    whole = pl.BlockSpec((rows, width), lambda one: (0, 0))
    return pl.pallas_call(
        merge_body,
        out_shape=[low_shape(*x_part.shape), low_shape(*y_part.shape)],
        grid=(1,),
        in_specs=at + [whole, whole],
        out_specs=at,
        input_output_aliases={0: 0, 1: 1},
        name="merge_body",
        cost_estimate=pl.CostEstimate(flops=1024, transcendentals=0, bytes_accessed=1024),
    )(x_part, y_part, left, right)


def gather_upper(value, devices, wait=()):
    masks = upper_masks(devices)
    if wait:
        value = after(value, *wait)
    if len(masks) == 2:
        one = swap_dp(value, masks[0], devices)
        two = swap_dp(value, masks[1], devices)
        return [value, one, two, swap_dp(one, masks[1], devices)]
    for mask in masks:
        value = jnp.concatenate([value, swap_dp(value, mask, devices)], axis=0)
    return [value]


def stack_sides(blocks, widths):
    if len(blocks) == 4:
        rows = 4 * blocks[0].shape[0]
        return stack_quarter(blocks, [(2 * rows, width) for width in widths])
    groups, first = [], 0
    for width in widths:
        middle, last = first + width, first + 2 * width
        groups.append(
            jnp.concatenate([blocks[0][:, first:middle], blocks[0][:, middle:last]], axis=0)
        )
        first = last
    return groups


def gather_lower(first, devices, x_wait=(), y_wait=(), last_wait=()):
    rows = first.shape[0] // 2
    x_part = swap_dp(after(first, *x_wait) if x_wait else first, 1, devices)
    y_part = swap_dp(after(first, *y_wait) if y_wait else first, 2, devices)
    left, right = x_part[:rows], y_part[rows:]
    if last_wait:
        left, right = after(left, *last_wait), after(right, *last_wait)
    return [first, x_part, y_part, swap_dp(left, 2, devices), swap_dp(right, 1, devices)]


def reduce_last(pieces, devices, wait=()):
    left, right = pieces[3:]
    if wait:
        left, right = after(left, *wait), after(right, *wait)
    return [swap_dp(left, 2, devices), swap_dp(right, 1, devices)]


def reduce_lower(pieces, came, devices, wait=()):
    x_part, y_part = merge_quarters(*pieces[1:3], *came)
    if wait:
        x_part, y_part = after(x_part, *wait), after(y_part, *wait)
    return [pieces[0], swap_dp(x_part, 1, devices), swap_dp(y_part, 2, devices)]


def reduce_upper(terms, devices, wait=()):
    masks = upper_masks(devices)
    if len(masks) == 2:
        own, one, two, three = fold_quarter(terms, 2)
        if wait:
            two, three = after(two, *wait), after(three, *wait)
        one = (one + swap_dp(three, masks[1], devices).astype(FULL)).astype(LOW)
        two = swap_dp(two, masks[1], devices)
        return own + two.astype(FULL) + swap_dp(one, masks[0], devices).astype(FULL)
    value = terms[0].astype(FULL) + terms[1].astype(FULL) + terms[2].astype(FULL)
    rows = value.shape[0] // 2
    value = jnp.concatenate([value[:rows], value[rows:]], axis=1)
    for mask in masks[::-1]:
        half = value.shape[0] // 2
        away = swap_dp(value[half:].astype(LOW), mask, devices)
        value = value[:half] + away.astype(FULL)
    return value


def first_across(value, devices):
    x_part, y_part = swap_dp(value, 1, devices), swap_dp(value, 2, devices)
    return [value, x_part, y_part, swap_dp(x_part, 2, devices)]


def gather_across(blocks, devices, wait):
    masks = upper_masks(devices)
    rows, width = blocks[0].shape
    first = after(stack_quarter(blocks, [(4 * rows, width)])[0], *wait)
    one, two = swap_dp(first, masks[0], devices), swap_dp(first, masks[1], devices)
    return [first, one, two, swap_dp(one, masks[1], devices)]


def reduce_across_last(pieces, devices):
    mask = upper_masks(devices)[1]
    return [swap_dp(pieces[3], mask, devices), swap_dp(pieces[2], mask, devices)]


def reduce_across(pieces, came, devices):
    mask = upper_masks(devices)[0]
    one = (pieces[1].astype(FULL) + came[0].astype(FULL)).astype(LOW)
    return [pieces[0], came[1], swap_dp(one, mask, devices)]


def reduce_across_first(terms, devices):
    own, x_part, y_part, last = fold_quarter(terms, 1)
    x_part = (x_part + swap_dp(last, 2, devices).astype(FULL)).astype(LOW)
    return (
        own
        + swap_dp(y_part, 2, devices).astype(FULL)
        + swap_dp(x_part, 1, devices).astype(FULL)
    )


def deal(value, order, devices):
    rows, width = value.shape
    first = lax.all_to_all(
        value.reshape(devices, rows // devices, width), "dp", split_axis=0, concat_axis=0, tiled=True
    )
    second = lax.all_to_all(
        jnp.take(first, order, axis=0), "dp", split_axis=0, concat_axis=0, tiled=True
    )
    return second.reshape(rows, width)


def on_device(
    tokens,
    encoder_states,
    cotangent,
    lengths,
    deal_order,
    bucket_index,
    rel_table,
    gain_self,
    self_query,
    self_key,
    self_value,
    self_output,
    gain_cross,
    cross_query,
    cross_key,
    cross_value,
    cross_output,
    gain_feed,
    feed_gate,
    feed_value,
    feed_output,
):
    devices = lax.axis_size("dp")
    myself = lax.axis_index("dp")
    core = lax.axis_index("tensor")
    rows, model = tokens.shape
    block = model // devices
    buckets, heads = rel_table.shape
    inner = self_query.shape[1]
    feed = feed_gate.shape[1]
    across = devices == 16

    numbers = jnp.arange(devices, dtype=jnp.int32)
    owner_of = jnp.sum(
        jnp.where(deal_order[:, None] == numbers[None, :], numbers[:, None], 0), axis=0
    )
    length = jnp.sum(jnp.where(numbers == myself, lengths, 0)).reshape(1)

    self_own = jnp.concatenate([self_query, self_key, self_value, self_output], axis=1)
    cross_own = jnp.concatenate([cross_key, cross_value, cross_query, cross_output], axis=1)
    feed_own = jnp.concatenate([feed_gate, feed_value], axis=1)
    self_blocks = gather_upper(self_own, devices)
    if across:
        down_blocks = first_across(feed_output, devices)
        self_blocks[3] = after(self_blocks[3], *down_blocks[1:3])
    (self_first,) = stack_sides(self_blocks, [2 * inner])
    cross_blocks = gather_upper(cross_own, devices, self_blocks[1:3])
    self_w = gather_lower(self_first, devices)
    (cross_first,) = stack_sides(cross_blocks, [2 * inner])
    cross_w = gather_lower(cross_first, devices, self_w[1:2], self_w[2:3])
    feed_blocks = gather_upper(feed_own, devices, cross_blocks[1:3])
    (feed_first,) = stack_sides(feed_blocks, [feed])
    if across:
        down = gather_across(down_blocks, devices, feed_blocks[1:3])
    else:
        down = gather_upper(feed_output, devices)[0]
        width = feed // 2
        down = gather_lower(
            jnp.concatenate([down[:, :width], down[:, width:]], axis=0), devices
        )
        middle = down[0].shape[0] // 2
        down = [
            jnp.concatenate([one[:middle], one[middle:]], axis=1) for one in down[:3]
        ] + [jnp.concatenate(down[3:], axis=1)]

    offsets = jnp.asarray(np.array(block_offsets(upper_masks(devices) + [1, 2]), np.int32))
    source = (
        ((myself ^ offsets) * block)[:, None] + jnp.arange(block, dtype=jnp.int32)[None, :]
    ).reshape(1, -1)
    permute, masked_input, grad_three, gains, normed_self = call(
        prepare_body,
        [
            low_shape(model, model),
            low_shape(rows, model),
            low_shape(rows, model),
            full_shape(3, model),
            low_shape(rows, model),
        ],
        (length,),
        (tokens, cotangent, jnp.stack([gain_self, gain_cross, gain_feed]), source),
        flops=4 * rows * model * model,
    )

    half = rows // 2
    memory_half = deal(
        lax.dynamic_slice_in_dim(encoder_states, core * half, half, axis=0), deal_order, devices
    )
    memory_other = swap_tensor(memory_half)

    skewed_bucket = jnp.concatenate(
        [bucket_index[:1], jnp.full((rows,), -1, jnp.int32), bucket_index[::-1][: rows - 1]]
    )
    onehot = (jnp.arange(buckets, dtype=jnp.int32)[:, None] == skewed_bucket[None, :]).astype(FULL)
    bias_rows = jnp.dot(rel_table.T, onehot, precision=HIGHEST)

    unit = 2 * rows * model * inner
    query_self, key_self, value_self, mixed_self, self_partial = call(
        self_forward_body,
        [low_shape(rows, inner)] * 4 + [low_shape(rows, model)],
        (length,),
        (bias_rows, normed_self, *self_w),
        flops=5 * unit,
    )
    memory, key_cross, value_cross = call(
        memory_body,
        [low_shape(rows, model)] + [low_shape(rows, inner)] * 2,
        (),
        (memory_half, memory_other, permute, *cross_w),
        flops=4 * unit,
    )
    hidden_one, normed_cross, query_cross, mixed_cross, partial = call(
        cross_forward_body,
        [full_shape(rows, model), low_shape(rows, model)]
        + [low_shape(rows, inner)] * 2
        + [low_shape(rows, model)],
        (),
        (
            masked_input,
            self_partial,
            swap_tensor(self_partial),
            gains,
            key_cross,
            value_cross,
            *cross_w,
        ),
        flops=3 * unit,
    )
    quarter_rows = model // 4
    feed_w = gather_lower(
        feed_first,
        devices,
        (cross_w[1], self_partial),
        (cross_w[2], self_partial),
        (partial,),
    )

    def group_shapes(width):
        return [low_shape(2 * quarter_rows, width)] * 3 + [low_shape(quarter_rows, width)] * 2

    feed_grads = group_shapes(feed) + [low_shape(quarter_rows, feed)] * 4
    outs = call(
        functools.partial(feed_body, across),
        [full_shape(rows, model), low_shape(rows, model), low_shape(rows, model)] + feed_grads,
        (),
        (hidden_one, partial, swap_tensor(partial), gains, grad_three, *feed_w, *down),
        scratch=[
            pltpu.VMEM((rows, model), LOW),
            pltpu.VMEM((model, rows), LOW),
            pltpu.VMEM((model, rows), LOW),
            pltpu.VMEM((model, feed), LOW),
            pltpu.VMEM((rows, model), FULL),
            pltpu.VMEM((rows, model), FULL),
        ],
        flops=18 * rows * model * feed,
    )
    hidden_two, partial, dpartial = outs[:3]
    dfeed, ddown = outs[3:8], outs[8:12]
    feed_came = reduce_last(dfeed, devices)
    if across:
        down_came = reduce_across_last(ddown, devices)
    else:
        width = feed // 2
        ddown = [
            jnp.concatenate([one[:, :width], one[:, width:]], axis=0) for one in ddown[:3]
        ] + [ddown[3][:, :width], ddown[3][:, width:]]
        down_came = reduce_last(ddown, devices)
    (layer_result,) = call(
        output_body,
        [low_shape(rows, model)],
        (length,),
        (permute, hidden_two, partial, swap_tensor(partial)),
        flops=2 * unit,
    )

    attention_scratch = [
        pltpu.VMEM((rows, model), LOW),
        pltpu.VMEM((model, rows), LOW),
    ] + [pltpu.VMEM((rows, inner), LOW)] * 4
    outs = call(
        cross_backward_body,
        [
            full_shape(rows, model),
            full_shape(1, model),
            low_shape(rows, model),
            low_shape(half, model),
            low_shape(half, model),
        ]
        + group_shapes(2 * inner),
        (),
        (
            hidden_two,
            dpartial,
            swap_tensor(dpartial),
            gains,
            grad_three,
            normed_cross,
            memory,
            query_cross,
            key_cross,
            value_cross,
            mixed_cross,
            *cross_w,
        ),
        scratch=attention_scratch,
        flops=9 * unit,
    )
    grad_two, dgain_feed, dpartial, keep, away = outs[:5]
    dcross = outs[5:10]
    feed_terms = reduce_lower(
        dfeed, [after(one, dpartial) for one in feed_came], devices
    )
    cross_came = reduce_last(dcross, devices, down_came[:1])
    cross_terms = reduce_lower(dcross, cross_came, devices, feed_terms[1:])
    (encoder_half,) = call(
        encoder_body,
        [low_shape(half, model)],
        (),
        (permute, keep, swap_tensor(away)),
        flops=unit,
    )
    encoder_grad = deal(encoder_half, owner_of, devices)

    outs = call(
        self_backward_body,
        [
            full_shape(rows, model),
            full_shape(1, model),
            low_shape(rows, model),
            full_shape(heads, 2 * rows),
        ]
        + group_shapes(2 * inner),
        (length,),
        (
            bias_rows,
            hidden_one,
            dpartial,
            swap_tensor(dpartial),
            gains,
            after(grad_two, *feed_came),
            normed_self,
            query_self,
            key_self,
            value_self,
            mixed_self,
            *self_w,
        ),
        scratch=attention_scratch,
        flops=10 * unit,
    )
    grad_one, dgain_cross, dpartial, diagonal = outs[:4]
    dself = outs[4:9]
    self_came = reduce_last(dself, devices, feed_terms[1:])
    self_terms = reduce_lower(dself, self_came, devices, cross_terms[1:])
    input_grad, dgains, dtable = call(
        finish_body,
        [low_shape(rows, model), full_shape(3, model), full_shape(buckets, heads)],
        (length,),
        (
            permute,
            masked_input,
            dpartial,
            swap_tensor(dpartial),
            gains,
            grad_one,
            dgain_cross,
            dgain_feed,
            onehot,
            diagonal,
        ),
        flops=2 * unit,
    )

    if across:
        down_terms = reduce_across(ddown, down_came, devices)
        feed_sums = reduce_upper(feed_terms, devices, down_terms[2:])
        down_sum = reduce_across_first(down_terms, devices)
    else:
        down_sum = reduce_upper(reduce_lower(ddown, down_came, devices), devices)
        feed_sums = reduce_upper(feed_terms, devices)
    cross_sums = reduce_upper(cross_terms, devices, (feed_sums,))
    self_sums = reduce_upper(self_terms, devices, (cross_sums,))
    small = total_small(
        jnp.concatenate([dgains.reshape(-1), dtable.reshape(-1)]).reshape(-1, 128), devices
    ).reshape(-1)
    gain_sums = small[: 3 * model].reshape(3, model)
    table_sum = small[3 * model :].reshape(buckets, heads)

    def column(value, number, width):
        return value[:, number * width : (number + 1) * width]

    return (
        layer_result,
        input_grad,
        encoder_grad,
        table_sum,
        gain_sums[0],
        column(self_sums, 0, inner),
        column(self_sums, 1, inner),
        column(self_sums, 2, inner),
        column(self_sums, 3, inner),
        gain_sums[1],
        column(cross_sums, 2, inner),
        column(cross_sums, 0, inner),
        column(cross_sums, 1, inner),
        column(cross_sums, 3, inner),
        gain_sums[2],
        column(feed_sums, 0, feed),
        column(feed_sums, 1, feed),
        down_sum,
    )


def solution(mesh):
    in_specs = (
        P("dp", None),
        P("dp", None),
        P("dp", None),
        P(),
        P(),
        P(),
        P(None, "tensor"),
        P(),
        P("dp", "tensor"),
        P("dp", "tensor"),
        P("dp", "tensor"),
        P("dp", "tensor"),
        P(),
        P("dp", "tensor"),
        P("dp", "tensor"),
        P("dp", "tensor"),
        P("dp", "tensor"),
        P(),
        P("dp", "tensor"),
        P("dp", "tensor"),
        P("dp", "tensor"),
    )
    out_specs = (
        P("dp", None),
        P("dp", None),
        P(("dp", "tensor"), None),
        P(None, "tensor"),
        P(),
        P("dp", "tensor"),
        P("dp", "tensor"),
        P("dp", "tensor"),
        P("dp", "tensor"),
        P(),
        P("dp", "tensor"),
        P("dp", "tensor"),
        P("dp", "tensor"),
        P("dp", "tensor"),
        P(),
        P("dp", "tensor"),
        P("dp", "tensor"),
        P("dp", "tensor"),
    )
    return jax.shard_map(
        on_device, mesh=mesh, in_specs=in_specs, out_specs=out_specs, check_vma=False
    )
```

profile of v0, /device:TPU:0, one launch (start us, length us, event | category | flops | bytes accessed | tf_op | source)
XLA Modules:
  0.0 378.5 jit_solution(7513123860283874995)
XLA Ops:
  4.1 5.0 %collective-permute-start = (bf16[64,2048]{1,0:T(8,128)(2,1)S(1)}, bf16[64,2048]{1,0:T(8,128)(2,1)S(1)}, u32[]{:S(2)}, u32[]{:S(2)}) collective-permute-start(bf16[64,2048]{1,0:T(8,128)(2,1)S(1)} %constant_dynamic-update-slice_fusion.refs_0_), channel_id=1, source_target_pairs={{0,24},{2,26},{4,28},{6,30},{8,16},{10,18},{12,20},{14,22},{16,8},... | collective-permute-start | bytes 786440 | tf_op jit(solution)/shard_map/ppermute | solution.py:34
  9.2 6.4 %collective-permute-done.refs_1_ = bf16[64,2048]{1,0:T(8,128)(2,1)S(1)} collective-permute-done((bf16[64,2048]{1,0:T(8,128)(2,1)S(1)}, bf16[64,2048]{1,0:T(8,128)(2,1)S(1)}, u32[]{:S(2)}, u32[]{:S(2)}) %collective-permute-start) | collective-permute-done | bytes 262176 | tf_op jit(solution)/shard_map/ppermute | solution.py:34
  15.6 5.2 %collective-permute-start.2 = (bf16[64,2048]{1,0:T(8,128)(2,1)S(1)}, bf16[64,2048]{1,0:T(8,128)(2,1)S(1)}, u32[]{:S(2)}, u32[]{:S(2)}) collective-permute-start(bf16[64,2048]{1,0:T(8,128)(2,1)S(1)} %collective-permute-done.refs_1_), channel_id=1, source_target_pairs={{0,8},{2,10},{4,12},{6,14},{8,0},{10,2},{12,4},{14,6},{16,24},{18,... | collective-permute-start | bytes 786440 | tf_op jit(solution)/shard_map/ppermute | solution.py:34
  24.6 4.6 %all-to-all-start = ((bf16[16,8,1024]{2,1,0:T(8,128)(2,1)}), bf16[16,8,1024]{2,1,0:T(8,128)(2,1)}, u32[]{:S(2)}, u32[]{:S(2)}) async-start(bf16[16,8,1024]{2,1,0:T(8,128)(2,1)} %dynamic-slice_bitcast_fusion), calls=%async_computation | async-start | bytes 524288 | tf_op jit(solution)/shard_map/all_to_all | solution.py:724
  30.0 4.2 %collective-permute-done.1.refs_2_ = bf16[64,2048]{1,0:T(8,128)(2,1)S(1)} collective-permute-done((bf16[64,2048]{1,0:T(8,128)(2,1)S(1)}, bf16[64,2048]{1,0:T(8,128)(2,1)S(1)}, u32[]{:S(2)}, u32[]{:S(2)}) %collective-permute-start.1) | collective-permute-done | bytes 262176 | tf_op jit(solution)/shard_map/ppermute | solution.py:34
  36.9 3.2 collective-permute-start.11
  41.5 5.4 %collective-permute-done.11.refs_1_ = bf16[64,2048]{1,0:T(8,128)(2,1)S(1)} collective-permute-done((bf16[64,2048]{1,0:T(8,128)(2,1)S(1)}, bf16[64,2048]{1,0:T(8,128)(2,1)S(1)}, u32[]{:S(2)}, u32[]{:S(2)}) %collective-permute-start.11) | collective-permute-done | bytes 262176 | tf_op jit(solution)/shard_map/ppermute | solution.py:34
  46.8 2.5 collective-permute-start.13
  50.3 2.1 collective-permute-start.19
  52.4 5.0 %collective-permute-done.13.refs_3_ = bf16[64,2048]{1,0:T(8,128)(2,1)S(1)} collective-permute-done((bf16[64,2048]{1,0:T(8,128)(2,1)S(1)}, bf16[64,2048]{1,0:T(8,128)(2,1)S(1)}, u32[]{:S(2)}, u32[]{:S(2)}) %collective-permute-start.13) | collective-permute-done | bytes 262176 | tf_op jit(solution)/shard_map/ppermute | solution.py:34
  68.6 2.6 collective-permute-done.20.refs_2_
  74.4 3.2 prepare_body.1
  80.0 2.2 gather_fusion
  84.0 6.1 %all-to-all-start.1 = ((bf16[16,8,1024]{2,1,0:T(8,128)(2,1)}), bf16[16,8,1024]{2,1,0:T(8,128)(2,1)}, u32[]{:S(2)}, u32[]{:S(2)}) async-start(bf16[16,8,1024]{2,1,0:T(8,128)(2,1)} %broadcast_select_fusion.1), calls=%async_computation.1 | async-start | bytes 524288 | tf_op jit(solution)/shard_map/all_to_all | solution.py:727
  90.1 1.9 collective-permute-start.26
  93.0 2.4 stack_body.6.refs_0_
  95.4 8.0 %self_forward_body.1 = (bf16[256,512]{1,0:T(8,128)(2,1)S(1)}, bf16[256,512]{1,0:T(8,128)(2,1)S(1)}, bf16[256,512]{1,0:T(8,128)(2,1)S(1)}, bf16[256,512]{1,0:T(8,128)(2,1)S(1)}, bf16[256,1024]{1,0:T(8,128)(2,1)S(1)}) custom-call(s32[1]{0:T(128)} %bitcast.length_ref, f32[8,512]{1,0:T(8,128)S(1)} %convolution_bitcast_fusion.bias_ref, ...), custom_call_target="tpu_custom_call" | custom-call | flops 1342177280 | bytes 1024 | tf_op jit(solution)/shard_map/self_forward_body/pallas_call | solution.py:214
  107.3 3.3 collective-permute-start.27
  115.0 10.5 %collective-permute-done.27.refs_6_ = bf16[256,1408]{1,0:T(8,128)(2,1)} collective-permute-done((bf16[256,1408]{1,0:T(8,128)(2,1)}, bf16[256,1408]{1,0:T(8,128)(2,1)}, u32[]{:S(2)}, u32[]{:S(2)}) %collective-permute-start.27) | collective-permute-done | bytes 720928 | tf_op jit(solution)/shard_map/ppermute | solution.py:34
  125.6 22.4 %collective-permute-done.17.refs_4_ = bf16[256,1024]{1,0:T(8,128)(2,1)S(1)} collective-permute-done((bf16[256,1024]{1,0:T(8,128)(2,1)S(1)}, bf16[256,1024]{1,0:T(8,128)(2,1)S(1)}, u32[]{:S(2)}, u32[]{:S(2)}) %collective-permute-start.17) | collective-permute-done | bytes 524320 | tf_op jit(solution)/shard_map/ppermute | solution.py:34
  150.0 2.9 memory_body.1
  153.0 6.4 %cross_forward_body.1 = (f32[256,1024]{1,0:T(8,128)S(1)}, bf16[256,1024]{1,0:T(8,128)(2,1)S(1)}, bf16[256,512]{1,0:T(8,128)(2,1)S(1)}, bf16[256,512]{1,0:T(8,128)(2,1)S(1)}, bf16[256,1024]{1,0:T(8,128)(2,1)S(1)}) custom-call(bf16[256,1024]{1,0:T(8,128)(2,1)S(1)} %copy-done.4, bf16[256,1024]{1,0:T(8,128)(2,1)S(1)} %copy-done.27, ...), custom_call_target="tpu_custom_call" | custom-call | flops 805306368 | bytes 1024 | tf_op jit(solution)/shard_map/cross_forward_body/pallas_call | solution.py:214
  165.3 2.0 collective-permute-done.28.refs_7_
  167.3 12.0 %collective-permute-done.29.refs_8_ = bf16[256,1408]{1,0:T(8,128)(2,1)S(1)} collective-permute-done((bf16[256,1408]{1,0:T(8,128)(2,1)}, bf16[256,1408]{1,0:T(8,128)(2,1)S(1)}, u32[]{:S(2)}, u32[]{:S(2)}) %collective-permute-start.29) | collective-permute-done | bytes 720928 | tf_op jit(solution)/shard_map/ppermute | solution.py:34
  180.2 15.5 %feed_body.1 = (f32[256,1024]{1,0:T(8,128)}, bf16[256,1024]{1,0:T(8,128)(2,1)}, bf16[256,1024]{1,0:T(8,128)(2,1)S(1)}, bf16[512,1408]{1,0:T(8,128)(2,1)}, bf16[5...) custom-call(f32[256,1024]{1,0:T(8,128)} %copy-done.41, ...), custom_call_target="tpu_custom_call" | custom-call | flops 6643777536 | bytes 1024 | tf_op jit(solution)/shard_map/feed_body/pallas_call | solution.py:214
  201.6 11.9 %cross_backward_body.1 = (f32[256,1024]{1,0:T(8,128)S(1)}, f32[1,1024]{1,0:T(1,128)S(1)}, bf16[256,1024]{1,0:T(8,128)(2,1)S(1)}, bf16[128,1024]{1,0:T(8,128)(2,1...) custom-call(f32[256,1024]{1,0:T(8,128)} %get-tuple-element.140.hidde, ...), custom_call_target="tpu_custom_call" | custom-call | flops 2415919104 | bytes 1024 | tf_op jit(solution)/shard_map/cross_backward_body/pallas_call | solution.py:214
  219.1 3.1 merge_body.3
  224.9 3.3 collective-permute-start.52
  230.3 12.6 %self_backward_body.1 = (f32[256,1024]{1,0:T(8,128)S(1)}, f32[1,1024]{1,0:T(1,128)S(1)}, bf16[256,1024]{1,0:T(8,128)(2,1)S(1)}, f32[8,512]{1,0:T(8,128)S(1)}, bf...) custom-call(s32[1]{0:T(128)} %bitcast.length_ref, ...), custom_call_target="tpu_custom_call" | custom-call | flops 2684354560 | bytes 1024 | tf_op jit(solution)/shard_map/self_backward_body/pallas_call | solution.py:214
  247.5 9.5 %collective-permute-done.41.refs_1_ = bf16[512,1408]{1,0:T(8,128)(2,1)S(1)} collective-permute-done((bf16[512,1408]{1,0:T(8,128)(2,1)}, bf16[512,1408]{1,0:T(8,128)(2,1)S(1)}, u32[]{:S(2)}, u32[]{:S(2)}) %collective-permute-start.41) | collective-permute-done | bytes 1441824 | tf_op jit(solution)/shard_map/ppermute | solution.py:34
  262.3 5.4 %all-to-all-start.2 = ((bf16[16,8,1024]{2,1,0:T(8,128)(2,1)}), bf16[16,8,1024]{2,1,0:T(8,128)(2,1)}, u32[]{:S(2)}, u32[]{:S(2)}) async-start(bf16[16,8,1024]{2,1,0:T(8,128)(2,1)} %bitcast.7), calls=%async_computation.2 | async-start | bytes 524288 | tf_op jit(solution)/shard_map/all_to_all | solution.py:724
  267.8 2.7 merge_body.5
  271.7 4.5 %finish_body.1 = (bf16[256,1024]{1,0:T(8,128)(2,1)}, f32[3,1024]{1,0:T(4,128)S(1)}, f32[32,8]{1,0:T(8,128)S(1)}) custom-call(s32[1]{0:T(128)} %bitcast.length_ref, bf16[1024,1024]{1,0:T(8,128)(2,1)S(1)} %get-tuple-element.120.permute_ref, bf16[256,1024]{1,0:T(8,128)(2,1)S(1)} %copy-done.5, bf16[256,1024]{1,0:T(8,128)(2,1)S(1)} %get-tuple-element.156.mine_ref, ...), custom_call_target="tpu_custom_call" | custom-call | flops 536870912 | bytes 1024 | tf_op jit(solution)/shard_map/finish_body/pallas_call | solution.py:214
  276.4 1.9 collective-permute-start.53
  281.2 2.0 add_convert_fusion.1
  283.2 2.4 collective-permute-start.55
  286.2 3.4 output_body.1
  291.2 13.3 %collective-permute-done.37 = f32[26,128]{1,0:T(8,128)S(1)} collective-permute-done((f32[26,128]{1,0:T(8,128)S(1)}, f32[26,128]{1,0:T(8,128)S(1)}, u32[]{:S(2)}, u32[]{:S(2)}) %collective-permute-start.37) | collective-permute-done | bytes 13344 | tf_op jit(solution)/shard_map/ppermute | solution.py:34
  308.7 2.3 convert_add_fusion
  311.0 2.6 fold_body.5
  318.1 4.7 %all-to-all-start.3 = ((bf16[16,8,1024]{2,1,0:T(8,128)(2,1)}), bf16[16,8,1024]{2,1,0:T(8,128)(2,1)}, u32[]{:S(2)}, u32[]{:S(2)}) async-start(bf16[16,8,1024]{2,1,0:T(8,128)(2,1)} %broadcast_select_fusion), calls=%async_computation.3 | async-start | bytes 524288 | tf_op jit(solution)/shard_map/all_to_all | solution.py:727
  327.1 3.0 collective-permute-done.39
  331.8 2.7 merge_body.4
  341.2 2.0 collective-permute-start.63
  345.2 2.4 collective-permute-done.58
  348.8 9.0 %collective-permute-done.51.refs_2_ = bf16[512,1024]{1,0:T(8,128)(2,1)S(1)} collective-permute-done((bf16[512,1024]{1,0:T(8,128)(2,1)}, bf16[512,1024]{1,0:T(8,128)(2,1)S(1)}, u32[]{:S(2)}, u32[]{:S(2)}) %collective-permute-start.51) | collective-permute-done | bytes 1048608 | tf_op jit(solution)/shard_map/ppermute | solution.py:34
  361.6 6.1 %collective-permute-done.60 = bf16[64,2048]{1,0:T(8,128)(2,1)S(1)} collective-permute-done((bf16[64,2048]{1,0:T(8,128)(2,1)S(1)}, bf16[64,2048]{1,0:T(8,128)(2,1)S(1)}, u32[]{:S(2)}, u32[]{:S(2)}) %collective-permute-start.60) | collective-permute-done | bytes 262176 | tf_op jit(solution)/shard_map/ppermute | solution.py:34
  370.5 5.5 %collective-permute-done.61 = bf16[64,2048]{1,0:T(8,128)(2,1)S(1)} collective-permute-done((bf16[64,2048]{1,0:T(8,128)(2,1)S(1)}, bf16[64,2048]{1,0:T(8,128)(2,1)S(1)}, u32[]{:S(2)}, u32[]{:S(2)}) %collective-permute-start.61) | collective-permute-done | bytes 262176 | tf_op jit(solution)/shard_map/ppermute | solution.py:34
  (348 shorter events, 115.4 us)
Async XLA Ops:
  15.6 14.4 %collective-permute-start.2 = (bf16[64,2048]{1,0:T(8,128)(2,1)S(1)}, bf16[64,2048]{1,0:T(8,128)(2,1)S(1)}, u32[]{:S(2)}, u32[]{:S(2)}) collective-permute-start(bf16[64,2048]{1,0:T(8,128)(2,1)S(1)} %collective-permute-done.refs_1_), channel_id=1, source_target_pairs={{0,8},{2,10},{4,12},{6,14},{8,0},{10,2},{12,4},{14,6},{16,24},{18,... | collective-permute-start | bytes 786440 | tf_op jit(solution)/shard_map/ppermute | solution.py:34
  24.6 55.5 %all-to-all-start = ((bf16[16,8,1024]{2,1,0:T(8,128)(2,1)}), bf16[16,8,1024]{2,1,0:T(8,128)(2,1)}, u32[]{:S(2)}, u32[]{:S(2)}) async-start(bf16[16,8,1024]{2,1,0:T(8,128)(2,1)} %dynamic-slice_bitcast_fusion), calls=%async_computation | async-start | bytes 524288 | tf_op jit(solution)/shard_map/all_to_all | solution.py:724
  34.3 23.4 %collective-permute-start.6 = (bf16[512,1024]{1,0:T(8,128)(2,1)S(1)}, bf16[512,1024]{1,0:T(8,128)(2,1)}, u32[]{:S(2)}, u32[]{:S(2)}) collective-permute-start(bf16[512,1024]{1,0:T(8,128)(2,1)S(1)} %stack_body.4.refs_0_), channel_id=1, source_target_pairs={{0,4},{2,6},{4,0},{6,2},{8,12},{10,14},{12,8},{14,10},{16,20},{18,... | collective-permute-start | bytes 3145736 | tf_op jit(solution)/shard_map/ppermute | solution.py:34
  35.3 23.5 %collective-permute-start.5 = (bf16[512,1024]{1,0:T(8,128)(2,1)S(1)}, bf16[512,1024]{1,0:T(8,128)(2,1)}, u32[]{:S(2)}, u32[]{:S(2)}) collective-permute-start(bf16[512,1024]{1,0:T(8,128)(2,1)S(1)} %stack_body.4.refs_0_), channel_id=1, source_target_pairs={{0,2},{2,0},{4,6},{6,4},{8,10},{10,8},{12,14},{14,12},{16,18},{18,... | collective-permute-start | bytes 3145736 | tf_op jit(solution)/shard_map/ppermute | solution.py:34
  50.3 17.1 %collective-permute-start.19 = (bf16[64,2816]{1,0:T(8,128)(2,1)S(1)}, bf16[64,2816]{1,0:T(8,128)(2,1)}, u32[]{:S(2)}, u32[]{:S(2)}) collective-permute-start(bf16[64,2816]{1,0:T(8,128)(2,1)S(1)} %pad_maximum_fusion.refs_0_), channel_id=1, source_target_pairs={{0,24},{2,26},{4,28},{6,30},{8,16},{10,18},{12,20},{14,22},{16,8},... | collective-permute-start | bytes 1081352 | tf_op jit(solution)/shard_map/ppermute | solution.py:34
  57.7 46.5 %collective-permute-start.15 = (bf16[512,1024]{1,0:T(8,128)(2,1)S(1)}, bf16[512,1024]{1,0:T(8,128)(2,1)}, u32[]{:S(2)}, u32[]{:S(2)}) collective-permute-start(bf16[512,1024]{1,0:T(8,128)(2,1)S(1)} %stack_body.5.refs_0_), channel_id=1, source_target_pairs={{0,4},{2,6},{4,0},{6,2},{8,12},{10,14},{12,8},{14,10},{16,20},{18,... | collective-permute-start | bytes 3145736 | tf_op jit(solution)/shard_map/ppermute | solution.py:34
  58.8 45.8 %collective-permute-start.14 = (bf16[512,1024]{1,0:T(8,128)(2,1)S(1)}, bf16[512,1024]{1,0:T(8,128)(2,1)}, u32[]{:S(2)}, u32[]{:S(2)}) collective-permute-start(bf16[512,1024]{1,0:T(8,128)(2,1)S(1)} %stack_body.5.refs_0_), channel_id=1, source_target_pairs={{0,2},{2,0},{4,6},{6,4},{8,10},{10,8},{12,14},{14,12},{16,18},{18,... | collective-permute-start | bytes 3145736 | tf_op jit(solution)/shard_map/ppermute | solution.py:34
  64.7 30.7 %collective-permute-start.7 = (bf16[256,1024]{1,0:T(8,128)(2,1)}, bf16[256,1024]{1,0:T(8,128)(2,1)}, u32[]{:S(2)}, u32[]{:S(2)}) collective-permute-start(bf16[256,1024]{1,0:T(8,128)(2,1)} %slice.105), channel_id=1, source_target_pairs={{0,4},{2,6},{4,0},{6,2},{8,12},{10,14},{12,8},{14,10},{16,20},{18,... | collective-permute-start | bytes 1572872 | tf_op jit(solution)/shard_map/ppermute | solution.py:34
  67.4 28.0 %collective-permute-start.8 = (bf16[256,1024]{1,0:T(8,128)(2,1)}, bf16[256,1024]{1,0:T(8,128)(2,1)}, u32[]{:S(2)}, u32[]{:S(2)}) collective-permute-start(bf16[256,1024]{1,0:T(8,128)(2,1)} %slice.106), channel_id=1, source_target_pairs={{0,2},{2,0},{4,6},{6,4},{8,10},{10,8},{12,14},{14,12},{16,18},{18,... | collective-permute-start | bytes 1572872 | tf_op jit(solution)/shard_map/ppermute | solution.py:34
  72.0 18.1 %collective-permute-start.21 = (bf16[64,2816]{1,0:T(8,128)(2,1)}, bf16[64,2816]{1,0:T(8,128)(2,1)}, u32[]{:S(2)}, u32[]{:S(2)}) collective-permute-start(bf16[64,2816]{1,0:T(8,128)(2,1)} %collective-permute-done.19.refs_1_), channel_id=1, source_target_pairs={{0,8},{2,10},{4,12},{6,14},{8,0},{10,2},{12,4},{14,6},{16,24},{18,... | collective-permute-start | bytes 1081352 | tf_op jit(solution)/shard_map/ppermute | solution.py:34
  84.0 26.6 %all-to-all-start.1 = ((bf16[16,8,1024]{2,1,0:T(8,128)(2,1)}), bf16[16,8,1024]{2,1,0:T(8,128)(2,1)}, u32[]{:S(2)}, u32[]{:S(2)}) async-start(bf16[16,8,1024]{2,1,0:T(8,128)(2,1)} %broadcast_select_fusion.1), calls=%async_computation.1 | async-start | bytes 524288 | tf_op jit(solution)/shard_map/all_to_all | solution.py:727
  90.1 16.2 %collective-permute-start.26 = (bf16[64,1408]{1,0:T(8,128)(2,1)}, bf16[64,1408]{1,0:T(8,128)(2,1)S(1)}, u32[]{:S(2)}, u32[]{:S(2)}) collective-permute-start(bf16[64,1408]{1,0:T(8,128)(2,1)} %copy-done.37), channel_id=1, source_target_pairs={{0,4},{2,6},{4,0},{6,2},{8,12},{10,14},{12,8},{14,10},{16,20},{18,... | collective-permute-start | bytes 540680 | tf_op jit(solution)/shard_map/ppermute | solution.py:34
  104.2 55.2 %collective-permute-start.23 = (bf16[512,1408]{1,0:T(8,128)(2,1)}, bf16[512,1408]{1,0:T(8,128)(2,1)}, u32[]{:S(2)}, u32[]{:S(2)}) collective-permute-start(bf16[512,1408]{1,0:T(8,128)(2,1)} %stack_body.6.refs_0_), channel_id=1, source_target_pairs={{0,4},{2,6},{4,0},{6,2},{8,12},{10,14},{12,8},{14,10},{16,20},{18,... | collective-permute-start | bytes 4325384 | tf_op jit(solution)/shard_map/ppermute | solution.py:34
  104.5 58.0 %collective-permute-start.22 = (bf16[512,1408]{1,0:T(8,128)(2,1)}, bf16[512,1408]{1,0:T(8,128)(2,1)}, u32[]{:S(2)}, u32[]{:S(2)}) collective-permute-start(bf16[512,1408]{1,0:T(8,128)(2,1)} %stack_body.6.refs_0_), channel_id=1, source_target_pairs={{0,2},{2,0},{4,6},{6,4},{8,10},{10,8},{12,14},{14,12},{16,18},{18,... | collective-permute-start | bytes 4325384 | tf_op jit(solution)/shard_map/ppermute | solution.py:34
  107.3 18.3 %collective-permute-start.27 = (bf16[256,1408]{1,0:T(8,128)(2,1)}, bf16[256,1408]{1,0:T(8,128)(2,1)}, u32[]{:S(2)}, u32[]{:S(2)}) collective-permute-start(bf16[256,1408]{1,0:T(8,128)(2,1)} %stack_body.7.refs_5_), channel_id=1, source_target_pairs={{0,24},{2,26},{4,28},{6,30},{8,16},{10,18},{12,20},{14,22},{16,8},... | collective-permute-start | bytes 2162696 | tf_op jit(solution)/shard_map/ppermute | solution.py:34
  111.8 36.2 %collective-permute-start.17 = (bf16[256,1024]{1,0:T(8,128)(2,1)S(1)}, bf16[256,1024]{1,0:T(8,128)(2,1)S(1)}, u32[]{:S(2)}, u32[]{:S(2)}) collective-permute-start(bf16[256,1024]{1,0:T(8,128)(2,1)S(1)} %slice.108), channel_id=1, source_target_pairs={{0,2},{2,0},{4,6},{6,4},{8,10},{10,8},{12,14},{14,12},{16,18},{18,... | collective-permute-start | bytes 1572872 | tf_op jit(solution)/shard_map/ppermute | solution.py:34
  113.5 36.0 %collective-permute-start.16 = (bf16[256,1024]{1,0:T(8,128)(2,1)S(1)}, bf16[256,1024]{1,0:T(8,128)(2,1)S(1)}, u32[]{:S(2)}, u32[]{:S(2)}) collective-permute-start(bf16[256,1024]{1,0:T(8,128)(2,1)S(1)} %slice.107), channel_id=1, source_target_pairs={{0,4},{2,6},{4,0},{6,2},{8,12},{10,14},{12,8},{14,10},{16,20},{18,... | collective-permute-start | bytes 1572872 | tf_op jit(solution)/shard_map/ppermute | solution.py:34
  125.5 27.4 %collective-permute-start.9 = (bf16[256,1024]{1,0:T(8,128)(2,1)S(1)}, bf16[256,1024]{1,0:T(8,128)(2,1)S(1)}, u32[]{:S(2)}, u32[]{:S(2)}) collective-permute-start(bf16[256,1024]{1,0:T(8,128)(2,1)S(1)} %copy-done.27), channel_id=1, source_target_pairs={{0,1},{1,0},{2,3},{3,2},{4,5},{5,4},{6,7},{7,6},{8,9},{9,8},{10,11... | collective-permute-start | bytes 1572872 | tf_op jit(solution)/shard_map/ppermute | solution.py:38
  148.0 19.3 %collective-permute-start.28 = (bf16[256,1408]{1,0:T(8,128)(2,1)}, bf16[256,1408]{1,0:T(8,128)(2,1)S(1)}, u32[]{:S(2)}, u32[]{:S(2)}) collective-permute-start(bf16[256,1408]{1,0:T(8,128)(2,1)} %stack_body.7.refs_5_), channel_id=1, source_target_pairs={{0,8},{2,10},{4,12},{6,14},{8,0},{10,2},{12,4},{14,6},{16,24},{18,... | collective-permute-start | bytes 2162696 | tf_op jit(solution)/shard_map/ppermute | solution.py:34
  149.5 29.7 %collective-permute-start.29 = (bf16[256,1408]{1,0:T(8,128)(2,1)}, bf16[256,1408]{1,0:T(8,128)(2,1)S(1)}, u32[]{:S(2)}, u32[]{:S(2)}) collective-permute-start(bf16[256,1408]{1,0:T(8,128)(2,1)} %collective-permute-done.27.refs_6_), channel_id=1, source_target_pairs={{0,8},{2,10},{4,12},{6,14},{8,0},{10,2},{12,4},{14,6},{16,24},{18,... | collective-permute-start | bytes 2162696 | tf_op jit(solution)/shard_map/ppermute | solution.py:34
  161.0 18.3 %collective-permute-start.25 = (bf16[256,1408]{1,0:T(8,128)(2,1)S(1)}, bf16[256,1408]{1,0:T(8,128)(2,1)S(1)}, u32[]{:S(2)}, u32[]{:S(2)}) collective-permute-start(bf16[256,1408]{1,0:T(8,128)(2,1)S(1)} %slice.110), channel_id=1, source_target_pairs={{0,2},{2,0},{4,6},{6,4},{8,10},{10,8},{12,14},{14,12},{16,18},{18,... | collective-permute-start | bytes 2162696 | tf_op jit(solution)/shard_map/ppermute | solution.py:34
  163.7 15.5 %collective-permute-start.24 = (bf16[256,1408]{1,0:T(8,128)(2,1)S(1)}, bf16[256,1408]{1,0:T(8,128)(2,1)S(1)}, u32[]{:S(2)}, u32[]{:S(2)}) collective-permute-start(bf16[256,1408]{1,0:T(8,128)(2,1)S(1)} %slice.109), channel_id=1, source_target_pairs={{0,4},{2,6},{4,0},{6,2},{8,12},{10,14},{12,8},{14,10},{16,20},{18,... | collective-permute-start | bytes 2162696 | tf_op jit(solution)/shard_map/ppermute | solution.py:34
  165.2 14.0 %collective-permute-start.18 = (bf16[256,1024]{1,0:T(8,128)(2,1)S(1)}, bf16[256,1024]{1,0:T(8,128)(2,1)S(1)}, u32[]{:S(2)}, u32[]{:S(2)}) collective-permute-start(bf16[256,1024]{1,0:T(8,128)(2,1)S(1)} %get-tuple-element.132.mine_ref), channel_id=1, source_target_pairs={{0,1},{1,0},{2,3},{3,2},{4,5},{5,4},{6,7},{7,6},{8,9},{9,8},{10,11... | collective-permute-start | bytes 1572872 | tf_op jit(solution)/shard_map/ppermute | solution.py:38
  197.4 19.9 %collective-permute-start.34 = (bf16[256,1408]{1,0:T(8,128)(2,1)S(1)}, bf16[256,1408]{1,0:T(8,128)(2,1)S(1)}, u32[]{:S(2)}, u32[]{:S(2)}) collective-permute-start(bf16[256,1408]{1,0:T(8,128)(2,1)S(1)} %get-tuple-element.150), channel_id=1, source_target_pairs={{0,2},{2,0},{4,6},{6,4},{8,10},{10,8},{12,14},{14,12},{16,18},{18,... | collective-permute-start | bytes 2162696 | tf_op jit(solution)/shard_map/ppermute | solution.py:34
  198.7 18.7 %collective-permute-start.33 = (bf16[256,1408]{1,0:T(8,128)(2,1)S(1)}, bf16[256,1408]{1,0:T(8,128)(2,1)S(1)}, u32[]{:S(2)}, u32[]{:S(2)}) collective-permute-start(bf16[256,1408]{1,0:T(8,128)(2,1)S(1)} %get-tuple-element.149), channel_id=1, source_target_pairs={{0,4},{2,6},{4,0},{6,2},{8,12},{10,14},{12,8},{14,10},{16,20},{18,... | collective-permute-start | bytes 2162696 | tf_op jit(solution)/shard_map/ppermute | solution.py:34
  200.1 23.5 %collective-permute-start.45 = (bf16[256,1408]{1,0:T(8,128)(2,1)}, bf16[256,1408]{1,0:T(8,128)(2,1)}, u32[]{:S(2)}, u32[]{:S(2)}) collective-permute-start(bf16[256,1408]{1,0:T(8,128)(2,1)} %get-tuple-element.183), channel_id=1, source_target_pairs={{0,8},{2,10},{4,12},{6,14},{8,0},{10,2},{12,4},{14,6},{16,24},{18,... | collective-permute-start | bytes 2162696 | tf_op jit(solution)/shard_map/ppermute | solution.py:34
  222.2 34.8 %collective-permute-start.41 = (bf16[512,1408]{1,0:T(8,128)(2,1)}, bf16[512,1408]{1,0:T(8,128)(2,1)S(1)}, u32[]{:S(2)}, u32[]{:S(2)}) collective-permute-start(bf16[512,1408]{1,0:T(8,128)(2,1)} %get-tuple-element.174), channel_id=1, source_target_pairs={{0,2},{2,0},{4,6},{6,4},{8,10},{10,8},{12,14},{14,12},{16,18},{18,... | collective-permute-start | bytes 4325384 | tf_op jit(solution)/shard_map/ppermute | solution.py:34
  222.8 34.7 %collective-permute-start.42 = (bf16[512,1408]{1,0:T(8,128)(2,1)}, bf16[512,1408]{1,0:T(8,128)(2,1)S(1)}, u32[]{:S(2)}, u32[]{:S(2)}) collective-permute-start(bf16[512,1408]{1,0:T(8,128)(2,1)} %get-tuple-element.175), channel_id=1, source_target_pairs={{0,4},{2,6},{4,0},{6,2},{8,12},{10,14},{12,8},{14,10},{16,20},{18,... | collective-permute-start | bytes 4325384 | tf_op jit(solution)/shard_map/ppermute | solution.py:34
  224.9 33.7 %collective-permute-start.52 = (bf16[256,1408]{1,0:T(8,128)(2,1)S(1)}, bf16[256,1408]{1,0:T(8,128)(2,1)S(1)}, u32[]{:S(2)}, u32[]{:S(2)}) collective-permute-start(bf16[256,1408]{1,0:T(8,128)(2,1)S(1)} %add_convert_fusion), channel_id=1, source_target_pairs={{0,24},{2,26},{4,28},{6,30},{8,16},{10,18},{12,20},{14,22},{16,8},... | collective-permute-start | bytes 2162696 | tf_op jit(solution)/shard_map/ppermute | solution.py:34
  228.3 39.4 %collective-permute-start.47 = (bf16[256,1024]{1,0:T(8,128)(2,1)}, bf16[256,1024]{1,0:T(8,128)(2,1)}, u32[]{:S(2)}, u32[]{:S(2)}) collective-permute-start(bf16[256,1024]{1,0:T(8,128)(2,1)} %get-tuple-element.186), channel_id=1, source_target_pairs={{0,2},{2,0},{4,6},{6,4},{8,10},{10,8},{12,14},{14,12},{16,18},{18,... | collective-permute-start | bytes 1572872 | tf_op jit(solution)/shard_map/ppermute | solution.py:34
  229.3 38.4 %collective-permute-start.46 = (bf16[256,1024]{1,0:T(8,128)(2,1)}, bf16[256,1024]{1,0:T(8,128)(2,1)}, u32[]{:S(2)}, u32[]{:S(2)}) collective-permute-start(bf16[256,1024]{1,0:T(8,128)(2,1)} %get-tuple-element.184), channel_id=1, source_target_pairs={{0,4},{2,6},{4,0},{6,2},{8,12},{10,14},{12,8},{14,10},{16,20},{18,... | collective-permute-start | bytes 1572872 | tf_op jit(solution)/shard_map/ppermute | solution.py:34
  259.7 21.5 %collective-permute-start.54 = (bf16[64,2816]{1,0:T(8,128)(2,1)}, bf16[64,2816]{1,0:T(8,128)(2,1)}, u32[]{:S(2)}, u32[]{:S(2)}) collective-permute-start(bf16[64,2816]{1,0:T(8,128)(2,1)} %get-tuple-element.206), channel_id=1, source_target_pairs={{0,8},{2,10},{4,12},{6,14},{8,0},{10,2},{12,4},{14,6},{16,24},{18,... | collective-permute-start | bytes 1081352 | tf_op jit(solution)/shard_map/ppermute | solution.py:34
  260.5 25.1 %collective-permute-start.30 = (bf16[256,1024]{1,0:T(8,128)(2,1)}, bf16[256,1024]{1,0:T(8,128)(2,1)}, u32[]{:S(2)}, u32[]{:S(2)}) collective-permute-start(bf16[256,1024]{1,0:T(8,128)(2,1)} %get-tuple-element.141.mine_ref), channel_id=1, source_target_pairs={{0,1},{1,0},{2,3},{3,2},{4,5},{5,4},{6,7},{7,6},{8,9},{9,8},{10,11... | collective-permute-start | bytes 1572872 | tf_op jit(solution)/shard_map/ppermute | solution.py:38
  262.3 27.3 %all-to-all-start.2 = ((bf16[16,8,1024]{2,1,0:T(8,128)(2,1)}), bf16[16,8,1024]{2,1,0:T(8,128)(2,1)}, u32[]{:S(2)}, u32[]{:S(2)}) async-start(bf16[16,8,1024]{2,1,0:T(8,128)(2,1)} %bitcast.7), calls=%async_computation.2 | async-start | bytes 524288 | tf_op jit(solution)/shard_map/all_to_all | solution.py:724
  276.4 28.8 %collective-permute-start.53 = (bf16[64,2816]{1,0:T(8,128)(2,1)}, bf16[64,2816]{1,0:T(8,128)(2,1)}, u32[]{:S(2)}, u32[]{:S(2)}) collective-permute-start(bf16[64,2816]{1,0:T(8,128)(2,1)} %copy-done.49), channel_id=1, source_target_pairs={{0,8},{2,10},{4,12},{6,14},{8,0},{10,2},{12,4},{14,6},{16,24},{18,... | collective-permute-start | bytes 1081352 | tf_op jit(solution)/shard_map/ppermute | solution.py:34
  278.3 28.9 %collective-permute-start.49 = (bf16[512,1024]{1,0:T(8,128)(2,1)}, bf16[512,1024]{1,0:T(8,128)(2,1)}, u32[]{:S(2)}, u32[]{:S(2)}) collective-permute-start(bf16[512,1024]{1,0:T(8,128)(2,1)} %get-tuple-element.190), channel_id=1, source_target_pairs={{0,4},{2,6},{4,0},{6,2},{8,12},{10,14},{12,8},{14,10},{16,20},{18,... | collective-permute-start | bytes 3145736 | tf_op jit(solution)/shard_map/ppermute | solution.py:34
  279.8 31.2 %collective-permute-start.48 = (bf16[512,1024]{1,0:T(8,128)(2,1)}, bf16[512,1024]{1,0:T(8,128)(2,1)}, u32[]{:S(2)}, u32[]{:S(2)}) collective-permute-start(bf16[512,1024]{1,0:T(8,128)(2,1)} %get-tuple-element.188), channel_id=1, source_target_pairs={{0,2},{2,0},{4,6},{6,4},{8,10},{10,8},{12,14},{14,12},{16,18},{18,... | collective-permute-start | bytes 3145736 | tf_op jit(solution)/shard_map/ppermute | solution.py:34
  283.2 22.4 %collective-permute-start.55 = (bf16[64,2816]{1,0:T(8,128)(2,1)}, bf16[64,2816]{1,0:T(8,128)(2,1)}, u32[]{:S(2)}, u32[]{:S(2)}) collective-permute-start(bf16[64,2816]{1,0:T(8,128)(2,1)} %add_convert_fusion.1), channel_id=1, source_target_pairs={{0,24},{2,26},{4,28},{6,30},{8,16},{10,18},{12,20},{14,22},{16,8},... | collective-permute-start | bytes 1081352 | tf_op jit(solution)/shard_map/ppermute | solution.py:34
  285.6 19.0 %collective-permute-start.37 = (f32[26,128]{1,0:T(8,128)S(1)}, f32[26,128]{1,0:T(8,128)S(1)}, u32[]{:S(2)}, u32[]{:S(2)}) collective-permute-start(f32[26,128]{1,0:T(8,128)S(1)} %maximum_bitcast_fusion), channel_id=1, source_target_pairs={{0,2},{2,0},{4,6},{6,4},{8,10},{10,8},{12,14},{14,12},{16,18},{18,... | collective-permute-start | bytes 39944 | tf_op jit(solution)/shard_map/ppermute | solution.py:34
  304.6 20.0 %collective-permute-start.62 = (bf16[256,1408]{1,0:T(8,128)(2,1)}, bf16[256,1408]{1,0:T(8,128)(2,1)S(1)}, u32[]{:S(2)}, u32[]{:S(2)}) collective-permute-start(bf16[256,1408]{1,0:T(8,128)(2,1)} %copy-done.42), channel_id=1, source_target_pairs={{0,8},{2,10},{4,12},{6,14},{8,0},{10,2},{12,4},{14,6},{16,24},{18,... | collective-permute-start | bytes 2162696 | tf_op jit(solution)/shard_map/ppermute | solution.py:34
  305.7 26.2 %collective-permute-start.44 = (bf16[256,1024]{1,0:T(8,128)(2,1)}, bf16[256,1024]{1,0:T(8,128)(2,1)}, u32[]{:S(2)}, u32[]{:S(2)}) collective-permute-start(bf16[256,1024]{1,0:T(8,128)(2,1)} %copy-done.46), channel_id=1, source_target_pairs={{0,2},{2,0},{4,6},{6,4},{8,10},{10,8},{12,14},{14,12},{16,18},{18,... | collective-permute-start | bytes 1572872 | tf_op jit(solution)/shard_map/ppermute | solution.py:34
  307.3 24.6 %collective-permute-start.43 = (bf16[256,1024]{1,0:T(8,128)(2,1)}, bf16[256,1024]{1,0:T(8,128)(2,1)}, u32[]{:S(2)}, u32[]{:S(2)}) collective-permute-start(bf16[256,1024]{1,0:T(8,128)(2,1)} %copy-done.45), channel_id=1, source_target_pairs={{0,4},{2,6},{4,0},{6,2},{8,12},{10,14},{12,8},{14,10},{16,20},{18,... | collective-permute-start | bytes 1572872 | tf_op jit(solution)/shard_map/ppermute | solution.py:34
  315.2 21.2 %collective-permute-start.57 = (bf16[64,2048]{1,0:T(8,128)(2,1)}, bf16[64,2048]{1,0:T(8,128)(2,1)S(1)}, u32[]{:S(2)}, u32[]{:S(2)}) collective-permute-start(bf16[64,2048]{1,0:T(8,128)(2,1)} %get-tuple-element.210), channel_id=1, source_target_pairs={{0,8},{2,10},{4,12},{6,14},{8,0},{10,2},{12,4},{14,6},{16,24},{18,... | collective-permute-start | bytes 786440 | tf_op jit(solution)/shard_map/ppermute | solution.py:34
  318.1 26.5 %all-to-all-start.3 = ((bf16[16,8,1024]{2,1,0:T(8,128)(2,1)}), bf16[16,8,1024]{2,1,0:T(8,128)(2,1)}, u32[]{:S(2)}, u32[]{:S(2)}) async-start(bf16[16,8,1024]{2,1,0:T(8,128)(2,1)} %broadcast_select_fusion), calls=%async_computation.3 | async-start | bytes 524288 | tf_op jit(solution)/shard_map/all_to_all | solution.py:727
  335.9 22.0 %collective-permute-start.51 = (bf16[512,1024]{1,0:T(8,128)(2,1)}, bf16[512,1024]{1,0:T(8,128)(2,1)S(1)}, u32[]{:S(2)}, u32[]{:S(2)}) collective-permute-start(bf16[512,1024]{1,0:T(8,128)(2,1)} %get-tuple-element.193), channel_id=1, source_target_pairs={{0,4},{2,6},{4,0},{6,2},{8,12},{10,14},{12,8},{14,10},{16,20},{18,... | collective-permute-start | bytes 3145736 | tf_op jit(solution)/shard_map/ppermute | solution.py:34
  336.4 21.6 %collective-permute-start.50 = (bf16[512,1024]{1,0:T(8,128)(2,1)}, bf16[512,1024]{1,0:T(8,128)(2,1)S(1)}, u32[]{:S(2)}, u32[]{:S(2)}) collective-permute-start(bf16[512,1024]{1,0:T(8,128)(2,1)} %get-tuple-element.191), channel_id=1, source_target_pairs={{0,2},{2,0},{4,6},{6,4},{8,10},{10,8},{12,14},{14,12},{16,18},{18,... | collective-permute-start | bytes 3145736 | tf_op jit(solution)/shard_map/ppermute | solution.py:34
  341.2 18.6 %collective-permute-start.63 = (bf16[64,1408]{1,0:T(8,128)(2,1)}, bf16[64,1408]{1,0:T(8,128)(2,1)S(1)}, u32[]{:S(2)}, u32[]{:S(2)}) collective-permute-start(bf16[64,1408]{1,0:T(8,128)(2,1)} %get-tuple-element.218), channel_id=1, source_target_pairs={{0,4},{2,6},{4,0},{6,2},{8,12},{10,14},{12,8},{14,10},{16,20},{18,... | collective-permute-start | bytes 540680 | tf_op jit(solution)/shard_map/ppermute | solution.py:34
  344.6 15.4 %collective-permute-start.65 = (bf16[64,1408]{1,0:T(8,128)(2,1)}, bf16[64,1408]{1,0:T(8,128)(2,1)S(1)}, u32[]{:S(2)}, u32[]{:S(2)}) collective-permute-start(bf16[64,1408]{1,0:T(8,128)(2,1)} %add_convert_fusion.4), channel_id=1, source_target_pairs={{0,2},{2,0},{4,6},{6,4},{8,10},{10,8},{12,14},{14,12},{16,18},{18,... | collective-permute-start | bytes 540680 | tf_op jit(solution)/shard_map/ppermute | solution.py:34
  (109 other events, 936.9 us)
where the time goes:
time: 380 us; the launch traced here: 379 us
  waiting for transfers between devices  123 us (32%)
  starting transfers between devices  103 us (27%)
  Pallas kernels  86.8 us (23%)
  local copies, waits for them, and re-layouts  49.2 us (13%)
  other arithmetic  14.8 us (4%)
    ppermute x58, waiting for transfers between devices, swap_dp(): lax.ppermute(value, 'dp', [(one, one ^ mask) for one in range(devices)])  123 us
    ppermute x58, starting transfers between devices, swap_dp(): lax.ppermute(value, 'dp', [(one, one ^ mask) for one in range(devices)])  82.1 us
    pallas_call x18, Pallas kernels, call(): pl.pallas_call(body, out_shape=list(out_shape), in_specs=[smem] * len(sca...  78.2 us
    unnamed x181, local copies, waits for them, and re-layouts  31.2 us
    all_to_all x2, starting transfers between devices, deal(): lax.all_to_all(jnp.take(first, order, axis=0), 'dp', split_axis=0, concat...  10.8 us
    all_to_all x2, starting transfers between devices, deal(): lax.all_to_all(value.reshape(devices, rows // devices, width), 'dp', spli...  9.97 us
    slice x6, local copies, waits for them, and re-layouts, gather_lower(): left, right = (x_part[:rows], y_part[rows:])  8.68 us
    pallas_call x3, Pallas kernels, merge_quarters(): pl.pallas_call(merge_body, out_shape=[low_shape(*x_part.shape), low_shape...  8.55 us
  transfers between devices with their start and end apart: 70, of which 23 were waited for; matrix products, arithmetic and copies ran while one was open for 8% of the time, Pallas kernels for 19%

commit v1 on v0

--- a/solution.py
+++ b/solution.py
@@ -208,14 +208,20 @@
     return jax.ShapeDtypeStruct(shape, FULL)
 
 
-def call(body, out_shape, scalars, arrays, scratch=(), flops=0):
+def call(body, out_shape, scalars, arrays, scratch=(), flops=0, sent=()):
     vmem = pl.BlockSpec(memory_space=pltpu.VMEM)
     smem = pl.BlockSpec(memory_space=pltpu.SMEM)
     return pl.pallas_call(
         body,
         out_shape=list(out_shape),
         in_specs=[smem] * len(scalars) + [vmem] * len(arrays),
-        out_specs=[vmem] * len(out_shape),
+        out_specs=[
+            pl.BlockSpec(one.shape, lambda step: (0, 0), pipeline_mode=pl.Buffered(1))
+            if number in sent
+            else vmem
+            for number, one in enumerate(out_shape)
+        ],
+        grid=(1,) if sent else (),
         scratch_shapes=list(scratch),
         name=getattr(body, "func", body).__name__,
         cost_estimate=pl.CostEstimate(
@@ -571,7 +577,7 @@
     rows = terms[0].shape[0] // (4 * sides_held)
     width = terms[0].shape[1] * sides_held
     kinds = [full_shape, full_shape, low_shape, low_shape]
-    return call(fold_body, [kind(rows, width) for kind in kinds], (), terms)
+    return call(fold_body, [kind(rows, width) for kind in kinds], (), terms, sent=(2, 3))
 
 
 def stack_body(*refs):
@@ -588,7 +594,9 @@
 
 
 def stack_quarter(parts, shapes):
-    return call(stack_body, [low_shape(*shape) for shape in shapes], (), parts)
+    return call(
+        stack_body, [low_shape(*shape) for shape in shapes], (), parts, sent=range(len(shapes))
+    )
 
 
 def merge_body(x_in, y_in, left, right, x_out, y_out):
@@ -622,7 +630,7 @@
     if len(masks) == 2:
         one = swap_dp(value, masks[0], devices)
         two = swap_dp(value, masks[1], devices)
-        return [value, one, two, swap_dp(one, masks[1], devices)]
+        return [value, one, two, swap_dp(after(one, two), masks[1], devices)]
     for mask in masks:
         value = jnp.concatenate([value, swap_dp(value, mask, devices)], axis=0)
     return [value]
@@ -660,10 +668,11 @@
 
 
 def reduce_lower(pieces, came, devices, wait=()):
-    x_part, y_part = merge_quarters(*pieces[1:3], *came)
+    merged = merge_quarters(*pieces[1:3], *came)
+    x_part, y_part = merged
     if wait:
         x_part, y_part = after(x_part, *wait), after(y_part, *wait)
-    return [pieces[0], swap_dp(x_part, 1, devices), swap_dp(y_part, 2, devices)]
+    return [pieces[0], swap_dp(x_part, 1, devices), swap_dp(y_part, 2, devices)], merged
 
 
 def reduce_upper(terms, devices, wait=()):
@@ -780,7 +789,7 @@
     cross_blocks = gather_upper(cross_own, devices, self_blocks[1:3])
     self_w = gather_lower(self_first, devices)
     (cross_first,) = stack_sides(cross_blocks, [2 * inner])
-    cross_w = gather_lower(cross_first, devices, self_w[1:2], self_w[2:3])
+    cross_w = gather_lower(cross_first, devices, self_w[1:3], self_w[1:3], self_w[3:])
     feed_blocks = gather_upper(feed_own, devices, cross_blocks[1:3])
     (feed_first,) = stack_sides(feed_blocks, [feed])
     if across:
@@ -885,6 +894,7 @@
             pltpu.VMEM((rows, model), FULL),
         ],
         flops=18 * rows * model * feed,
+        sent=range(3, 12),
     )
     hidden_two, partial, dpartial = outs[:3]
     dfeed, ddown = outs[3:8], outs[8:12]
@@ -936,14 +946,15 @@
         ),
         scratch=attention_scratch,
         flops=9 * unit,
+        sent=range(5, 10),
     )
     grad_two, dgain_feed, dpartial, keep, away = outs[:5]
     dcross = outs[5:10]
-    feed_terms = reduce_lower(
+    feed_terms, feed_merged = reduce_lower(
         dfeed, [after(one, dpartial) for one in feed_came], devices
     )
     cross_came = reduce_last(dcross, devices, down_came[:1])
-    cross_terms = reduce_lower(dcross, cross_came, devices, feed_terms[1:])
+    cross_terms, cross_merged = reduce_lower(dcross, cross_came, devices, feed_terms[1:])
     (encoder_half,) = call(
         encoder_body,
         [low_shape(half, model)],
@@ -979,11 +990,12 @@
         ),
         scratch=attention_scratch,
         flops=10 * unit,
+        sent=range(4, 9),
     )
     grad_one, dgain_cross, dpartial, diagonal = outs[:4]
     dself = outs[4:9]
     self_came = reduce_last(dself, devices, feed_terms[1:])
-    self_terms = reduce_lower(dself, self_came, devices, cross_terms[1:])
+    self_terms, self_merged = reduce_lower(dself, self_came, devices, cross_terms[1:])
     input_grad, dgains, dtable = call(
         finish_body,
         [low_shape(rows, model), full_shape(3, model), full_shape(buckets, heads)],
@@ -1008,7 +1020,7 @@
         feed_sums = reduce_upper(feed_terms, devices, down_terms[2:])
         down_sum = reduce_across_first(down_terms, devices)
     else:
-        down_sum = reduce_upper(reduce_lower(ddown, down_came, devices), devices)
+        down_sum = reduce_upper(reduce_lower(ddown, down_came, devices)[0], devices)
         feed_sums = reduce_upper(feed_terms, devices)
     cross_sums = reduce_upper(cross_terms, devices, (feed_sums,))
     self_sums = reduce_upper(self_terms, devices, (cross_sums,))

time: 380 us -> 376 us (0.989)
  starting transfers between devices: 103 us -> 95.5 us
    ppermute x58, starting transfers between devices: 82.1 us -> 76.3 us  [swap_dp(): lax.ppermute(value, 'dp', [(one, one ^ mask) for one in range(devices)])]
  transfers between devices with their start and end apart: 70 -> 70, of which waited for: 23 -> 21; matrix products, arithmetic and copies ran while one was open for 8% -> 9% of each run, Pallas kernels for 19% -> 19%
where the time goes in v1:
time: 376 us; the launch traced here: 374 us
  waiting for transfers between devices  125 us (33%)
  starting transfers between devices  95.5 us (25%)
  Pallas kernels  86.8 us (23%)
  local copies, waits for them, and re-layouts  49.8 us (13%)
  other arithmetic  15.6 us (4%)
    ppermute x58, waiting for transfers between devices, swap_dp(): lax.ppermute(value, 'dp', [(one, one ^ mask) for one in range(devices)])  125 us
    pallas_call x18, Pallas kernels, call(): pl.pallas_call(body, out_shape=list(out_shape), in_specs=[smem] * len(sca...  78.2 us
    ppermute x58, starting transfers between devices, swap_dp(): lax.ppermute(value, 'dp', [(one, one ^ mask) for one in range(devices)])  76.3 us
    unnamed x181, local copies, waits for them, and re-layouts  31.8 us
    all_to_all x2, starting transfers between devices, deal(): lax.all_to_all(value.reshape(devices, rows // devices, width), 'dp', spli...  9.73 us
    all_to_all x2, starting transfers between devices, deal(): lax.all_to_all(jnp.take(first, order, axis=0), 'dp', split_axis=0, concat...  9.27 us
    slice x6, local copies, waits for them, and re-layouts, gather_lower(): left, right = (x_part[:rows], y_part[rows:])  8.68 us
    pallas_call x3, Pallas kernels, merge_quarters(): pl.pallas_call(merge_body, out_shape=[low_shape(*x_part.shape), low_shape...  8.55 us
  transfers between devices with their start and end apart: 70, of which 21 were waited for; matrix products, arithmetic and copies ran while one was open for 9% of the time, Pallas kernels for 19%

profile of v1, /device:TPU:0, one launch (start us, length us, event | category | flops | bytes accessed | tf_op | source)
XLA Modules:
  0.0 374.4 jit_solution(15313590718688726867)
XLA Ops:
  4.1 5.0 %collective-permute-start = (bf16[64,2048]{1,0:T(8,128)(2,1)S(1)}, bf16[64,2048]{1,0:T(8,128)(2,1)S(1)}, u32[]{:S(2)}, u32[]{:S(2)}) collective-permute-start(bf16[64,2048]{1,0:T(8,128)(2,1)S(1)} %constant_dynamic-update-slice_fusion.refs_0_), channel_id=1, source_target_pairs={{0,24},{2,26},{4,28},{6,30},{8,16},{10,18},{12,20},{14,22},{16,8},... | collective-permute-start | bytes 786440 | tf_op jit(solution)/shard_map/ppermute | solution.py:34
  9.2 7.2 %collective-permute-done.refs_1_ = bf16[64,2048]{1,0:T(8,128)(2,1)S(1)} collective-permute-done((bf16[64,2048]{1,0:T(8,128)(2,1)S(1)}, bf16[64,2048]{1,0:T(8,128)(2,1)S(1)}, u32[]{:S(2)}, u32[]{:S(2)}) %collective-permute-start) | collective-permute-done | bytes 262176 | tf_op jit(solution)/shard_map/ppermute | solution.py:34
  16.4 4.8 %collective-permute-done.1.refs_2_ = bf16[64,2048]{1,0:T(8,128)(2,1)S(1)} collective-permute-done((bf16[64,2048]{1,0:T(8,128)(2,1)S(1)}, bf16[64,2048]{1,0:T(8,128)(2,1)S(1)}, u32[]{:S(2)}, u32[]{:S(2)}) %collective-permute-start.1) | collective-permute-done | bytes 262176 | tf_op jit(solution)/shard_map/ppermute | solution.py:34
  26.6 4.3 %all-to-all-start = ((bf16[16,8,1024]{2,1,0:T(8,128)(2,1)}), bf16[16,8,1024]{2,1,0:T(8,128)(2,1)}, u32[]{:S(2)}, u32[]{:S(2)}) async-start(bf16[16,8,1024]{2,1,0:T(8,128)(2,1)} %dynamic-slice_bitcast_fusion), calls=%async_computation | async-start | bytes 524288 | tf_op jit(solution)/shard_map/all_to_all | solution.py:733
  35.9 3.4 collective-permute-start.11
  40.2 6.7 %collective-permute-done.11.refs_1_ = bf16[64,2048]{1,0:T(8,128)(2,1)S(1)} collective-permute-done((bf16[64,2048]{1,0:T(8,128)(2,1)S(1)}, bf16[64,2048]{1,0:T(8,128)(2,1)S(1)}, u32[]{:S(2)}, u32[]{:S(2)}) %collective-permute-start.11) | collective-permute-done | bytes 262176 | tf_op jit(solution)/shard_map/ppermute | solution.py:34
  46.9 2.7 collective-permute-done.12.refs_2_
  52.5 12.4 %collective-permute-done.13.refs_3_ = bf16[64,2048]{1,0:T(8,128)(2,1)S(1)} collective-permute-done((bf16[64,2048]{1,0:T(8,128)(2,1)S(1)}, bf16[64,2048]{1,0:T(8,128)(2,1)S(1)}, u32[]{:S(2)}, u32[]{:S(2)}) %collective-permute-start.13) | collective-permute-done | bytes 262176 | tf_op jit(solution)/shard_map/ppermute | solution.py:34
  66.6 1.9 slice.105
  72.2 2.0 collective-permute-start.8
  75.6 2.0 collective-permute-start.21
  79.7 3.2 prepare_body.1
  85.4 2.2 gather_fusion
  89.3 4.6 %all-to-all-start.1 = ((bf16[16,8,1024]{2,1,0:T(8,128)(2,1)}), bf16[16,8,1024]{2,1,0:T(8,128)(2,1)}, u32[]{:S(2)}, u32[]{:S(2)}) async-start(bf16[16,8,1024]{2,1,0:T(8,128)(2,1)} %broadcast_select_fusion.1), calls=%async_computation.1 | async-start | bytes 524288 | tf_op jit(solution)/shard_map/all_to_all | solution.py:736
  93.9 1.9 collective-permute-start.26
  96.8 2.4 stack_body.6.refs_0_
  99.3 8.0 %self_forward_body.1 = (bf16[256,512]{1,0:T(8,128)(2,1)S(1)}, bf16[256,512]{1,0:T(8,128)(2,1)S(1)}, bf16[256,512]{1,0:T(8,128)(2,1)S(1)}, bf16[256,512]{1,0:T(8,128)(2,1)S(1)}, bf16[256,1024]{1,0:T(8,128)(2,1)S(1)}) custom-call(s32[1]{0:T(128)} %bitcast.length_ref, f32[8,512]{1,0:T(8,128)S(1)} %convolution_bitcast_fusion.bias_ref, ...), custom_call_target="tpu_custom_call" | custom-call | flops 1342177280 | bytes 1024 | tf_op jit(solution)/shard_map/self_forward_body/pallas_call | solution.py:214
  111.1 3.3 collective-permute-start.27
  118.8 6.5 %collective-permute-done.27.refs_6_ = bf16[256,1408]{1,0:T(8,128)(2,1)} collective-permute-done((bf16[256,1408]{1,0:T(8,128)(2,1)}, bf16[256,1408]{1,0:T(8,128)(2,1)}, u32[]{:S(2)}, u32[]{:S(2)}) %collective-permute-start.27) | collective-permute-done | bytes 720928 | tf_op jit(solution)/shard_map/ppermute | solution.py:34
  125.3 22.4 %collective-permute-done.17.refs_4_ = bf16[256,1024]{1,0:T(8,128)(2,1)S(1)} collective-permute-done((bf16[256,1024]{1,0:T(8,128)(2,1)S(1)}, bf16[256,1024]{1,0:T(8,128)(2,1)S(1)}, u32[]{:S(2)}, u32[]{:S(2)}) %collective-permute-start.17) | collective-permute-done | bytes 524320 | tf_op jit(solution)/shard_map/ppermute | solution.py:34
  149.8 2.9 memory_body.1
  152.8 6.4 %cross_forward_body.1 = (f32[256,1024]{1,0:T(8,128)S(1)}, bf16[256,1024]{1,0:T(8,128)(2,1)S(1)}, bf16[256,512]{1,0:T(8,128)(2,1)S(1)}, bf16[256,512]{1,0:T(8,128)(2,1)S(1)}, bf16[256,1024]{1,0:T(8,128)(2,1)S(1)}) custom-call(bf16[256,1024]{1,0:T(8,128)(2,1)S(1)} %copy-done.4, bf16[256,1024]{1,0:T(8,128)(2,1)S(1)} %copy-done.27, ...), custom_call_target="tpu_custom_call" | custom-call | flops 805306368 | bytes 1024 | tf_op jit(solution)/shard_map/cross_forward_body/pallas_call | solution.py:214
  165.0 2.0 collective-permute-done.28.refs_7_
  167.0 8.1 %collective-permute-done.29.refs_8_ = bf16[256,1408]{1,0:T(8,128)(2,1)S(1)} collective-permute-done((bf16[256,1408]{1,0:T(8,128)(2,1)}, bf16[256,1408]{1,0:T(8,128)(2,1)S(1)}, u32[]{:S(2)}, u32[]{:S(2)}) %collective-permute-start.29) | collective-permute-done | bytes 720928 | tf_op jit(solution)/shard_map/ppermute | solution.py:34
  176.0 15.5 %feed_body.1 = (f32[256,1024]{1,0:T(8,128)}, bf16[256,1024]{1,0:T(8,128)(2,1)}, bf16[256,1024]{1,0:T(8,128)(2,1)S(1)}, bf16[512,1408]{1,0:T(8,128)(2,1)}, bf16[5...) custom-call(f32[256,1024]{1,0:T(8,128)} %copy-done.41, ...), custom_call_target="tpu_custom_call" | custom-call | flops 6643777536 | bytes 1024 | tf_op jit(solution)/shard_map/feed_body/pallas_call | solution.py:214
  197.4 11.9 %cross_backward_body.1 = (f32[256,1024]{1,0:T(8,128)S(1)}, f32[1,1024]{1,0:T(1,128)S(1)}, bf16[256,1024]{1,0:T(8,128)(2,1)S(1)}, bf16[128,1024]{1,0:T(8,128)(2,1...) custom-call(f32[256,1024]{1,0:T(8,128)} %get-tuple-element.148.hidde, ...), custom_call_target="tpu_custom_call" | custom-call | flops 2415919104 | bytes 1024 | tf_op jit(solution)/shard_map/cross_backward_body/pallas_call | solution.py:214
  214.9 3.1 merge_body.3
  220.8 3.3 collective-permute-start.52
  226.1 12.6 %self_backward_body.1 = (f32[256,1024]{1,0:T(8,128)S(1)}, f32[1,1024]{1,0:T(1,128)S(1)}, bf16[256,1024]{1,0:T(8,128)(2,1)S(1)}, f32[8,512]{1,0:T(8,128)S(1)}, bf...) custom-call(s32[1]{0:T(128)} %bitcast.length_ref, ...), custom_call_target="tpu_custom_call" | custom-call | flops 2684354560 | bytes 1024 | tf_op jit(solution)/shard_map/self_backward_body/pallas_call | solution.py:214
  243.3 9.5 %collective-permute-done.41.refs_1_ = bf16[512,1408]{1,0:T(8,128)(2,1)S(1)} collective-permute-done((bf16[512,1408]{1,0:T(8,128)(2,1)}, bf16[512,1408]{1,0:T(8,128)(2,1)S(1)}, u32[]{:S(2)}, u32[]{:S(2)}) %collective-permute-start.41) | collective-permute-done | bytes 1441824 | tf_op jit(solution)/shard_map/ppermute | solution.py:34
  258.2 5.4 %all-to-all-start.2 = ((bf16[16,8,1024]{2,1,0:T(8,128)(2,1)}), bf16[16,8,1024]{2,1,0:T(8,128)(2,1)}, u32[]{:S(2)}, u32[]{:S(2)}) async-start(bf16[16,8,1024]{2,1,0:T(8,128)(2,1)} %bitcast.7), calls=%async_computation.2 | async-start | bytes 524288 | tf_op jit(solution)/shard_map/all_to_all | solution.py:733
  263.6 2.7 merge_body.5
  267.6 4.5 %finish_body.1 = (bf16[256,1024]{1,0:T(8,128)(2,1)}, f32[3,1024]{1,0:T(4,128)S(1)}, f32[32,8]{1,0:T(8,128)S(1)}) custom-call(s32[1]{0:T(128)} %bitcast.length_ref, bf16[1024,1024]{1,0:T(8,128)(2,1)S(1)} %get-tuple-element.124.permute_ref, bf16[256,1024]{1,0:T(8,128)(2,1)S(1)} %copy-done.5, bf16[256,1024]{1,0:T(8,128)(2,1)S(1)} %get-tuple-element.164.mine_ref, ...), custom_call_target="tpu_custom_call" | custom-call | flops 536870912 | bytes 1024 | tf_op jit(solution)/shard_map/finish_body/pallas_call | solution.py:214
  272.2 1.9 collective-permute-start.53
  277.1 2.0 add_convert_fusion.1
  279.1 2.4 collective-permute-start.55
  282.1 3.4 output_body.1
  287.1 13.3 %collective-permute-done.37 = f32[26,128]{1,0:T(8,128)S(1)} collective-permute-done((f32[26,128]{1,0:T(8,128)S(1)}, f32[26,128]{1,0:T(8,128)S(1)}, u32[]{:S(2)}, u32[]{:S(2)}) %collective-permute-start.37) | collective-permute-done | bytes 13344 | tf_op jit(solution)/shard_map/ppermute | solution.py:34
  304.6 2.3 convert_add_fusion
  306.9 2.6 fold_body.5
  314.0 4.7 %all-to-all-start.3 = ((bf16[16,8,1024]{2,1,0:T(8,128)(2,1)}), bf16[16,8,1024]{2,1,0:T(8,128)(2,1)}, u32[]{:S(2)}, u32[]{:S(2)}) async-start(bf16[16,8,1024]{2,1,0:T(8,128)(2,1)} %broadcast_select_fusion), calls=%async_computation.3 | async-start | bytes 524288 | tf_op jit(solution)/shard_map/all_to_all | solution.py:736
  323.0 3.0 collective-permute-done.39
  327.7 2.7 merge_body.4
  337.1 2.0 collective-permute-start.63
  341.0 2.4 collective-permute-done.58
  344.7 9.0 %collective-permute-done.51.refs_2_ = bf16[512,1024]{1,0:T(8,128)(2,1)S(1)} collective-permute-done((bf16[512,1024]{1,0:T(8,128)(2,1)}, bf16[512,1024]{1,0:T(8,128)(2,1)S(1)}, u32[]{:S(2)}, u32[]{:S(2)}) %collective-permute-start.51) | collective-permute-done | bytes 1048608 | tf_op jit(solution)/shard_map/ppermute | solution.py:34
  357.5 6.1 %collective-permute-done.60 = bf16[64,2048]{1,0:T(8,128)(2,1)S(1)} collective-permute-done((bf16[64,2048]{1,0:T(8,128)(2,1)S(1)}, bf16[64,2048]{1,0:T(8,128)(2,1)S(1)}, u32[]{:S(2)}, u32[]{:S(2)}) %collective-permute-start.60) | collective-permute-done | bytes 262176 | tf_op jit(solution)/shard_map/ppermute | solution.py:34
  366.4 5.5 %collective-permute-done.61 = bf16[64,2048]{1,0:T(8,128)(2,1)S(1)} collective-permute-done((bf16[64,2048]{1,0:T(8,128)(2,1)S(1)}, bf16[64,2048]{1,0:T(8,128)(2,1)S(1)}, u32[]{:S(2)}, u32[]{:S(2)}) %collective-permute-start.61) | collective-permute-done | bytes 262176 | tf_op jit(solution)/shard_map/ppermute | solution.py:34
  (348 shorter events, 114.5 us)
Async XLA Ops:
  26.6 58.8 %all-to-all-start = ((bf16[16,8,1024]{2,1,0:T(8,128)(2,1)}), bf16[16,8,1024]{2,1,0:T(8,128)(2,1)}, u32[]{:S(2)}, u32[]{:S(2)}) async-start(bf16[16,8,1024]{2,1,0:T(8,128)(2,1)} %dynamic-slice_bitcast_fusion), calls=%async_computation | async-start | bytes 524288 | tf_op jit(solution)/shard_map/all_to_all | solution.py:733
  32.5 32.6 %collective-permute-start.5 = (bf16[512,1024]{1,0:T(8,128)(2,1)S(1)}, bf16[512,1024]{1,0:T(8,128)(2,1)}, u32[]{:S(2)}, u32[]{:S(2)}) collective-permute-start(bf16[512,1024]{1,0:T(8,128)(2,1)S(1)} %stack_body.4.refs_0_), channel_id=1, source_target_pairs={{0,2},{2,0},{4,6},{6,4},{8,10},{10,8},{12,14},{14,12},{16,18},{18,... | collective-permute-start | bytes 3145736 | tf_op jit(solution)/shard_map/ppermute | solution.py:34
  34.3 30.8 %collective-permute-start.6 = (bf16[512,1024]{1,0:T(8,128)(2,1)S(1)}, bf16[512,1024]{1,0:T(8,128)(2,1)}, u32[]{:S(2)}, u32[]{:S(2)}) collective-permute-start(bf16[512,1024]{1,0:T(8,128)(2,1)S(1)} %stack_body.4.refs_0_), channel_id=1, source_target_pairs={{0,4},{2,6},{4,0},{6,2},{8,12},{10,14},{12,8},{14,10},{16,20},{18,... | collective-permute-start | bytes 3145736 | tf_op jit(solution)/shard_map/ppermute | solution.py:34
  49.6 15.3 %collective-permute-start.13 = (bf16[64,2048]{1,0:T(8,128)(2,1)S(1)}, bf16[64,2048]{1,0:T(8,128)(2,1)S(1)}, u32[]{:S(2)}, u32[]{:S(2)}) collective-permute-start(bf16[64,2048]{1,0:T(8,128)(2,1)S(1)} %collective-permute-done.11.refs_1_), channel_id=1, source_target_pairs={{0,8},{2,10},{4,12},{6,14},{8,0},{10,2},{12,4},{14,6},{16,24},{18,... | collective-permute-start | bytes 786440 | tf_op jit(solution)/shard_map/ppermute | solution.py:34
  51.4 20.8 %collective-permute-start.19 = (bf16[64,2816]{1,0:T(8,128)(2,1)S(1)}, bf16[64,2816]{1,0:T(8,128)(2,1)}, u32[]{:S(2)}, u32[]{:S(2)}) collective-permute-start(bf16[64,2816]{1,0:T(8,128)(2,1)S(1)} %pad_maximum_fusion.refs_0_), channel_id=1, source_target_pairs={{0,24},{2,26},{4,28},{6,30},{8,16},{10,18},{12,20},{14,22},{16,8},... | collective-permute-start | bytes 1081352 | tf_op jit(solution)/shard_map/ppermute | solution.py:34
  65.1 43.0 %collective-permute-start.15 = (bf16[512,1024]{1,0:T(8,128)(2,1)S(1)}, bf16[512,1024]{1,0:T(8,128)(2,1)}, u32[]{:S(2)}, u32[]{:S(2)}) collective-permute-start(bf16[512,1024]{1,0:T(8,128)(2,1)S(1)} %stack_body.5.refs_0_), channel_id=1, source_target_pairs={{0,4},{2,6},{4,0},{6,2},{8,12},{10,14},{12,8},{14,10},{16,20},{18,... | collective-permute-start | bytes 3145736 | tf_op jit(solution)/shard_map/ppermute | solution.py:34
  65.1 43.2 %collective-permute-start.14 = (bf16[512,1024]{1,0:T(8,128)(2,1)S(1)}, bf16[512,1024]{1,0:T(8,128)(2,1)}, u32[]{:S(2)}, u32[]{:S(2)}) collective-permute-start(bf16[512,1024]{1,0:T(8,128)(2,1)S(1)} %stack_body.5.refs_0_), channel_id=1, source_target_pairs={{0,2},{2,0},{4,6},{6,4},{8,10},{10,8},{12,14},{14,12},{16,18},{18,... | collective-permute-start | bytes 3145736 | tf_op jit(solution)/shard_map/ppermute | solution.py:34
  68.5 30.7 %collective-permute-start.7 = (bf16[256,1024]{1,0:T(8,128)(2,1)}, bf16[256,1024]{1,0:T(8,128)(2,1)}, u32[]{:S(2)}, u32[]{:S(2)}) collective-permute-start(bf16[256,1024]{1,0:T(8,128)(2,1)} %slice.105), channel_id=1, source_target_pairs={{0,4},{2,6},{4,0},{6,2},{8,12},{10,14},{12,8},{14,10},{16,20},{18,... | collective-permute-start | bytes 1572872 | tf_op jit(solution)/shard_map/ppermute | solution.py:34
  72.2 27.0 %collective-permute-start.8 = (bf16[256,1024]{1,0:T(8,128)(2,1)}, bf16[256,1024]{1,0:T(8,128)(2,1)}, u32[]{:S(2)}, u32[]{:S(2)}) collective-permute-start(bf16[256,1024]{1,0:T(8,128)(2,1)} %slice.106), channel_id=1, source_target_pairs={{0,2},{2,0},{4,6},{6,4},{8,10},{10,8},{12,14},{14,12},{16,18},{18,... | collective-permute-start | bytes 1572872 | tf_op jit(solution)/shard_map/ppermute | solution.py:34
  75.6 18.3 %collective-permute-start.21 = (bf16[64,2816]{1,0:T(8,128)(2,1)}, bf16[64,2816]{1,0:T(8,128)(2,1)}, u32[]{:S(2)}, u32[]{:S(2)}) collective-permute-start(bf16[64,2816]{1,0:T(8,128)(2,1)} %collective-permute-done.19.refs_1_), channel_id=1, source_target_pairs={{0,8},{2,10},{4,12},{6,14},{8,0},{10,2},{12,4},{14,6},{16,24},{18,... | collective-permute-start | bytes 1081352 | tf_op jit(solution)/shard_map/ppermute | solution.py:34
  89.3 25.1 %all-to-all-start.1 = ((bf16[16,8,1024]{2,1,0:T(8,128)(2,1)}), bf16[16,8,1024]{2,1,0:T(8,128)(2,1)}, u32[]{:S(2)}, u32[]{:S(2)}) async-start(bf16[16,8,1024]{2,1,0:T(8,128)(2,1)} %broadcast_select_fusion.1), calls=%async_computation.1 | async-start | bytes 524288 | tf_op jit(solution)/shard_map/all_to_all | solution.py:736
  93.9 16.2 %collective-permute-start.26 = (bf16[64,1408]{1,0:T(8,128)(2,1)}, bf16[64,1408]{1,0:T(8,128)(2,1)S(1)}, u32[]{:S(2)}, u32[]{:S(2)}) collective-permute-start(bf16[64,1408]{1,0:T(8,128)(2,1)} %copy-done.37), channel_id=1, source_target_pairs={{0,4},{2,6},{4,0},{6,2},{8,12},{10,14},{12,8},{14,10},{16,20},{18,... | collective-permute-start | bytes 540680 | tf_op jit(solution)/shard_map/ppermute | solution.py:34
  108.0 51.1 %collective-permute-start.23 = (bf16[512,1408]{1,0:T(8,128)(2,1)}, bf16[512,1408]{1,0:T(8,128)(2,1)}, u32[]{:S(2)}, u32[]{:S(2)}) collective-permute-start(bf16[512,1408]{1,0:T(8,128)(2,1)} %stack_body.6.refs_0_), channel_id=1, source_target_pairs={{0,4},{2,6},{4,0},{6,2},{8,12},{10,14},{12,8},{14,10},{16,20},{18,... | collective-permute-start | bytes 4325384 | tf_op jit(solution)/shard_map/ppermute | solution.py:34
  108.3 54.0 %collective-permute-start.22 = (bf16[512,1408]{1,0:T(8,128)(2,1)}, bf16[512,1408]{1,0:T(8,128)(2,1)}, u32[]{:S(2)}, u32[]{:S(2)}) collective-permute-start(bf16[512,1408]{1,0:T(8,128)(2,1)} %stack_body.6.refs_0_), channel_id=1, source_target_pairs={{0,2},{2,0},{4,6},{6,4},{8,10},{10,8},{12,14},{14,12},{16,18},{18,... | collective-permute-start | bytes 4325384 | tf_op jit(solution)/shard_map/ppermute | solution.py:34
  111.1 14.2 %collective-permute-start.27 = (bf16[256,1408]{1,0:T(8,128)(2,1)}, bf16[256,1408]{1,0:T(8,128)(2,1)}, u32[]{:S(2)}, u32[]{:S(2)}) collective-permute-start(bf16[256,1408]{1,0:T(8,128)(2,1)} %stack_body.7.refs_5_), channel_id=1, source_target_pairs={{0,24},{2,26},{4,28},{6,30},{8,16},{10,18},{12,20},{14,22},{16,8},... | collective-permute-start | bytes 2162696 | tf_op jit(solution)/shard_map/ppermute | solution.py:34
  115.6 32.2 %collective-permute-start.17 = (bf16[256,1024]{1,0:T(8,128)(2,1)S(1)}, bf16[256,1024]{1,0:T(8,128)(2,1)S(1)}, u32[]{:S(2)}, u32[]{:S(2)}) collective-permute-start(bf16[256,1024]{1,0:T(8,128)(2,1)S(1)} %slice.108), channel_id=1, source_target_pairs={{0,2},{2,0},{4,6},{6,4},{8,10},{10,8},{12,14},{14,12},{16,18},{18,... | collective-permute-start | bytes 1572872 | tf_op jit(solution)/shard_map/ppermute | solution.py:34
  117.3 32.0 %collective-permute-start.16 = (bf16[256,1024]{1,0:T(8,128)(2,1)S(1)}, bf16[256,1024]{1,0:T(8,128)(2,1)S(1)}, u32[]{:S(2)}, u32[]{:S(2)}) collective-permute-start(bf16[256,1024]{1,0:T(8,128)(2,1)S(1)} %slice.107), channel_id=1, source_target_pairs={{0,4},{2,6},{4,0},{6,2},{8,12},{10,14},{12,8},{14,10},{16,20},{18,... | collective-permute-start | bytes 1572872 | tf_op jit(solution)/shard_map/ppermute | solution.py:34
  125.3 27.4 %collective-permute-start.9 = (bf16[256,1024]{1,0:T(8,128)(2,1)S(1)}, bf16[256,1024]{1,0:T(8,128)(2,1)S(1)}, u32[]{:S(2)}, u32[]{:S(2)}) collective-permute-start(bf16[256,1024]{1,0:T(8,128)(2,1)S(1)} %copy-done.27), channel_id=1, source_target_pairs={{0,1},{1,0},{2,3},{3,2},{4,5},{5,4},{6,7},{7,6},{8,9},{9,8},{10,11... | collective-permute-start | bytes 1572872 | tf_op jit(solution)/shard_map/ppermute | solution.py:38
  147.7 19.3 %collective-permute-start.28 = (bf16[256,1408]{1,0:T(8,128)(2,1)}, bf16[256,1408]{1,0:T(8,128)(2,1)S(1)}, u32[]{:S(2)}, u32[]{:S(2)}) collective-permute-start(bf16[256,1408]{1,0:T(8,128)(2,1)} %stack_body.7.refs_5_), channel_id=1, source_target_pairs={{0,8},{2,10},{4,12},{6,14},{8,0},{10,2},{12,4},{14,6},{16,24},{18,... | collective-permute-start | bytes 2162696 | tf_op jit(solution)/shard_map/ppermute | solution.py:34
  149.3 25.8 %collective-permute-start.29 = (bf16[256,1408]{1,0:T(8,128)(2,1)}, bf16[256,1408]{1,0:T(8,128)(2,1)S(1)}, u32[]{:S(2)}, u32[]{:S(2)}) collective-permute-start(bf16[256,1408]{1,0:T(8,128)(2,1)} %collective-permute-done.27.refs_6_), channel_id=1, source_target_pairs={{0,8},{2,10},{4,12},{6,14},{8,0},{10,2},{12,4},{14,6},{16,24},{18,... | collective-permute-start | bytes 2162696 | tf_op jit(solution)/shard_map/ppermute | solution.py:34
  160.7 14.4 %collective-permute-start.25 = (bf16[256,1408]{1,0:T(8,128)(2,1)S(1)}, bf16[256,1408]{1,0:T(8,128)(2,1)S(1)}, u32[]{:S(2)}, u32[]{:S(2)}) collective-permute-start(bf16[256,1408]{1,0:T(8,128)(2,1)S(1)} %slice.110), channel_id=1, source_target_pairs={{0,2},{2,0},{4,6},{6,4},{8,10},{10,8},{12,14},{14,12},{16,18},{18,... | collective-permute-start | bytes 2162696 | tf_op jit(solution)/shard_map/ppermute | solution.py:34
  193.3 19.9 %collective-permute-start.34 = (bf16[256,1408]{1,0:T(8,128)(2,1)S(1)}, bf16[256,1408]{1,0:T(8,128)(2,1)S(1)}, u32[]{:S(2)}, u32[]{:S(2)}) collective-permute-start(bf16[256,1408]{1,0:T(8,128)(2,1)S(1)} %get-tuple-element.158), channel_id=1, source_target_pairs={{0,2},{2,0},{4,6},{6,4},{8,10},{10,8},{12,14},{14,12},{16,18},{18,... | collective-permute-start | bytes 2162696 | tf_op jit(solution)/shard_map/ppermute | solution.py:34
  194.5 18.7 %collective-permute-start.33 = (bf16[256,1408]{1,0:T(8,128)(2,1)S(1)}, bf16[256,1408]{1,0:T(8,128)(2,1)S(1)}, u32[]{:S(2)}, u32[]{:S(2)}) collective-permute-start(bf16[256,1408]{1,0:T(8,128)(2,1)S(1)} %get-tuple-element.157), channel_id=1, source_target_pairs={{0,4},{2,6},{4,0},{6,2},{8,12},{10,14},{12,8},{14,10},{16,20},{18,... | collective-permute-start | bytes 2162696 | tf_op jit(solution)/shard_map/ppermute | solution.py:34
  196.0 23.5 %collective-permute-start.45 = (bf16[256,1408]{1,0:T(8,128)(2,1)}, bf16[256,1408]{1,0:T(8,128)(2,1)}, u32[]{:S(2)}, u32[]{:S(2)}) collective-permute-start(bf16[256,1408]{1,0:T(8,128)(2,1)} %get-tuple-element.191), channel_id=1, source_target_pairs={{0,8},{2,10},{4,12},{6,14},{8,0},{10,2},{12,4},{14,6},{16,24},{18,... | collective-permute-start | bytes 2162696 | tf_op jit(solution)/shard_map/ppermute | solution.py:34
  218.1 34.8 %collective-permute-start.41 = (bf16[512,1408]{1,0:T(8,128)(2,1)}, bf16[512,1408]{1,0:T(8,128)(2,1)S(1)}, u32[]{:S(2)}, u32[]{:S(2)}) collective-permute-start(bf16[512,1408]{1,0:T(8,128)(2,1)} %get-tuple-element.182), channel_id=1, source_target_pairs={{0,2},{2,0},{4,6},{6,4},{8,10},{10,8},{12,14},{14,12},{16,18},{18,... | collective-permute-start | bytes 4325384 | tf_op jit(solution)/shard_map/ppermute | solution.py:34
  218.7 34.7 %collective-permute-start.42 = (bf16[512,1408]{1,0:T(8,128)(2,1)}, bf16[512,1408]{1,0:T(8,128)(2,1)S(1)}, u32[]{:S(2)}, u32[]{:S(2)}) collective-permute-start(bf16[512,1408]{1,0:T(8,128)(2,1)} %get-tuple-element.183), channel_id=1, source_target_pairs={{0,4},{2,6},{4,0},{6,2},{8,12},{10,14},{12,8},{14,10},{16,20},{18,... | collective-permute-start | bytes 4325384 | tf_op jit(solution)/shard_map/ppermute | solution.py:34
  220.8 33.7 %collective-permute-start.52 = (bf16[256,1408]{1,0:T(8,128)(2,1)S(1)}, bf16[256,1408]{1,0:T(8,128)(2,1)S(1)}, u32[]{:S(2)}, u32[]{:S(2)}) collective-permute-start(bf16[256,1408]{1,0:T(8,128)(2,1)S(1)} %add_convert_fusion), channel_id=1, source_target_pairs={{0,24},{2,26},{4,28},{6,30},{8,16},{10,18},{12,20},{14,22},{16,8},... | collective-permute-start | bytes 2162696 | tf_op jit(solution)/shard_map/ppermute | solution.py:34
  224.2 39.4 %collective-permute-start.47 = (bf16[256,1024]{1,0:T(8,128)(2,1)}, bf16[256,1024]{1,0:T(8,128)(2,1)}, u32[]{:S(2)}, u32[]{:S(2)}) collective-permute-start(bf16[256,1024]{1,0:T(8,128)(2,1)} %get-tuple-element.194), channel_id=1, source_target_pairs={{0,2},{2,0},{4,6},{6,4},{8,10},{10,8},{12,14},{14,12},{16,18},{18,... | collective-permute-start | bytes 1572872 | tf_op jit(solution)/shard_map/ppermute | solution.py:34
  225.2 38.4 %collective-permute-start.46 = (bf16[256,1024]{1,0:T(8,128)(2,1)}, bf16[256,1024]{1,0:T(8,128)(2,1)}, u32[]{:S(2)}, u32[]{:S(2)}) collective-permute-start(bf16[256,1024]{1,0:T(8,128)(2,1)} %get-tuple-element.192), channel_id=1, source_target_pairs={{0,4},{2,6},{4,0},{6,2},{8,12},{10,14},{12,8},{14,10},{16,20},{18,... | collective-permute-start | bytes 1572872 | tf_op jit(solution)/shard_map/ppermute | solution.py:34
  252.8 13.5 %collective-permute-start.35 = (bf16[256,1024]{1,0:T(8,128)(2,1)S(1)}, bf16[256,1024]{1,0:T(8,128)(2,1)}, u32[]{:S(2)}, u32[]{:S(2)}) collective-permute-start(bf16[256,1024]{1,0:T(8,128)(2,1)S(1)} %get-tuple-element.164.mine_ref), channel_id=1, source_target_pairs={{0,1},{1,0},{2,3},{3,2},{4,5},{5,4},{6,7},{7,6},{8,9},{9,8},{10,11... | collective-permute-start | bytes 1572872 | tf_op jit(solution)/shard_map/ppermute | solution.py:38
  255.6 21.5 %collective-permute-start.54 = (bf16[64,2816]{1,0:T(8,128)(2,1)}, bf16[64,2816]{1,0:T(8,128)(2,1)}, u32[]{:S(2)}, u32[]{:S(2)}) collective-permute-start(bf16[64,2816]{1,0:T(8,128)(2,1)} %get-tuple-element.214), channel_id=1, source_target_pairs={{0,8},{2,10},{4,12},{6,14},{8,0},{10,2},{12,4},{14,6},{16,24},{18,... | collective-permute-start | bytes 1081352 | tf_op jit(solution)/shard_map/ppermute | solution.py:34
  256.4 25.1 %collective-permute-start.30 = (bf16[256,1024]{1,0:T(8,128)(2,1)}, bf16[256,1024]{1,0:T(8,128)(2,1)}, u32[]{:S(2)}, u32[]{:S(2)}) collective-permute-start(bf16[256,1024]{1,0:T(8,128)(2,1)} %get-tuple-element.149.mine_ref), channel_id=1, source_target_pairs={{0,1},{1,0},{2,3},{3,2},{4,5},{5,4},{6,7},{7,6},{8,9},{9,8},{10,11... | collective-permute-start | bytes 1572872 | tf_op jit(solution)/shard_map/ppermute | solution.py:38
  258.2 27.3 %all-to-all-start.2 = ((bf16[16,8,1024]{2,1,0:T(8,128)(2,1)}), bf16[16,8,1024]{2,1,0:T(8,128)(2,1)}, u32[]{:S(2)}, u32[]{:S(2)}) async-start(bf16[16,8,1024]{2,1,0:T(8,128)(2,1)} %bitcast.7), calls=%async_computation.2 | async-start | bytes 524288 | tf_op jit(solution)/shard_map/all_to_all | solution.py:733
  272.2 28.8 %collective-permute-start.53 = (bf16[64,2816]{1,0:T(8,128)(2,1)}, bf16[64,2816]{1,0:T(8,128)(2,1)}, u32[]{:S(2)}, u32[]{:S(2)}) collective-permute-start(bf16[64,2816]{1,0:T(8,128)(2,1)} %copy-done.49), channel_id=1, source_target_pairs={{0,8},{2,10},{4,12},{6,14},{8,0},{10,2},{12,4},{14,6},{16,24},{18,... | collective-permute-start | bytes 1081352 | tf_op jit(solution)/shard_map/ppermute | solution.py:34
  274.2 29.0 %collective-permute-start.49 = (bf16[512,1024]{1,0:T(8,128)(2,1)}, bf16[512,1024]{1,0:T(8,128)(2,1)}, u32[]{:S(2)}, u32[]{:S(2)}) collective-permute-start(bf16[512,1024]{1,0:T(8,128)(2,1)} %get-tuple-element.198), channel_id=1, source_target_pairs={{0,4},{2,6},{4,0},{6,2},{8,12},{10,14},{12,8},{14,10},{16,20},{18,... | collective-permute-start | bytes 3145736 | tf_op jit(solution)/shard_map/ppermute | solution.py:34
  275.6 31.2 %collective-permute-start.48 = (bf16[512,1024]{1,0:T(8,128)(2,1)}, bf16[512,1024]{1,0:T(8,128)(2,1)}, u32[]{:S(2)}, u32[]{:S(2)}) collective-permute-start(bf16[512,1024]{1,0:T(8,128)(2,1)} %get-tuple-element.196), channel_id=1, source_target_pairs={{0,2},{2,0},{4,6},{6,4},{8,10},{10,8},{12,14},{14,12},{16,18},{18,... | collective-permute-start | bytes 3145736 | tf_op jit(solution)/shard_map/ppermute | solution.py:34
  279.1 22.4 %collective-permute-start.55 = (bf16[64,2816]{1,0:T(8,128)(2,1)}, bf16[64,2816]{1,0:T(8,128)(2,1)}, u32[]{:S(2)}, u32[]{:S(2)}) collective-permute-start(bf16[64,2816]{1,0:T(8,128)(2,1)} %add_convert_fusion.1), channel_id=1, source_target_pairs={{0,24},{2,26},{4,28},{6,30},{8,16},{10,18},{12,20},{14,22},{16,8},... | collective-permute-start | bytes 1081352 | tf_op jit(solution)/shard_map/ppermute | solution.py:34
  281.5 19.0 %collective-permute-start.37 = (f32[26,128]{1,0:T(8,128)S(1)}, f32[26,128]{1,0:T(8,128)S(1)}, u32[]{:S(2)}, u32[]{:S(2)}) collective-permute-start(f32[26,128]{1,0:T(8,128)S(1)} %maximum_bitcast_fusion), channel_id=1, source_target_pairs={{0,2},{2,0},{4,6},{6,4},{8,10},{10,8},{12,14},{14,12},{16,18},{18,... | collective-permute-start | bytes 39944 | tf_op jit(solution)/shard_map/ppermute | solution.py:34
  300.4 20.0 %collective-permute-start.62 = (bf16[256,1408]{1,0:T(8,128)(2,1)}, bf16[256,1408]{1,0:T(8,128)(2,1)S(1)}, u32[]{:S(2)}, u32[]{:S(2)}) collective-permute-start(bf16[256,1408]{1,0:T(8,128)(2,1)} %copy-done.42), channel_id=1, source_target_pairs={{0,8},{2,10},{4,12},{6,14},{8,0},{10,2},{12,4},{14,6},{16,24},{18,... | collective-permute-start | bytes 2162696 | tf_op jit(solution)/shard_map/ppermute | solution.py:34
  301.5 26.2 %collective-permute-start.44 = (bf16[256,1024]{1,0:T(8,128)(2,1)}, bf16[256,1024]{1,0:T(8,128)(2,1)}, u32[]{:S(2)}, u32[]{:S(2)}) collective-permute-start(bf16[256,1024]{1,0:T(8,128)(2,1)} %copy-done.46), channel_id=1, source_target_pairs={{0,2},{2,0},{4,6},{6,4},{8,10},{10,8},{12,14},{14,12},{16,18},{18,... | collective-permute-start | bytes 1572872 | tf_op jit(solution)/shard_map/ppermute | solution.py:34
  303.1 24.6 %collective-permute-start.43 = (bf16[256,1024]{1,0:T(8,128)(2,1)}, bf16[256,1024]{1,0:T(8,128)(2,1)}, u32[]{:S(2)}, u32[]{:S(2)}) collective-permute-start(bf16[256,1024]{1,0:T(8,128)(2,1)} %copy-done.45), channel_id=1, source_target_pairs={{0,4},{2,6},{4,0},{6,2},{8,12},{10,14},{12,8},{14,10},{16,20},{18,... | collective-permute-start | bytes 1572872 | tf_op jit(solution)/shard_map/ppermute | solution.py:34
  311.1 21.2 %collective-permute-start.57 = (bf16[64,2048]{1,0:T(8,128)(2,1)}, bf16[64,2048]{1,0:T(8,128)(2,1)S(1)}, u32[]{:S(2)}, u32[]{:S(2)}) collective-permute-start(bf16[64,2048]{1,0:T(8,128)(2,1)} %get-tuple-element.218), channel_id=1, source_target_pairs={{0,8},{2,10},{4,12},{6,14},{8,0},{10,2},{12,4},{14,6},{16,24},{18,... | collective-permute-start | bytes 786440 | tf_op jit(solution)/shard_map/ppermute | solution.py:34
  312.5 13.5 %collective-permute-start.39 = (f32[26,128]{1,0:T(8,128)S(1)}, f32[26,128]{1,0:T(8,128)S(1)}, u32[]{:S(2)}, u32[]{:S(2)}) collective-permute-start(f32[26,128]{1,0:T(8,128)S(1)} %fusion.8), channel_id=1, source_target_pairs={{0,8},{2,10},{4,12},{6,14},{8,0},{10,2},{12,4},{14,6},{16,24},{18,... | collective-permute-start | bytes 39944 | tf_op jit(solution)/shard_map/ppermute | solution.py:34
  314.0 26.5 %all-to-all-start.3 = ((bf16[16,8,1024]{2,1,0:T(8,128)(2,1)}), bf16[16,8,1024]{2,1,0:T(8,128)(2,1)}, u32[]{:S(2)}, u32[]{:S(2)}) async-start(bf16[16,8,1024]{2,1,0:T(8,128)(2,1)} %broadcast_select_fusion), calls=%async_computation.3 | async-start | bytes 524288 | tf_op jit(solution)/shard_map/all_to_all | solution.py:736
  331.7 22.0 %collective-permute-start.51 = (bf16[512,1024]{1,0:T(8,128)(2,1)}, bf16[512,1024]{1,0:T(8,128)(2,1)S(1)}, u32[]{:S(2)}, u32[]{:S(2)}) collective-permute-start(bf16[512,1024]{1,0:T(8,128)(2,1)} %get-tuple-element.201), channel_id=1, source_target_pairs={{0,4},{2,6},{4,0},{6,2},{8,12},{10,14},{12,8},{14,10},{16,20},{18,... | collective-permute-start | bytes 3145736 | tf_op jit(solution)/shard_map/ppermute | solution.py:34
  332.3 21.6 %collective-permute-start.50 = (bf16[512,1024]{1,0:T(8,128)(2,1)}, bf16[512,1024]{1,0:T(8,128)(2,1)S(1)}, u32[]{:S(2)}, u32[]{:S(2)}) collective-permute-start(bf16[512,1024]{1,0:T(8,128)(2,1)} %get-tuple-element.199), channel_id=1, source_target_pairs={{0,2},{2,0},{4,6},{6,4},{8,10},{10,8},{12,14},{14,12},{16,18},{18,... | collective-permute-start | bytes 3145736 | tf_op jit(solution)/shard_map/ppermute | solution.py:34
  337.1 18.6 %collective-permute-start.63 = (bf16[64,1408]{1,0:T(8,128)(2,1)}, bf16[64,1408]{1,0:T(8,128)(2,1)S(1)}, u32[]{:S(2)}, u32[]{:S(2)}) collective-permute-start(bf16[64,1408]{1,0:T(8,128)(2,1)} %get-tuple-element.226), channel_id=1, source_target_pairs={{0,4},{2,6},{4,0},{6,2},{8,12},{10,14},{12,8},{14,10},{16,20},{18,... | collective-permute-start | bytes 540680 | tf_op jit(solution)/shard_map/ppermute | solution.py:34
  340.4 15.4 %collective-permute-start.65 = (bf16[64,1408]{1,0:T(8,128)(2,1)}, bf16[64,1408]{1,0:T(8,128)(2,1)S(1)}, u32[]{:S(2)}, u32[]{:S(2)}) collective-permute-start(bf16[64,1408]{1,0:T(8,128)(2,1)} %add_convert_fusion.4), channel_id=1, source_target_pairs={{0,2},{2,0},{4,6},{6,4},{8,10},{10,8},{12,14},{14,12},{16,18},{18,... | collective-permute-start | bytes 540680 | tf_op jit(solution)/shard_map/ppermute | solution.py:34
  (109 other events, 919.4 us)

commit v2 on v1

--- a/solution.py
+++ b/solution.py
@@ -128,7 +128,7 @@
 
 def softmax_rows(scores):
     exponent = jnp.exp(scores - jnp.max(scores, axis=-1, keepdims=True))
-    return exponent / jnp.sum(exponent, axis=-1, keepdims=True)
+    return exponent * (1.0 / jnp.sum(exponent, axis=-1, keepdims=True))
 
 
 def attention_forward(query_ref, key_ref, value_ref, out_ref, length_ref=None, bias_ref=None):
@@ -606,16 +606,16 @@
 
 def merge_quarters(x_part, y_part, left, right):
     rows, width = left.shape
-    at = [
-        pl.BlockSpec((rows, width), lambda one: (0, 0)),
-        pl.BlockSpec((rows, width), lambda one: (1, 0)),
-    ]
-    whole = pl.BlockSpec((rows, width), lambda one: (0, 0))
+    steps = 2
+    part = rows // steps
+    first = pl.BlockSpec((part, width), lambda step: (step, 0))
+    second = pl.BlockSpec((part, width), lambda step: (steps + step, 0))
+    at = [first, second]
     return pl.pallas_call(
         merge_body,
         out_shape=[low_shape(*x_part.shape), low_shape(*y_part.shape)],
-        grid=(1,),
-        in_specs=at + [whole, whole],
+        grid=(steps,),
+        in_specs=at + [first, first],
         out_specs=at,
         input_output_aliases={0: 0, 1: 1},
         name="merge_body",
@@ -953,7 +953,7 @@
     feed_terms, feed_merged = reduce_lower(
         dfeed, [after(one, dpartial) for one in feed_came], devices
     )
-    cross_came = reduce_last(dcross, devices, down_came[:1])
+    cross_came = reduce_last(dcross, devices, feed_came)
     cross_terms, cross_merged = reduce_lower(dcross, cross_came, devices, feed_terms[1:])
     (encoder_half,) = call(
         encoder_body,
@@ -980,7 +980,7 @@
             dpartial,
             swap_tensor(dpartial),
             gains,
-            after(grad_two, *feed_came),
+            after(grad_two, *feed_merged),
             normed_self,
             query_self,
             key_self,
@@ -995,7 +995,7 @@
     grad_one, dgain_cross, dpartial, diagonal = outs[:4]
     dself = outs[4:9]
     self_came = reduce_last(dself, devices, feed_terms[1:])
-    self_terms, self_merged = reduce_lower(dself, self_came, devices, cross_terms[1:])
+    self_terms, self_merged = reduce_lower(dself, self_came, devices)
     input_grad, dgains, dtable = call(
         finish_body,
         [low_shape(rows, model), full_shape(3, model), full_shape(buckets, heads)],

time: 376 us -> 375 us (level)
  transfers between devices with their start and end apart: 70 -> 70, of which waited for: 21 -> 20; matrix products, arithmetic and copies ran while one was open for 9% -> 9% of each run, Pallas kernels for 19% -> 19%
where the time goes in v2:
time: 375 us; the launch traced here: 373 us
  waiting for transfers between devices  123 us (33%)
  starting transfers between devices  97 us (26%)
  Pallas kernels  85.9 us (23%)
  local copies, waits for them, and re-layouts  49.9 us (13%)
  other arithmetic  15.6 us (4%)
    ppermute x58, waiting for transfers between devices, swap_dp(): lax.ppermute(value, 'dp', [(one, one ^ mask) for one in range(devices)])  123 us
    pallas_call x18, Pallas kernels, call(): pl.pallas_call(body, out_shape=list(out_shape), in_specs=[smem] * len(sca...  78.2 us
    ppermute x58, starting transfers between devices, swap_dp(): lax.ppermute(value, 'dp', [(one, one ^ mask) for one in range(devices)])  77.8 us
    unnamed x181, local copies, waits for them, and re-layouts  31.8 us
    all_to_all x2, starting transfers between devices, deal(): lax.all_to_all(value.reshape(devices, rows // devices, width), 'dp', spli...  9.74 us
    all_to_all x2, starting transfers between devices, deal(): lax.all_to_all(jnp.take(first, order, axis=0), 'dp', split_axis=0, concat...  9.21 us
    slice x6, local copies, waits for them, and re-layouts, gather_lower(): left, right = (x_part[:rows], y_part[rows:])  8.75 us
    pallas_call x3, Pallas kernels, merge_quarters(): pl.pallas_call(merge_body, out_shape=[low_shape(*x_part.shape), low_shape...  7.66 us
  transfers between devices with their start and end apart: 70, of which 20 were waited for; matrix products, arithmetic and copies ran while one was open for 9% of the time, Pallas kernels for 19%

profile of v2, /device:TPU:0, one launch (start us, length us, event | category | flops | bytes accessed | tf_op | source)
XLA Modules:
  0.0 373.4 jit_solution(6759296375925299370)
XLA Ops:
  4.1 5.0 %collective-permute-start = (bf16[64,2048]{1,0:T(8,128)(2,1)S(1)}, bf16[64,2048]{1,0:T(8,128)(2,1)S(1)}, u32[]{:S(2)}, u32[]{:S(2)}) collective-permute-start(bf16[64,2048]{1,0:T(8,128)(2,1)S(1)} %constant_dynamic-update-slice_fusion.refs_0_), channel_id=1, source_target_pairs={{0,24},{2,26},{4,28},{6,30},{8,16},{10,18},{12,20},{14,22},{16,8},... | collective-permute-start | bytes 786440 | tf_op jit(solution)/shard_map/ppermute | solution.py:34
  9.2 7.2 %collective-permute-done.refs_1_ = bf16[64,2048]{1,0:T(8,128)(2,1)S(1)} collective-permute-done((bf16[64,2048]{1,0:T(8,128)(2,1)S(1)}, bf16[64,2048]{1,0:T(8,128)(2,1)S(1)}, u32[]{:S(2)}, u32[]{:S(2)}) %collective-permute-start) | collective-permute-done | bytes 262176 | tf_op jit(solution)/shard_map/ppermute | solution.py:34
  16.4 4.8 %collective-permute-done.1.refs_2_ = bf16[64,2048]{1,0:T(8,128)(2,1)S(1)} collective-permute-done((bf16[64,2048]{1,0:T(8,128)(2,1)S(1)}, bf16[64,2048]{1,0:T(8,128)(2,1)S(1)}, u32[]{:S(2)}, u32[]{:S(2)}) %collective-permute-start.1) | collective-permute-done | bytes 262176 | tf_op jit(solution)/shard_map/ppermute | solution.py:34
  26.6 4.3 %all-to-all-start = ((bf16[16,8,1024]{2,1,0:T(8,128)(2,1)}), bf16[16,8,1024]{2,1,0:T(8,128)(2,1)}, u32[]{:S(2)}, u32[]{:S(2)}) async-start(bf16[16,8,1024]{2,1,0:T(8,128)(2,1)} %dynamic-slice_bitcast_fusion), calls=%async_computation | async-start | bytes 524288 | tf_op jit(solution)/shard_map/all_to_all | solution.py:733
  35.9 3.4 collective-permute-start.11
  40.1 6.7 %collective-permute-done.11.refs_1_ = bf16[64,2048]{1,0:T(8,128)(2,1)S(1)} collective-permute-done((bf16[64,2048]{1,0:T(8,128)(2,1)S(1)}, bf16[64,2048]{1,0:T(8,128)(2,1)S(1)}, u32[]{:S(2)}, u32[]{:S(2)}) %collective-permute-start.11) | collective-permute-done | bytes 262176 | tf_op jit(solution)/shard_map/ppermute | solution.py:34
  46.9 2.7 collective-permute-done.12.refs_2_
  52.5 12.4 %collective-permute-done.13.refs_3_ = bf16[64,2048]{1,0:T(8,128)(2,1)S(1)} collective-permute-done((bf16[64,2048]{1,0:T(8,128)(2,1)S(1)}, bf16[64,2048]{1,0:T(8,128)(2,1)S(1)}, u32[]{:S(2)}, u32[]{:S(2)}) %collective-permute-start.13) | collective-permute-done | bytes 262176 | tf_op jit(solution)/shard_map/ppermute | solution.py:34
  70.4 1.9 slice.106
  72.3 2.0 collective-permute-start.8
  75.7 2.0 collective-permute-start.21
  79.8 3.2 prepare_body.1
  85.4 2.2 gather_fusion
  89.4 4.5 %all-to-all-start.1 = ((bf16[16,8,1024]{2,1,0:T(8,128)(2,1)}), bf16[16,8,1024]{2,1,0:T(8,128)(2,1)}, u32[]{:S(2)}, u32[]{:S(2)}) async-start(bf16[16,8,1024]{2,1,0:T(8,128)(2,1)} %broadcast_select_fusion.1), calls=%async_computation.1 | async-start | bytes 524288 | tf_op jit(solution)/shard_map/all_to_all | solution.py:736
  96.9 2.4 stack_body.6.refs_0_
  99.3 7.9 %self_forward_body.1 = (bf16[256,512]{1,0:T(8,128)(2,1)S(1)}, bf16[256,512]{1,0:T(8,128)(2,1)S(1)}, bf16[256,512]{1,0:T(8,128)(2,1)S(1)}, bf16[256,512]{1,0:T(8,128)(2,1)S(1)}, bf16[256,1024]{1,0:T(8,128)(2,1)S(1)}) custom-call(s32[1]{0:T(128)} %bitcast.length_ref, f32[8,512]{1,0:T(8,128)S(1)} %convolution_bitcast_fusion.bias_ref, ...), custom_call_target="tpu_custom_call" | custom-call | flops 1342177280 | bytes 1024 | tf_op jit(solution)/shard_map/self_forward_body/pallas_call | solution.py:214
  111.1 3.3 collective-permute-start.27
  118.9 6.4 %collective-permute-done.27.refs_6_ = bf16[256,1408]{1,0:T(8,128)(2,1)} collective-permute-done((bf16[256,1408]{1,0:T(8,128)(2,1)}, bf16[256,1408]{1,0:T(8,128)(2,1)}, u32[]{:S(2)}, u32[]{:S(2)}) %collective-permute-start.27) | collective-permute-done | bytes 720928 | tf_op jit(solution)/shard_map/ppermute | solution.py:34
  125.3 22.4 %collective-permute-done.17.refs_4_ = bf16[256,1024]{1,0:T(8,128)(2,1)S(1)} collective-permute-done((bf16[256,1024]{1,0:T(8,128)(2,1)S(1)}, bf16[256,1024]{1,0:T(8,128)(2,1)S(1)}, u32[]{:S(2)}, u32[]{:S(2)}) %collective-permute-start.17) | collective-permute-done | bytes 524320 | tf_op jit(solution)/shard_map/ppermute | solution.py:34
  149.7 2.9 memory_body.1
  152.7 6.4 %cross_forward_body.1 = (f32[256,1024]{1,0:T(8,128)S(1)}, bf16[256,1024]{1,0:T(8,128)(2,1)S(1)}, bf16[256,512]{1,0:T(8,128)(2,1)S(1)}, bf16[256,512]{1,0:T(8,128)(2,1)S(1)}, bf16[256,1024]{1,0:T(8,128)(2,1)S(1)}) custom-call(bf16[256,1024]{1,0:T(8,128)(2,1)S(1)} %copy-done.4, bf16[256,1024]{1,0:T(8,128)(2,1)S(1)} %copy-done.27, ...), custom_call_target="tpu_custom_call" | custom-call | flops 805306368 | bytes 1024 | tf_op jit(solution)/shard_map/cross_forward_body/pallas_call | solution.py:214
  165.0 2.0 collective-permute-done.28.refs_7_
  167.0 8.0 %collective-permute-done.29.refs_8_ = bf16[256,1408]{1,0:T(8,128)(2,1)S(1)} collective-permute-done((bf16[256,1408]{1,0:T(8,128)(2,1)}, bf16[256,1408]{1,0:T(8,128)(2,1)S(1)}, u32[]{:S(2)}, u32[]{:S(2)}) %collective-permute-start.29) | collective-permute-done | bytes 720928 | tf_op jit(solution)/shard_map/ppermute | solution.py:34
  175.9 15.5 %feed_body.1 = (f32[256,1024]{1,0:T(8,128)}, bf16[256,1024]{1,0:T(8,128)(2,1)}, bf16[256,1024]{1,0:T(8,128)(2,1)S(1)}, bf16[512,1408]{1,0:T(8,128)(2,1)}, bf16[5...) custom-call(f32[256,1024]{1,0:T(8,128)} %copy-done.41, ...), custom_call_target="tpu_custom_call" | custom-call | flops 6643777536 | bytes 1024 | tf_op jit(solution)/shard_map/feed_body/pallas_call | solution.py:214
  197.4 11.9 %cross_backward_body.1 = (f32[256,1024]{1,0:T(8,128)S(1)}, f32[1,1024]{1,0:T(1,128)S(1)}, bf16[256,1024]{1,0:T(8,128)(2,1)S(1)}, bf16[128,1024]{1,0:T(8,128)(2,1...) custom-call(f32[256,1024]{1,0:T(8,128)} %get-tuple-element.146.hidde, ...), custom_call_target="tpu_custom_call" | custom-call | flops 2415919104 | bytes 1024 | tf_op jit(solution)/shard_map/cross_backward_body/pallas_call | solution.py:214
  214.8 2.7 merge_body.3
  220.3 3.3 collective-permute-start.52
  225.7 12.6 %self_backward_body.1 = (f32[256,1024]{1,0:T(8,128)S(1)}, f32[1,1024]{1,0:T(1,128)S(1)}, bf16[256,1024]{1,0:T(8,128)(2,1)S(1)}, f32[8,512]{1,0:T(8,128)S(1)}, bf...) custom-call(s32[1]{0:T(128)} %bitcast.length_ref, ...), custom_call_target="tpu_custom_call" | custom-call | flops 2684354560 | bytes 1024 | tf_op jit(solution)/shard_map/self_backward_body/pallas_call | solution.py:214
  242.8 9.5 %collective-permute-done.41.refs_1_ = bf16[512,1408]{1,0:T(8,128)(2,1)S(1)} collective-permute-done((bf16[512,1408]{1,0:T(8,128)(2,1)}, bf16[512,1408]{1,0:T(8,128)(2,1)S(1)}, u32[]{:S(2)}, u32[]{:S(2)}) %collective-permute-start.41) | collective-permute-done | bytes 1441824 | tf_op jit(solution)/shard_map/ppermute | solution.py:34
  257.7 5.4 %all-to-all-start.2 = ((bf16[16,8,1024]{2,1,0:T(8,128)(2,1)}), bf16[16,8,1024]{2,1,0:T(8,128)(2,1)}, u32[]{:S(2)}, u32[]{:S(2)}) async-start(bf16[16,8,1024]{2,1,0:T(8,128)(2,1)} %bitcast.7), calls=%async_computation.2 | async-start | bytes 524288 | tf_op jit(solution)/shard_map/all_to_all | solution.py:733
  263.2 2.5 merge_body.5
  266.9 4.5 %finish_body.1 = (bf16[256,1024]{1,0:T(8,128)(2,1)}, f32[3,1024]{1,0:T(4,128)S(1)}, f32[32,8]{1,0:T(8,128)S(1)}) custom-call(s32[1]{0:T(128)} %bitcast.length_ref, bf16[1024,1024]{1,0:T(8,128)(2,1)S(1)} %get-tuple-element.122.permute_ref, bf16[256,1024]{1,0:T(8,128)(2,1)S(1)} %copy-done.5, bf16[256,1024]{1,0:T(8,128)(2,1)S(1)} %get-tuple-element.168.mine_ref, ...), custom_call_target="tpu_custom_call" | custom-call | flops 536870912 | bytes 1024 | tf_op jit(solution)/shard_map/finish_body/pallas_call | solution.py:214
  271.5 1.9 collective-permute-start.53
  276.4 2.0 add_convert_fusion.1
  278.4 2.4 collective-permute-start.55
  281.4 3.4 output_body.1
  286.4 13.3 %collective-permute-done.37 = f32[26,128]{1,0:T(8,128)S(1)} collective-permute-done((f32[26,128]{1,0:T(8,128)S(1)}, f32[26,128]{1,0:T(8,128)S(1)}, u32[]{:S(2)}, u32[]{:S(2)}) %collective-permute-start.37) | collective-permute-done | bytes 13344 | tf_op jit(solution)/shard_map/ppermute | solution.py:34
  303.9 2.3 convert_add_fusion
  306.2 2.6 fold_body.5
  313.3 4.7 %all-to-all-start.3 = ((bf16[16,8,1024]{2,1,0:T(8,128)(2,1)}), bf16[16,8,1024]{2,1,0:T(8,128)(2,1)}, u32[]{:S(2)}, u32[]{:S(2)}) async-start(bf16[16,8,1024]{2,1,0:T(8,128)(2,1)} %broadcast_select_fusion), calls=%async_computation.3 | async-start | bytes 524288 | tf_op jit(solution)/shard_map/all_to_all | solution.py:736
  322.3 3.0 collective-permute-done.39
  327.0 2.5 merge_body.4
  336.1 2.0 collective-permute-start.63
  340.1 2.4 collective-permute-done.58
  343.7 8.2 %collective-permute-done.45.refs_1_ = bf16[512,1024]{1,0:T(8,128)(2,1)S(1)} collective-permute-done((bf16[512,1024]{1,0:T(8,128)(2,1)}, bf16[512,1024]{1,0:T(8,128)(2,1)S(1)}, u32[]{:S(2)}, u32[]{:S(2)}) %collective-permute-start.45) | collective-permute-done | bytes 1048608 | tf_op jit(solution)/shard_map/ppermute | solution.py:34
  356.7 5.7 %collective-permute-done.60 = bf16[64,2048]{1,0:T(8,128)(2,1)S(1)} collective-permute-done((bf16[64,2048]{1,0:T(8,128)(2,1)S(1)}, bf16[64,2048]{1,0:T(8,128)(2,1)S(1)}, u32[]{:S(2)}, u32[]{:S(2)}) %collective-permute-start.60) | collective-permute-done | bytes 262176 | tf_op jit(solution)/shard_map/ppermute | solution.py:34
  362.5 2.2 collective-permute-start.61
  366.4 4.4 %collective-permute-done.61 = bf16[64,2048]{1,0:T(8,128)(2,1)S(1)} collective-permute-done((bf16[64,2048]{1,0:T(8,128)(2,1)S(1)}, bf16[64,2048]{1,0:T(8,128)(2,1)S(1)}, u32[]{:S(2)}, u32[]{:S(2)}) %collective-permute-start.61) | collective-permute-done | bytes 262176 | tf_op jit(solution)/shard_map/ppermute | solution.py:34
  (348 shorter events, 116.4 us)
Async XLA Ops:
  26.6 58.8 %all-to-all-start = ((bf16[16,8,1024]{2,1,0:T(8,128)(2,1)}), bf16[16,8,1024]{2,1,0:T(8,128)(2,1)}, u32[]{:S(2)}, u32[]{:S(2)}) async-start(bf16[16,8,1024]{2,1,0:T(8,128)(2,1)} %dynamic-slice_bitcast_fusion), calls=%async_computation | async-start | bytes 524288 | tf_op jit(solution)/shard_map/all_to_all | solution.py:733
  32.4 32.6 %collective-permute-start.5 = (bf16[512,1024]{1,0:T(8,128)(2,1)S(1)}, bf16[512,1024]{1,0:T(8,128)(2,1)}, u32[]{:S(2)}, u32[]{:S(2)}) collective-permute-start(bf16[512,1024]{1,0:T(8,128)(2,1)S(1)} %stack_body.4.refs_0_), channel_id=1, source_target_pairs={{0,2},{2,0},{4,6},{6,4},{8,10},{10,8},{12,14},{14,12},{16,18},{18,... | collective-permute-start | bytes 3145736 | tf_op jit(solution)/shard_map/ppermute | solution.py:34
  34.3 30.8 %collective-permute-start.6 = (bf16[512,1024]{1,0:T(8,128)(2,1)S(1)}, bf16[512,1024]{1,0:T(8,128)(2,1)}, u32[]{:S(2)}, u32[]{:S(2)}) collective-permute-start(bf16[512,1024]{1,0:T(8,128)(2,1)S(1)} %stack_body.4.refs_0_), channel_id=1, source_target_pairs={{0,4},{2,6},{4,0},{6,2},{8,12},{10,14},{12,8},{14,10},{16,20},{18,... | collective-permute-start | bytes 3145736 | tf_op jit(solution)/shard_map/ppermute | solution.py:34
  49.6 15.4 %collective-permute-start.13 = (bf16[64,2048]{1,0:T(8,128)(2,1)S(1)}, bf16[64,2048]{1,0:T(8,128)(2,1)S(1)}, u32[]{:S(2)}, u32[]{:S(2)}) collective-permute-start(bf16[64,2048]{1,0:T(8,128)(2,1)S(1)} %collective-permute-done.11.refs_1_), channel_id=1, source_target_pairs={{0,8},{2,10},{4,12},{6,14},{8,0},{10,2},{12,4},{14,6},{16,24},{18,... | collective-permute-start | bytes 786440 | tf_op jit(solution)/shard_map/ppermute | solution.py:34
  51.4 20.9 %collective-permute-start.19 = (bf16[64,2816]{1,0:T(8,128)(2,1)S(1)}, bf16[64,2816]{1,0:T(8,128)(2,1)}, u32[]{:S(2)}, u32[]{:S(2)}) collective-permute-start(bf16[64,2816]{1,0:T(8,128)(2,1)S(1)} %pad_maximum_fusion.refs_0_), channel_id=1, source_target_pairs={{0,24},{2,26},{4,28},{6,30},{8,16},{10,18},{12,20},{14,22},{16,8},... | collective-permute-start | bytes 1081352 | tf_op jit(solution)/shard_map/ppermute | solution.py:34
  65.1 43.0 %collective-permute-start.15 = (bf16[512,1024]{1,0:T(8,128)(2,1)S(1)}, bf16[512,1024]{1,0:T(8,128)(2,1)}, u32[]{:S(2)}, u32[]{:S(2)}) collective-permute-start(bf16[512,1024]{1,0:T(8,128)(2,1)S(1)} %stack_body.5.refs_0_), channel_id=1, source_target_pairs={{0,4},{2,6},{4,0},{6,2},{8,12},{10,14},{12,8},{14,10},{16,20},{18,... | collective-permute-start | bytes 3145736 | tf_op jit(solution)/shard_map/ppermute | solution.py:34
  65.2 43.2 %collective-permute-start.14 = (bf16[512,1024]{1,0:T(8,128)(2,1)S(1)}, bf16[512,1024]{1,0:T(8,128)(2,1)}, u32[]{:S(2)}, u32[]{:S(2)}) collective-permute-start(bf16[512,1024]{1,0:T(8,128)(2,1)S(1)} %stack_body.5.refs_0_), channel_id=1, source_target_pairs={{0,2},{2,0},{4,6},{6,4},{8,10},{10,8},{12,14},{14,12},{16,18},{18,... | collective-permute-start | bytes 3145736 | tf_op jit(solution)/shard_map/ppermute | solution.py:34
  68.6 30.7 %collective-permute-start.7 = (bf16[256,1024]{1,0:T(8,128)(2,1)}, bf16[256,1024]{1,0:T(8,128)(2,1)}, u32[]{:S(2)}, u32[]{:S(2)}) collective-permute-start(bf16[256,1024]{1,0:T(8,128)(2,1)} %slice.105), channel_id=1, source_target_pairs={{0,4},{2,6},{4,0},{6,2},{8,12},{10,14},{12,8},{14,10},{16,20},{18,... | collective-permute-start | bytes 1572872 | tf_op jit(solution)/shard_map/ppermute | solution.py:34
  72.3 26.9 %collective-permute-start.8 = (bf16[256,1024]{1,0:T(8,128)(2,1)}, bf16[256,1024]{1,0:T(8,128)(2,1)}, u32[]{:S(2)}, u32[]{:S(2)}) collective-permute-start(bf16[256,1024]{1,0:T(8,128)(2,1)} %slice.106), channel_id=1, source_target_pairs={{0,2},{2,0},{4,6},{6,4},{8,10},{10,8},{12,14},{14,12},{16,18},{18,... | collective-permute-start | bytes 1572872 | tf_op jit(solution)/shard_map/ppermute | solution.py:34
  75.7 18.3 %collective-permute-start.21 = (bf16[64,2816]{1,0:T(8,128)(2,1)}, bf16[64,2816]{1,0:T(8,128)(2,1)}, u32[]{:S(2)}, u32[]{:S(2)}) collective-permute-start(bf16[64,2816]{1,0:T(8,128)(2,1)} %collective-permute-done.19.refs_1_), channel_id=1, source_target_pairs={{0,8},{2,10},{4,12},{6,14},{8,0},{10,2},{12,4},{14,6},{16,24},{18,... | collective-permute-start | bytes 1081352 | tf_op jit(solution)/shard_map/ppermute | solution.py:34
  89.4 25.0 %all-to-all-start.1 = ((bf16[16,8,1024]{2,1,0:T(8,128)(2,1)}), bf16[16,8,1024]{2,1,0:T(8,128)(2,1)}, u32[]{:S(2)}, u32[]{:S(2)}) async-start(bf16[16,8,1024]{2,1,0:T(8,128)(2,1)} %broadcast_select_fusion.1), calls=%async_computation.1 | async-start | bytes 524288 | tf_op jit(solution)/shard_map/all_to_all | solution.py:736
  93.9 16.2 %collective-permute-start.26 = (bf16[64,1408]{1,0:T(8,128)(2,1)}, bf16[64,1408]{1,0:T(8,128)(2,1)S(1)}, u32[]{:S(2)}, u32[]{:S(2)}) collective-permute-start(bf16[64,1408]{1,0:T(8,128)(2,1)} %copy-done.37), channel_id=1, source_target_pairs={{0,4},{2,6},{4,0},{6,2},{8,12},{10,14},{12,8},{14,10},{16,20},{18,... | collective-permute-start | bytes 540680 | tf_op jit(solution)/shard_map/ppermute | solution.py:34
  108.1 51.1 %collective-permute-start.23 = (bf16[512,1408]{1,0:T(8,128)(2,1)}, bf16[512,1408]{1,0:T(8,128)(2,1)}, u32[]{:S(2)}, u32[]{:S(2)}) collective-permute-start(bf16[512,1408]{1,0:T(8,128)(2,1)} %stack_body.6.refs_0_), channel_id=1, source_target_pairs={{0,4},{2,6},{4,0},{6,2},{8,12},{10,14},{12,8},{14,10},{16,20},{18,... | collective-permute-start | bytes 4325384 | tf_op jit(solution)/shard_map/ppermute | solution.py:34
  108.4 53.9 %collective-permute-start.22 = (bf16[512,1408]{1,0:T(8,128)(2,1)}, bf16[512,1408]{1,0:T(8,128)(2,1)}, u32[]{:S(2)}, u32[]{:S(2)}) collective-permute-start(bf16[512,1408]{1,0:T(8,128)(2,1)} %stack_body.6.refs_0_), channel_id=1, source_target_pairs={{0,2},{2,0},{4,6},{6,4},{8,10},{10,8},{12,14},{14,12},{16,18},{18,... | collective-permute-start | bytes 4325384 | tf_op jit(solution)/shard_map/ppermute | solution.py:34
  111.1 14.2 %collective-permute-start.27 = (bf16[256,1408]{1,0:T(8,128)(2,1)}, bf16[256,1408]{1,0:T(8,128)(2,1)}, u32[]{:S(2)}, u32[]{:S(2)}) collective-permute-start(bf16[256,1408]{1,0:T(8,128)(2,1)} %stack_body.7.refs_5_), channel_id=1, source_target_pairs={{0,24},{2,26},{4,28},{6,30},{8,16},{10,18},{12,20},{14,22},{16,8},... | collective-permute-start | bytes 2162696 | tf_op jit(solution)/shard_map/ppermute | solution.py:34
  115.6 32.1 %collective-permute-start.17 = (bf16[256,1024]{1,0:T(8,128)(2,1)S(1)}, bf16[256,1024]{1,0:T(8,128)(2,1)S(1)}, u32[]{:S(2)}, u32[]{:S(2)}) collective-permute-start(bf16[256,1024]{1,0:T(8,128)(2,1)S(1)} %slice.108), channel_id=1, source_target_pairs={{0,2},{2,0},{4,6},{6,4},{8,10},{10,8},{12,14},{14,12},{16,18},{18,... | collective-permute-start | bytes 1572872 | tf_op jit(solution)/shard_map/ppermute | solution.py:34
  117.3 31.9 %collective-permute-start.16 = (bf16[256,1024]{1,0:T(8,128)(2,1)S(1)}, bf16[256,1024]{1,0:T(8,128)(2,1)S(1)}, u32[]{:S(2)}, u32[]{:S(2)}) collective-permute-start(bf16[256,1024]{1,0:T(8,128)(2,1)S(1)} %slice.107), channel_id=1, source_target_pairs={{0,4},{2,6},{4,0},{6,2},{8,12},{10,14},{12,8},{14,10},{16,20},{18,... | collective-permute-start | bytes 1572872 | tf_op jit(solution)/shard_map/ppermute | solution.py:34
  125.3 27.4 %collective-permute-start.9 = (bf16[256,1024]{1,0:T(8,128)(2,1)S(1)}, bf16[256,1024]{1,0:T(8,128)(2,1)S(1)}, u32[]{:S(2)}, u32[]{:S(2)}) collective-permute-start(bf16[256,1024]{1,0:T(8,128)(2,1)S(1)} %copy-done.27), channel_id=1, source_target_pairs={{0,1},{1,0},{2,3},{3,2},{4,5},{5,4},{6,7},{7,6},{8,9},{9,8},{10,11... | collective-permute-start | bytes 1572872 | tf_op jit(solution)/shard_map/ppermute | solution.py:38
  147.7 19.3 %collective-permute-start.28 = (bf16[256,1408]{1,0:T(8,128)(2,1)}, bf16[256,1408]{1,0:T(8,128)(2,1)S(1)}, u32[]{:S(2)}, u32[]{:S(2)}) collective-permute-start(bf16[256,1408]{1,0:T(8,128)(2,1)} %stack_body.7.refs_5_), channel_id=1, source_target_pairs={{0,8},{2,10},{4,12},{6,14},{8,0},{10,2},{12,4},{14,6},{16,24},{18,... | collective-permute-start | bytes 2162696 | tf_op jit(solution)/shard_map/ppermute | solution.py:34
  149.2 25.8 %collective-permute-start.29 = (bf16[256,1408]{1,0:T(8,128)(2,1)}, bf16[256,1408]{1,0:T(8,128)(2,1)S(1)}, u32[]{:S(2)}, u32[]{:S(2)}) collective-permute-start(bf16[256,1408]{1,0:T(8,128)(2,1)} %collective-permute-done.27.refs_6_), channel_id=1, source_target_pairs={{0,8},{2,10},{4,12},{6,14},{8,0},{10,2},{12,4},{14,6},{16,24},{18,... | collective-permute-start | bytes 2162696 | tf_op jit(solution)/shard_map/ppermute | solution.py:34
  160.7 14.3 %collective-permute-start.25 = (bf16[256,1408]{1,0:T(8,128)(2,1)S(1)}, bf16[256,1408]{1,0:T(8,128)(2,1)S(1)}, u32[]{:S(2)}, u32[]{:S(2)}) collective-permute-start(bf16[256,1408]{1,0:T(8,128)(2,1)S(1)} %slice.110), channel_id=1, source_target_pairs={{0,2},{2,0},{4,6},{6,4},{8,10},{10,8},{12,14},{14,12},{16,18},{18,... | collective-permute-start | bytes 2162696 | tf_op jit(solution)/shard_map/ppermute | solution.py:34
  193.2 19.9 %collective-permute-start.34 = (bf16[256,1408]{1,0:T(8,128)(2,1)S(1)}, bf16[256,1408]{1,0:T(8,128)(2,1)S(1)}, u32[]{:S(2)}, u32[]{:S(2)}) collective-permute-start(bf16[256,1408]{1,0:T(8,128)(2,1)S(1)} %get-tuple-element.159), channel_id=1, source_target_pairs={{0,2},{2,0},{4,6},{6,4},{8,10},{10,8},{12,14},{14,12},{16,18},{18,... | collective-permute-start | bytes 2162696 | tf_op jit(solution)/shard_map/ppermute | solution.py:34
  194.4 18.7 %collective-permute-start.33 = (bf16[256,1408]{1,0:T(8,128)(2,1)S(1)}, bf16[256,1408]{1,0:T(8,128)(2,1)S(1)}, u32[]{:S(2)}, u32[]{:S(2)}) collective-permute-start(bf16[256,1408]{1,0:T(8,128)(2,1)S(1)} %get-tuple-element.157), channel_id=1, source_target_pairs={{0,4},{2,6},{4,0},{6,2},{8,12},{10,14},{12,8},{14,10},{16,20},{18,... | collective-permute-start | bytes 2162696 | tf_op jit(solution)/shard_map/ppermute | solution.py:34
  195.9 23.1 %collective-permute-start.51 = (bf16[256,1408]{1,0:T(8,128)(2,1)}, bf16[256,1408]{1,0:T(8,128)(2,1)}, u32[]{:S(2)}, u32[]{:S(2)}) collective-permute-start(bf16[256,1408]{1,0:T(8,128)(2,1)} %get-tuple-element.206), channel_id=1, source_target_pairs={{0,8},{2,10},{4,12},{6,14},{8,0},{10,2},{12,4},{14,6},{16,24},{18,... | collective-permute-start | bytes 2162696 | tf_op jit(solution)/shard_map/ppermute | solution.py:34
  217.6 34.8 %collective-permute-start.41 = (bf16[512,1408]{1,0:T(8,128)(2,1)}, bf16[512,1408]{1,0:T(8,128)(2,1)S(1)}, u32[]{:S(2)}, u32[]{:S(2)}) collective-permute-start(bf16[512,1408]{1,0:T(8,128)(2,1)} %get-tuple-element.161), channel_id=1, source_target_pairs={{0,2},{2,0},{4,6},{6,4},{8,10},{10,8},{12,14},{14,12},{16,18},{18,... | collective-permute-start | bytes 4325384 | tf_op jit(solution)/shard_map/ppermute | solution.py:34
  218.2 34.7 %collective-permute-start.42 = (bf16[512,1408]{1,0:T(8,128)(2,1)}, bf16[512,1408]{1,0:T(8,128)(2,1)S(1)}, u32[]{:S(2)}, u32[]{:S(2)}) collective-permute-start(bf16[512,1408]{1,0:T(8,128)(2,1)} %get-tuple-element.162), channel_id=1, source_target_pairs={{0,4},{2,6},{4,0},{6,2},{8,12},{10,14},{12,8},{14,10},{16,20},{18,... | collective-permute-start | bytes 4325384 | tf_op jit(solution)/shard_map/ppermute | solution.py:34
  220.3 33.7 %collective-permute-start.52 = (bf16[256,1408]{1,0:T(8,128)(2,1)S(1)}, bf16[256,1408]{1,0:T(8,128)(2,1)S(1)}, u32[]{:S(2)}, u32[]{:S(2)}) collective-permute-start(bf16[256,1408]{1,0:T(8,128)(2,1)S(1)} %add_convert_fusion), channel_id=1, source_target_pairs={{0,24},{2,26},{4,28},{6,30},{8,16},{10,18},{12,20},{14,22},{16,8},... | collective-permute-start | bytes 2162696 | tf_op jit(solution)/shard_map/ppermute | solution.py:34
  223.7 39.4 %collective-permute-start.48 = (bf16[256,1024]{1,0:T(8,128)(2,1)}, bf16[256,1024]{1,0:T(8,128)(2,1)}, u32[]{:S(2)}, u32[]{:S(2)}) collective-permute-start(bf16[256,1024]{1,0:T(8,128)(2,1)} %get-tuple-element.195), channel_id=1, source_target_pairs={{0,2},{2,0},{4,6},{6,4},{8,10},{10,8},{12,14},{14,12},{16,18},{18,... | collective-permute-start | bytes 1572872 | tf_op jit(solution)/shard_map/ppermute | solution.py:34
  224.7 38.4 %collective-permute-start.47 = (bf16[256,1024]{1,0:T(8,128)(2,1)}, bf16[256,1024]{1,0:T(8,128)(2,1)}, u32[]{:S(2)}, u32[]{:S(2)}) collective-permute-start(bf16[256,1024]{1,0:T(8,128)(2,1)} %get-tuple-element.193), channel_id=1, source_target_pairs={{0,4},{2,6},{4,0},{6,2},{8,12},{10,14},{12,8},{14,10},{16,20},{18,... | collective-permute-start | bytes 1572872 | tf_op jit(solution)/shard_map/ppermute | solution.py:34
  252.4 13.2 %collective-permute-start.35 = (bf16[256,1024]{1,0:T(8,128)(2,1)S(1)}, bf16[256,1024]{1,0:T(8,128)(2,1)}, u32[]{:S(2)}, u32[]{:S(2)}) collective-permute-start(bf16[256,1024]{1,0:T(8,128)(2,1)S(1)} %get-tuple-element.168.mine_ref), channel_id=1, source_target_pairs={{0,1},{1,0},{2,3},{3,2},{4,5},{5,4},{6,7},{7,6},{8,9},{9,8},{10,11... | collective-permute-start | bytes 1572872 | tf_op jit(solution)/shard_map/ppermute | solution.py:38
  255.1 21.3 %collective-permute-start.54 = (bf16[64,2816]{1,0:T(8,128)(2,1)}, bf16[64,2816]{1,0:T(8,128)(2,1)}, u32[]{:S(2)}, u32[]{:S(2)}) collective-permute-start(bf16[64,2816]{1,0:T(8,128)(2,1)} %get-tuple-element.210), channel_id=1, source_target_pairs={{0,8},{2,10},{4,12},{6,14},{8,0},{10,2},{12,4},{14,6},{16,24},{18,... | collective-permute-start | bytes 1081352 | tf_op jit(solution)/shard_map/ppermute | solution.py:34
  255.9 24.8 %collective-permute-start.30 = (bf16[256,1024]{1,0:T(8,128)(2,1)}, bf16[256,1024]{1,0:T(8,128)(2,1)}, u32[]{:S(2)}, u32[]{:S(2)}) collective-permute-start(bf16[256,1024]{1,0:T(8,128)(2,1)} %get-tuple-element.147.mine_ref), channel_id=1, source_target_pairs={{0,1},{1,0},{2,3},{3,2},{4,5},{5,4},{6,7},{7,6},{8,9},{9,8},{10,11... | collective-permute-start | bytes 1572872 | tf_op jit(solution)/shard_map/ppermute | solution.py:38
  257.7 27.1 %all-to-all-start.2 = ((bf16[16,8,1024]{2,1,0:T(8,128)(2,1)}), bf16[16,8,1024]{2,1,0:T(8,128)(2,1)}, u32[]{:S(2)}, u32[]{:S(2)}) async-start(bf16[16,8,1024]{2,1,0:T(8,128)(2,1)} %bitcast.7), calls=%async_computation.2 | async-start | bytes 524288 | tf_op jit(solution)/shard_map/all_to_all | solution.py:733
  271.5 28.8 %collective-permute-start.53 = (bf16[64,2816]{1,0:T(8,128)(2,1)}, bf16[64,2816]{1,0:T(8,128)(2,1)}, u32[]{:S(2)}, u32[]{:S(2)}) collective-permute-start(bf16[64,2816]{1,0:T(8,128)(2,1)} %copy-done.49), channel_id=1, source_target_pairs={{0,8},{2,10},{4,12},{6,14},{8,0},{10,2},{12,4},{14,6},{16,24},{18,... | collective-permute-start | bytes 1081352 | tf_op jit(solution)/shard_map/ppermute | solution.py:34
  273.5 29.0 %collective-permute-start.50 = (bf16[512,1024]{1,0:T(8,128)(2,1)}, bf16[512,1024]{1,0:T(8,128)(2,1)}, u32[]{:S(2)}, u32[]{:S(2)}) collective-permute-start(bf16[512,1024]{1,0:T(8,128)(2,1)} %get-tuple-element.199), channel_id=1, source_target_pairs={{0,4},{2,6},{4,0},{6,2},{8,12},{10,14},{12,8},{14,10},{16,20},{18,... | collective-permute-start | bytes 3145736 | tf_op jit(solution)/shard_map/ppermute | solution.py:34
  274.9 31.3 %collective-permute-start.49 = (bf16[512,1024]{1,0:T(8,128)(2,1)}, bf16[512,1024]{1,0:T(8,128)(2,1)}, u32[]{:S(2)}, u32[]{:S(2)}) collective-permute-start(bf16[512,1024]{1,0:T(8,128)(2,1)} %get-tuple-element.197), channel_id=1, source_target_pairs={{0,2},{2,0},{4,6},{6,4},{8,10},{10,8},{12,14},{14,12},{16,18},{18,... | collective-permute-start | bytes 3145736 | tf_op jit(solution)/shard_map/ppermute | solution.py:34
  278.4 22.4 %collective-permute-start.55 = (bf16[64,2816]{1,0:T(8,128)(2,1)}, bf16[64,2816]{1,0:T(8,128)(2,1)}, u32[]{:S(2)}, u32[]{:S(2)}) collective-permute-start(bf16[64,2816]{1,0:T(8,128)(2,1)} %add_convert_fusion.1), channel_id=1, source_target_pairs={{0,24},{2,26},{4,28},{6,30},{8,16},{10,18},{12,20},{14,22},{16,8},... | collective-permute-start | bytes 1081352 | tf_op jit(solution)/shard_map/ppermute | solution.py:34
  280.8 19.0 %collective-permute-start.37 = (f32[26,128]{1,0:T(8,128)S(1)}, f32[26,128]{1,0:T(8,128)S(1)}, u32[]{:S(2)}, u32[]{:S(2)}) collective-permute-start(f32[26,128]{1,0:T(8,128)S(1)} %maximum_bitcast_fusion), channel_id=1, source_target_pairs={{0,2},{2,0},{4,6},{6,4},{8,10},{10,8},{12,14},{14,12},{16,18},{18,... | collective-permute-start | bytes 39944 | tf_op jit(solution)/shard_map/ppermute | solution.py:34
  299.7 20.0 %collective-permute-start.62 = (bf16[256,1408]{1,0:T(8,128)(2,1)}, bf16[256,1408]{1,0:T(8,128)(2,1)S(1)}, u32[]{:S(2)}, u32[]{:S(2)}) collective-permute-start(bf16[256,1408]{1,0:T(8,128)(2,1)} %copy-done.42), channel_id=1, source_target_pairs={{0,8},{2,10},{4,12},{6,14},{8,0},{10,2},{12,4},{14,6},{16,24},{18,... | collective-permute-start | bytes 2162696 | tf_op jit(solution)/shard_map/ppermute | solution.py:34
  300.8 26.2 %collective-permute-start.44 = (bf16[256,1024]{1,0:T(8,128)(2,1)}, bf16[256,1024]{1,0:T(8,128)(2,1)}, u32[]{:S(2)}, u32[]{:S(2)}) collective-permute-start(bf16[256,1024]{1,0:T(8,128)(2,1)} %copy-done.46), channel_id=1, source_target_pairs={{0,2},{2,0},{4,6},{6,4},{8,10},{10,8},{12,14},{14,12},{16,18},{18,... | collective-permute-start | bytes 1572872 | tf_op jit(solution)/shard_map/ppermute | solution.py:34
  302.4 24.6 %collective-permute-start.43 = (bf16[256,1024]{1,0:T(8,128)(2,1)}, bf16[256,1024]{1,0:T(8,128)(2,1)}, u32[]{:S(2)}, u32[]{:S(2)}) collective-permute-start(bf16[256,1024]{1,0:T(8,128)(2,1)} %copy-done.45), channel_id=1, source_target_pairs={{0,4},{2,6},{4,0},{6,2},{8,12},{10,14},{12,8},{14,10},{16,20},{18,... | collective-permute-start | bytes 1572872 | tf_op jit(solution)/shard_map/ppermute | solution.py:34
  310.4 21.1 %collective-permute-start.57 = (bf16[64,2048]{1,0:T(8,128)(2,1)}, bf16[64,2048]{1,0:T(8,128)(2,1)S(1)}, u32[]{:S(2)}, u32[]{:S(2)}) collective-permute-start(bf16[64,2048]{1,0:T(8,128)(2,1)} %get-tuple-element.214), channel_id=1, source_target_pairs={{0,8},{2,10},{4,12},{6,14},{8,0},{10,2},{12,4},{14,6},{16,24},{18,... | collective-permute-start | bytes 786440 | tf_op jit(solution)/shard_map/ppermute | solution.py:34
  311.9 13.4 %collective-permute-start.39 = (f32[26,128]{1,0:T(8,128)S(1)}, f32[26,128]{1,0:T(8,128)S(1)}, u32[]{:S(2)}, u32[]{:S(2)}) collective-permute-start(f32[26,128]{1,0:T(8,128)S(1)} %fusion.8), channel_id=1, source_target_pairs={{0,8},{2,10},{4,12},{6,14},{8,0},{10,2},{12,4},{14,6},{16,24},{18,... | collective-permute-start | bytes 39944 | tf_op jit(solution)/shard_map/ppermute | solution.py:34
  313.3 26.2 %all-to-all-start.3 = ((bf16[16,8,1024]{2,1,0:T(8,128)(2,1)}), bf16[16,8,1024]{2,1,0:T(8,128)(2,1)}, u32[]{:S(2)}, u32[]{:S(2)}) async-start(bf16[16,8,1024]{2,1,0:T(8,128)(2,1)} %broadcast_select_fusion), calls=%async_computation.3 | async-start | bytes 524288 | tf_op jit(solution)/shard_map/all_to_all | solution.py:736
  329.5 22.4 %collective-permute-start.45 = (bf16[512,1024]{1,0:T(8,128)(2,1)}, bf16[512,1024]{1,0:T(8,128)(2,1)S(1)}, u32[]{:S(2)}, u32[]{:S(2)}) collective-permute-start(bf16[512,1024]{1,0:T(8,128)(2,1)} %get-tuple-element.185), channel_id=1, source_target_pairs={{0,2},{2,0},{4,6},{6,4},{8,10},{10,8},{12,14},{14,12},{16,18},{18,... | collective-permute-start | bytes 3145736 | tf_op jit(solution)/shard_map/ppermute | solution.py:34
  330.9 22.1 %collective-permute-start.46 = (bf16[512,1024]{1,0:T(8,128)(2,1)}, bf16[512,1024]{1,0:T(8,128)(2,1)S(1)}, u32[]{:S(2)}, u32[]{:S(2)}) collective-permute-start(bf16[512,1024]{1,0:T(8,128)(2,1)} %get-tuple-element.186), channel_id=1, source_target_pairs={{0,4},{2,6},{4,0},{6,2},{8,12},{10,14},{12,8},{14,10},{16,20},{18,... | collective-permute-start | bytes 3145736 | tf_op jit(solution)/shard_map/ppermute | solution.py:34
  336.1 18.9 %collective-permute-start.63 = (bf16[64,1408]{1,0:T(8,128)(2,1)}, bf16[64,1408]{1,0:T(8,128)(2,1)S(1)}, u32[]{:S(2)}, u32[]{:S(2)}) collective-permute-start(bf16[64,1408]{1,0:T(8,128)(2,1)} %get-tuple-element.222), channel_id=1, source_target_pairs={{0,4},{2,6},{4,0},{6,2},{8,12},{10,14},{12,8},{14,10},{16,20},{18,... | collective-permute-start | bytes 540680 | tf_op jit(solution)/shard_map/ppermute | solution.py:34
  339.5 15.5 %collective-permute-start.65 = (bf16[64,1408]{1,0:T(8,128)(2,1)}, bf16[64,1408]{1,0:T(8,128)(2,1)S(1)}, u32[]{:S(2)}, u32[]{:S(2)}) collective-permute-start(bf16[64,1408]{1,0:T(8,128)(2,1)} %add_convert_fusion.4), channel_id=1, source_target_pairs={{0,2},{2,0},{4,6},{6,4},{8,10},{10,8},{12,14},{14,12},{16,18},{18,... | collective-permute-start | bytes 540680 | tf_op jit(solution)/shard_map/ppermute | solution.py:34
  (109 other events, 917.4 us)

commit v3 on v2

--- a/solution.py
+++ b/solution.py
@@ -307,7 +307,7 @@
 
 GELU_SCALE = float(np.sqrt(2.0 / np.pi))
 GELU_CUBE = 0.044715
-CHUNK = 256
+CHUNK = 512
 
 
 def feed_body(transposed, hidden_in_ref, mine_ref, other_ref, gains_ref, grad_ref, *refs):

time: 375 us -> 374 us (level)
  no operation moved by 1% of the time
where the time goes in v3:
time: 374 us; the launch traced here: 372 us
  waiting for transfers between devices  123 us (33%)
  starting transfers between devices  97 us (26%)
  Pallas kernels  85.1 us (23%)
  local copies, waits for them, and re-layouts  49.9 us (13%)
  other arithmetic  15.6 us (4%)
    ppermute x58, waiting for transfers between devices, swap_dp(): lax.ppermute(value, 'dp', [(one, one ^ mask) for one in range(devices)])  123 us
    ppermute x58, starting transfers between devices, swap_dp(): lax.ppermute(value, 'dp', [(one, one ^ mask) for one in range(devices)])  78 us
    pallas_call x18, Pallas kernels, call(): pl.pallas_call(body, out_shape=list(out_shape), in_specs=[smem] * len(sca...  77.5 us
    unnamed x181, local copies, waits for them, and re-layouts  31.8 us
    all_to_all x2, starting transfers between devices, deal(): lax.all_to_all(value.reshape(devices, rows // devices, width), 'dp', spli...  9.5 us
    all_to_all x2, starting transfers between devices, deal(): lax.all_to_all(jnp.take(first, order, axis=0), 'dp', split_axis=0, concat...  9.21 us
    slice x6, local copies, waits for them, and re-layouts, gather_lower(): left, right = (x_part[:rows], y_part[rows:])  8.75 us
    pallas_call x3, Pallas kernels, merge_quarters(): pl.pallas_call(merge_body, out_shape=[low_shape(*x_part.shape), low_shape...  7.66 us
  transfers between devices with their start and end apart: 70, of which 20 were waited for; matrix products, arithmetic and copies ran while one was open for 9% of the time, Pallas kernels for 19%

profile of v3, /device:TPU:0, one launch (start us, length us, event | category | flops | bytes accessed | tf_op | source)
XLA Modules:
  0.0 372.4 jit_solution(881187771893006517)
XLA Ops:
  4.1 5.0 %collective-permute-start = (bf16[64,2048]{1,0:T(8,128)(2,1)S(1)}, bf16[64,2048]{1,0:T(8,128)(2,1)S(1)}, u32[]{:S(2)}, u32[]{:S(2)}) collective-permute-start(bf16[64,2048]{1,0:T(8,128)(2,1)S(1)} %constant_dynamic-update-slice_fusion.refs_0_), channel_id=1, source_target_pairs={{0,24},{2,26},{4,28},{6,30},{8,16},{10,18},{12,20},{14,22},{16,8},... | collective-permute-start | bytes 786440 | tf_op jit(solution)/shard_map/ppermute | solution.py:34
  9.2 7.2 %collective-permute-done.refs_1_ = bf16[64,2048]{1,0:T(8,128)(2,1)S(1)} collective-permute-done((bf16[64,2048]{1,0:T(8,128)(2,1)S(1)}, bf16[64,2048]{1,0:T(8,128)(2,1)S(1)}, u32[]{:S(2)}, u32[]{:S(2)}) %collective-permute-start) | collective-permute-done | bytes 262176 | tf_op jit(solution)/shard_map/ppermute | solution.py:34
  16.4 4.8 %collective-permute-done.1.refs_2_ = bf16[64,2048]{1,0:T(8,128)(2,1)S(1)} collective-permute-done((bf16[64,2048]{1,0:T(8,128)(2,1)S(1)}, bf16[64,2048]{1,0:T(8,128)(2,1)S(1)}, u32[]{:S(2)}, u32[]{:S(2)}) %collective-permute-start.1) | collective-permute-done | bytes 262176 | tf_op jit(solution)/shard_map/ppermute | solution.py:34
  26.6 4.3 %all-to-all-start = ((bf16[16,8,1024]{2,1,0:T(8,128)(2,1)}), bf16[16,8,1024]{2,1,0:T(8,128)(2,1)}, u32[]{:S(2)}, u32[]{:S(2)}) async-start(bf16[16,8,1024]{2,1,0:T(8,128)(2,1)} %dynamic-slice_bitcast_fusion), calls=%async_computation | async-start | bytes 524288 | tf_op jit(solution)/shard_map/all_to_all | solution.py:733
  35.9 3.4 collective-permute-start.11
  40.1 6.7 %collective-permute-done.11.refs_1_ = bf16[64,2048]{1,0:T(8,128)(2,1)S(1)} collective-permute-done((bf16[64,2048]{1,0:T(8,128)(2,1)S(1)}, bf16[64,2048]{1,0:T(8,128)(2,1)S(1)}, u32[]{:S(2)}, u32[]{:S(2)}) %collective-permute-start.11) | collective-permute-done | bytes 262176 | tf_op jit(solution)/shard_map/ppermute | solution.py:34
  46.9 2.7 collective-permute-done.12.refs_2_
  52.5 12.4 %collective-permute-done.13.refs_3_ = bf16[64,2048]{1,0:T(8,128)(2,1)S(1)} collective-permute-done((bf16[64,2048]{1,0:T(8,128)(2,1)S(1)}, bf16[64,2048]{1,0:T(8,128)(2,1)S(1)}, u32[]{:S(2)}, u32[]{:S(2)}) %collective-permute-start.13) | collective-permute-done | bytes 262176 | tf_op jit(solution)/shard_map/ppermute | solution.py:34
  70.4 1.9 slice.106
  72.3 2.0 collective-permute-start.8
  75.7 2.0 collective-permute-start.21
  79.8 3.2 prepare_body.1
  85.4 2.2 gather_fusion
  89.4 4.5 %all-to-all-start.1 = ((bf16[16,8,1024]{2,1,0:T(8,128)(2,1)}), bf16[16,8,1024]{2,1,0:T(8,128)(2,1)}, u32[]{:S(2)}, u32[]{:S(2)}) async-start(bf16[16,8,1024]{2,1,0:T(8,128)(2,1)} %broadcast_select_fusion.1), calls=%async_computation.1 | async-start | bytes 524288 | tf_op jit(solution)/shard_map/all_to_all | solution.py:736
  96.9 2.4 stack_body.6.refs_0_
  99.3 7.9 %self_forward_body.1 = (bf16[256,512]{1,0:T(8,128)(2,1)S(1)}, bf16[256,512]{1,0:T(8,128)(2,1)S(1)}, bf16[256,512]{1,0:T(8,128)(2,1)S(1)}, bf16[256,512]{1,0:T(8,128)(2,1)S(1)}, bf16[256,1024]{1,0:T(8,128)(2,1)S(1)}) custom-call(s32[1]{0:T(128)} %bitcast.length_ref, f32[8,512]{1,0:T(8,128)S(1)} %convolution_bitcast_fusion.bias_ref, ...), custom_call_target="tpu_custom_call" | custom-call | flops 1342177280 | bytes 1024 | tf_op jit(solution)/shard_map/self_forward_body/pallas_call | solution.py:214
  111.1 3.3 collective-permute-start.27
  118.9 6.4 %collective-permute-done.27.refs_6_ = bf16[256,1408]{1,0:T(8,128)(2,1)} collective-permute-done((bf16[256,1408]{1,0:T(8,128)(2,1)}, bf16[256,1408]{1,0:T(8,128)(2,1)}, u32[]{:S(2)}, u32[]{:S(2)}) %collective-permute-start.27) | collective-permute-done | bytes 720928 | tf_op jit(solution)/shard_map/ppermute | solution.py:34
  125.3 22.4 %collective-permute-done.17.refs_4_ = bf16[256,1024]{1,0:T(8,128)(2,1)S(1)} collective-permute-done((bf16[256,1024]{1,0:T(8,128)(2,1)S(1)}, bf16[256,1024]{1,0:T(8,128)(2,1)S(1)}, u32[]{:S(2)}, u32[]{:S(2)}) %collective-permute-start.17) | collective-permute-done | bytes 524320 | tf_op jit(solution)/shard_map/ppermute | solution.py:34
  149.7 2.9 memory_body.1
  152.7 6.4 %cross_forward_body.1 = (f32[256,1024]{1,0:T(8,128)S(1)}, bf16[256,1024]{1,0:T(8,128)(2,1)S(1)}, bf16[256,512]{1,0:T(8,128)(2,1)S(1)}, bf16[256,512]{1,0:T(8,128)(2,1)S(1)}, bf16[256,1024]{1,0:T(8,128)(2,1)S(1)}) custom-call(bf16[256,1024]{1,0:T(8,128)(2,1)S(1)} %copy-done.4, bf16[256,1024]{1,0:T(8,128)(2,1)S(1)} %copy-done.27, ...), custom_call_target="tpu_custom_call" | custom-call | flops 805306368 | bytes 1024 | tf_op jit(solution)/shard_map/cross_forward_body/pallas_call | solution.py:214
  165.0 2.0 collective-permute-done.28.refs_7_
  167.0 8.0 %collective-permute-done.29.refs_8_ = bf16[256,1408]{1,0:T(8,128)(2,1)S(1)} collective-permute-done((bf16[256,1408]{1,0:T(8,128)(2,1)}, bf16[256,1408]{1,0:T(8,128)(2,1)S(1)}, u32[]{:S(2)}, u32[]{:S(2)}) %collective-permute-start.29) | collective-permute-done | bytes 720928 | tf_op jit(solution)/shard_map/ppermute | solution.py:34
  175.9 14.8 %feed_body.1 = (f32[256,1024]{1,0:T(8,128)}, bf16[256,1024]{1,0:T(8,128)(2,1)}, bf16[256,1024]{1,0:T(8,128)(2,1)S(1)}, bf16[512,1408]{1,0:T(8,128)(2,1)}, bf16[5...) custom-call(f32[256,1024]{1,0:T(8,128)} %copy-done.41, ...), custom_call_target="tpu_custom_call" | custom-call | flops 6643777536 | bytes 1024 | tf_op jit(solution)/shard_map/feed_body/pallas_call | solution.py:214
  196.6 11.7 %cross_backward_body.1 = (f32[256,1024]{1,0:T(8,128)S(1)}, f32[1,1024]{1,0:T(1,128)S(1)}, bf16[256,1024]{1,0:T(8,128)(2,1)S(1)}, bf16[128,1024]{1,0:T(8,128)(2,1...) custom-call(f32[256,1024]{1,0:T(8,128)} %get-tuple-element.146.hidde, ...), custom_call_target="tpu_custom_call" | custom-call | flops 2415919104 | bytes 1024 | tf_op jit(solution)/shard_map/cross_backward_body/pallas_call | solution.py:214
  213.8 2.7 merge_body.3
  219.5 3.3 collective-permute-start.52
  224.7 12.8 %self_backward_body.1 = (f32[256,1024]{1,0:T(8,128)S(1)}, f32[1,1024]{1,0:T(1,128)S(1)}, bf16[256,1024]{1,0:T(8,128)(2,1)S(1)}, f32[8,512]{1,0:T(8,128)S(1)}, bf...) custom-call(s32[1]{0:T(128)} %bitcast.length_ref, ...), custom_call_target="tpu_custom_call" | custom-call | flops 2684354560 | bytes 1024 | tf_op jit(solution)/shard_map/self_backward_body/pallas_call | solution.py:214
  242.1 9.3 %collective-permute-done.41.refs_1_ = bf16[512,1408]{1,0:T(8,128)(2,1)S(1)} collective-permute-done((bf16[512,1408]{1,0:T(8,128)(2,1)}, bf16[512,1408]{1,0:T(8,128)(2,1)S(1)}, u32[]{:S(2)}, u32[]{:S(2)}) %collective-permute-start.41) | collective-permute-done | bytes 1441824 | tf_op jit(solution)/shard_map/ppermute | solution.py:34
  256.9 5.2 %all-to-all-start.2 = ((bf16[16,8,1024]{2,1,0:T(8,128)(2,1)}), bf16[16,8,1024]{2,1,0:T(8,128)(2,1)}, u32[]{:S(2)}, u32[]{:S(2)}) async-start(bf16[16,8,1024]{2,1,0:T(8,128)(2,1)} %bitcast.7), calls=%async_computation.2 | async-start | bytes 524288 | tf_op jit(solution)/shard_map/all_to_all | solution.py:733
  262.1 2.5 merge_body.5
  265.8 4.5 %finish_body.1 = (bf16[256,1024]{1,0:T(8,128)(2,1)}, f32[3,1024]{1,0:T(4,128)S(1)}, f32[32,8]{1,0:T(8,128)S(1)}) custom-call(s32[1]{0:T(128)} %bitcast.length_ref, bf16[1024,1024]{1,0:T(8,128)(2,1)S(1)} %get-tuple-element.122.permute_ref, bf16[256,1024]{1,0:T(8,128)(2,1)S(1)} %copy-done.5, bf16[256,1024]{1,0:T(8,128)(2,1)S(1)} %get-tuple-element.168.mine_ref, ...), custom_call_target="tpu_custom_call" | custom-call | flops 536870912 | bytes 1024 | tf_op jit(solution)/shard_map/finish_body/pallas_call | solution.py:214
  270.5 1.9 collective-permute-start.53
  275.4 2.0 add_convert_fusion.1
  277.4 2.4 collective-permute-start.55
  280.4 3.4 output_body.1
  285.4 13.3 %collective-permute-done.37 = f32[26,128]{1,0:T(8,128)S(1)} collective-permute-done((f32[26,128]{1,0:T(8,128)S(1)}, f32[26,128]{1,0:T(8,128)S(1)}, u32[]{:S(2)}, u32[]{:S(2)}) %collective-permute-start.37) | collective-permute-done | bytes 13344 | tf_op jit(solution)/shard_map/ppermute | solution.py:34
  302.9 2.3 convert_add_fusion
  305.2 2.6 fold_body.5
  312.3 4.7 %all-to-all-start.3 = ((bf16[16,8,1024]{2,1,0:T(8,128)(2,1)}), bf16[16,8,1024]{2,1,0:T(8,128)(2,1)}, u32[]{:S(2)}, u32[]{:S(2)}) async-start(bf16[16,8,1024]{2,1,0:T(8,128)(2,1)} %broadcast_select_fusion), calls=%async_computation.3 | async-start | bytes 524288 | tf_op jit(solution)/shard_map/all_to_all | solution.py:736
  321.3 3.0 collective-permute-done.39
  326.0 2.5 merge_body.4
  335.1 2.0 collective-permute-start.63
  339.1 2.4 collective-permute-done.58
  342.7 8.2 %collective-permute-done.45.refs_1_ = bf16[512,1024]{1,0:T(8,128)(2,1)S(1)} collective-permute-done((bf16[512,1024]{1,0:T(8,128)(2,1)}, bf16[512,1024]{1,0:T(8,128)(2,1)S(1)}, u32[]{:S(2)}, u32[]{:S(2)}) %collective-permute-start.45) | collective-permute-done | bytes 1048608 | tf_op jit(solution)/shard_map/ppermute | solution.py:34
  355.7 5.7 %collective-permute-done.60 = bf16[64,2048]{1,0:T(8,128)(2,1)S(1)} collective-permute-done((bf16[64,2048]{1,0:T(8,128)(2,1)S(1)}, bf16[64,2048]{1,0:T(8,128)(2,1)S(1)}, u32[]{:S(2)}, u32[]{:S(2)}) %collective-permute-start.60) | collective-permute-done | bytes 262176 | tf_op jit(solution)/shard_map/ppermute | solution.py:34
  361.5 2.2 collective-permute-start.61
  365.4 4.4 %collective-permute-done.61 = bf16[64,2048]{1,0:T(8,128)(2,1)S(1)} collective-permute-done((bf16[64,2048]{1,0:T(8,128)(2,1)S(1)}, bf16[64,2048]{1,0:T(8,128)(2,1)S(1)}, u32[]{:S(2)}, u32[]{:S(2)}) %collective-permute-start.61) | collective-permute-done | bytes 262176 | tf_op jit(solution)/shard_map/ppermute | solution.py:34
  (348 shorter events, 116.6 us)
Async XLA Ops:
  26.6 58.8 %all-to-all-start = ((bf16[16,8,1024]{2,1,0:T(8,128)(2,1)}), bf16[16,8,1024]{2,1,0:T(8,128)(2,1)}, u32[]{:S(2)}, u32[]{:S(2)}) async-start(bf16[16,8,1024]{2,1,0:T(8,128)(2,1)} %dynamic-slice_bitcast_fusion), calls=%async_computation | async-start | bytes 524288 | tf_op jit(solution)/shard_map/all_to_all | solution.py:733
  32.4 32.6 %collective-permute-start.5 = (bf16[512,1024]{1,0:T(8,128)(2,1)S(1)}, bf16[512,1024]{1,0:T(8,128)(2,1)}, u32[]{:S(2)}, u32[]{:S(2)}) collective-permute-start(bf16[512,1024]{1,0:T(8,128)(2,1)S(1)} %stack_body.4.refs_0_), channel_id=1, source_target_pairs={{0,2},{2,0},{4,6},{6,4},{8,10},{10,8},{12,14},{14,12},{16,18},{18,... | collective-permute-start | bytes 3145736 | tf_op jit(solution)/shard_map/ppermute | solution.py:34
  34.3 30.8 %collective-permute-start.6 = (bf16[512,1024]{1,0:T(8,128)(2,1)S(1)}, bf16[512,1024]{1,0:T(8,128)(2,1)}, u32[]{:S(2)}, u32[]{:S(2)}) collective-permute-start(bf16[512,1024]{1,0:T(8,128)(2,1)S(1)} %stack_body.4.refs_0_), channel_id=1, source_target_pairs={{0,4},{2,6},{4,0},{6,2},{8,12},{10,14},{12,8},{14,10},{16,20},{18,... | collective-permute-start | bytes 3145736 | tf_op jit(solution)/shard_map/ppermute | solution.py:34
  49.6 15.4 %collective-permute-start.13 = (bf16[64,2048]{1,0:T(8,128)(2,1)S(1)}, bf16[64,2048]{1,0:T(8,128)(2,1)S(1)}, u32[]{:S(2)}, u32[]{:S(2)}) collective-permute-start(bf16[64,2048]{1,0:T(8,128)(2,1)S(1)} %collective-permute-done.11.refs_1_), channel_id=1, source_target_pairs={{0,8},{2,10},{4,12},{6,14},{8,0},{10,2},{12,4},{14,6},{16,24},{18,... | collective-permute-start | bytes 786440 | tf_op jit(solution)/shard_map/ppermute | solution.py:34
  51.4 20.9 %collective-permute-start.19 = (bf16[64,2816]{1,0:T(8,128)(2,1)S(1)}, bf16[64,2816]{1,0:T(8,128)(2,1)}, u32[]{:S(2)}, u32[]{:S(2)}) collective-permute-start(bf16[64,2816]{1,0:T(8,128)(2,1)S(1)} %pad_maximum_fusion.refs_0_), channel_id=1, source_target_pairs={{0,24},{2,26},{4,28},{6,30},{8,16},{10,18},{12,20},{14,22},{16,8},... | collective-permute-start | bytes 1081352 | tf_op jit(solution)/shard_map/ppermute | solution.py:34
  65.1 43.0 %collective-permute-start.15 = (bf16[512,1024]{1,0:T(8,128)(2,1)S(1)}, bf16[512,1024]{1,0:T(8,128)(2,1)}, u32[]{:S(2)}, u32[]{:S(2)}) collective-permute-start(bf16[512,1024]{1,0:T(8,128)(2,1)S(1)} %stack_body.5.refs_0_), channel_id=1, source_target_pairs={{0,4},{2,6},{4,0},{6,2},{8,12},{10,14},{12,8},{14,10},{16,20},{18,... | collective-permute-start | bytes 3145736 | tf_op jit(solution)/shard_map/ppermute | solution.py:34
  65.2 43.2 %collective-permute-start.14 = (bf16[512,1024]{1,0:T(8,128)(2,1)S(1)}, bf16[512,1024]{1,0:T(8,128)(2,1)}, u32[]{:S(2)}, u32[]{:S(2)}) collective-permute-start(bf16[512,1024]{1,0:T(8,128)(2,1)S(1)} %stack_body.5.refs_0_), channel_id=1, source_target_pairs={{0,2},{2,0},{4,6},{6,4},{8,10},{10,8},{12,14},{14,12},{16,18},{18,... | collective-permute-start | bytes 3145736 | tf_op jit(solution)/shard_map/ppermute | solution.py:34
  68.6 30.7 %collective-permute-start.7 = (bf16[256,1024]{1,0:T(8,128)(2,1)}, bf16[256,1024]{1,0:T(8,128)(2,1)}, u32[]{:S(2)}, u32[]{:S(2)}) collective-permute-start(bf16[256,1024]{1,0:T(8,128)(2,1)} %slice.105), channel_id=1, source_target_pairs={{0,4},{2,6},{4,0},{6,2},{8,12},{10,14},{12,8},{14,10},{16,20},{18,... | collective-permute-start | bytes 1572872 | tf_op jit(solution)/shard_map/ppermute | solution.py:34
  72.3 26.9 %collective-permute-start.8 = (bf16[256,1024]{1,0:T(8,128)(2,1)}, bf16[256,1024]{1,0:T(8,128)(2,1)}, u32[]{:S(2)}, u32[]{:S(2)}) collective-permute-start(bf16[256,1024]{1,0:T(8,128)(2,1)} %slice.106), channel_id=1, source_target_pairs={{0,2},{2,0},{4,6},{6,4},{8,10},{10,8},{12,14},{14,12},{16,18},{18,... | collective-permute-start | bytes 1572872 | tf_op jit(solution)/shard_map/ppermute | solution.py:34
  75.7 18.3 %collective-permute-start.21 = (bf16[64,2816]{1,0:T(8,128)(2,1)}, bf16[64,2816]{1,0:T(8,128)(2,1)}, u32[]{:S(2)}, u32[]{:S(2)}) collective-permute-start(bf16[64,2816]{1,0:T(8,128)(2,1)} %collective-permute-done.19.refs_1_), channel_id=1, source_target_pairs={{0,8},{2,10},{4,12},{6,14},{8,0},{10,2},{12,4},{14,6},{16,24},{18,... | collective-permute-start | bytes 1081352 | tf_op jit(solution)/shard_map/ppermute | solution.py:34
  89.4 25.0 %all-to-all-start.1 = ((bf16[16,8,1024]{2,1,0:T(8,128)(2,1)}), bf16[16,8,1024]{2,1,0:T(8,128)(2,1)}, u32[]{:S(2)}, u32[]{:S(2)}) async-start(bf16[16,8,1024]{2,1,0:T(8,128)(2,1)} %broadcast_select_fusion.1), calls=%async_computation.1 | async-start | bytes 524288 | tf_op jit(solution)/shard_map/all_to_all | solution.py:736
  93.9 16.2 %collective-permute-start.26 = (bf16[64,1408]{1,0:T(8,128)(2,1)}, bf16[64,1408]{1,0:T(8,128)(2,1)S(1)}, u32[]{:S(2)}, u32[]{:S(2)}) collective-permute-start(bf16[64,1408]{1,0:T(8,128)(2,1)} %copy-done.37), channel_id=1, source_target_pairs={{0,4},{2,6},{4,0},{6,2},{8,12},{10,14},{12,8},{14,10},{16,20},{18,... | collective-permute-start | bytes 540680 | tf_op jit(solution)/shard_map/ppermute | solution.py:34
  108.1 51.1 %collective-permute-start.23 = (bf16[512,1408]{1,0:T(8,128)(2,1)}, bf16[512,1408]{1,0:T(8,128)(2,1)}, u32[]{:S(2)}, u32[]{:S(2)}) collective-permute-start(bf16[512,1408]{1,0:T(8,128)(2,1)} %stack_body.6.refs_0_), channel_id=1, source_target_pairs={{0,4},{2,6},{4,0},{6,2},{8,12},{10,14},{12,8},{14,10},{16,20},{18,... | collective-permute-start | bytes 4325384 | tf_op jit(solution)/shard_map/ppermute | solution.py:34
  108.4 53.9 %collective-permute-start.22 = (bf16[512,1408]{1,0:T(8,128)(2,1)}, bf16[512,1408]{1,0:T(8,128)(2,1)}, u32[]{:S(2)}, u32[]{:S(2)}) collective-permute-start(bf16[512,1408]{1,0:T(8,128)(2,1)} %stack_body.6.refs_0_), channel_id=1, source_target_pairs={{0,2},{2,0},{4,6},{6,4},{8,10},{10,8},{12,14},{14,12},{16,18},{18,... | collective-permute-start | bytes 4325384 | tf_op jit(solution)/shard_map/ppermute | solution.py:34
  111.1 14.2 %collective-permute-start.27 = (bf16[256,1408]{1,0:T(8,128)(2,1)}, bf16[256,1408]{1,0:T(8,128)(2,1)}, u32[]{:S(2)}, u32[]{:S(2)}) collective-permute-start(bf16[256,1408]{1,0:T(8,128)(2,1)} %stack_body.7.refs_5_), channel_id=1, source_target_pairs={{0,24},{2,26},{4,28},{6,30},{8,16},{10,18},{12,20},{14,22},{16,8},... | collective-permute-start | bytes 2162696 | tf_op jit(solution)/shard_map/ppermute | solution.py:34
  115.6 32.1 %collective-permute-start.17 = (bf16[256,1024]{1,0:T(8,128)(2,1)S(1)}, bf16[256,1024]{1,0:T(8,128)(2,1)S(1)}, u32[]{:S(2)}, u32[]{:S(2)}) collective-permute-start(bf16[256,1024]{1,0:T(8,128)(2,1)S(1)} %slice.108), channel_id=1, source_target_pairs={{0,2},{2,0},{4,6},{6,4},{8,10},{10,8},{12,14},{14,12},{16,18},{18,... | collective-permute-start | bytes 1572872 | tf_op jit(solution)/shard_map/ppermute | solution.py:34
  117.3 31.9 %collective-permute-start.16 = (bf16[256,1024]{1,0:T(8,128)(2,1)S(1)}, bf16[256,1024]{1,0:T(8,128)(2,1)S(1)}, u32[]{:S(2)}, u32[]{:S(2)}) collective-permute-start(bf16[256,1024]{1,0:T(8,128)(2,1)S(1)} %slice.107), channel_id=1, source_target_pairs={{0,4},{2,6},{4,0},{6,2},{8,12},{10,14},{12,8},{14,10},{16,20},{18,... | collective-permute-start | bytes 1572872 | tf_op jit(solution)/shard_map/ppermute | solution.py:34
  125.3 27.4 %collective-permute-start.9 = (bf16[256,1024]{1,0:T(8,128)(2,1)S(1)}, bf16[256,1024]{1,0:T(8,128)(2,1)S(1)}, u32[]{:S(2)}, u32[]{:S(2)}) collective-permute-start(bf16[256,1024]{1,0:T(8,128)(2,1)S(1)} %copy-done.27), channel_id=1, source_target_pairs={{0,1},{1,0},{2,3},{3,2},{4,5},{5,4},{6,7},{7,6},{8,9},{9,8},{10,11... | collective-permute-start | bytes 1572872 | tf_op jit(solution)/shard_map/ppermute | solution.py:38
  147.7 19.3 %collective-permute-start.28 = (bf16[256,1408]{1,0:T(8,128)(2,1)}, bf16[256,1408]{1,0:T(8,128)(2,1)S(1)}, u32[]{:S(2)}, u32[]{:S(2)}) collective-permute-start(bf16[256,1408]{1,0:T(8,128)(2,1)} %stack_body.7.refs_5_), channel_id=1, source_target_pairs={{0,8},{2,10},{4,12},{6,14},{8,0},{10,2},{12,4},{14,6},{16,24},{18,... | collective-permute-start | bytes 2162696 | tf_op jit(solution)/shard_map/ppermute | solution.py:34
  149.2 25.8 %collective-permute-start.29 = (bf16[256,1408]{1,0:T(8,128)(2,1)}, bf16[256,1408]{1,0:T(8,128)(2,1)S(1)}, u32[]{:S(2)}, u32[]{:S(2)}) collective-permute-start(bf16[256,1408]{1,0:T(8,128)(2,1)} %collective-permute-done.27.refs_6_), channel_id=1, source_target_pairs={{0,8},{2,10},{4,12},{6,14},{8,0},{10,2},{12,4},{14,6},{16,24},{18,... | collective-permute-start | bytes 2162696 | tf_op jit(solution)/shard_map/ppermute | solution.py:34
  160.7 14.3 %collective-permute-start.25 = (bf16[256,1408]{1,0:T(8,128)(2,1)S(1)}, bf16[256,1408]{1,0:T(8,128)(2,1)S(1)}, u32[]{:S(2)}, u32[]{:S(2)}) collective-permute-start(bf16[256,1408]{1,0:T(8,128)(2,1)S(1)} %slice.110), channel_id=1, source_target_pairs={{0,2},{2,0},{4,6},{6,4},{8,10},{10,8},{12,14},{14,12},{16,18},{18,... | collective-permute-start | bytes 2162696 | tf_op jit(solution)/shard_map/ppermute | solution.py:34
  192.4 19.7 %collective-permute-start.34 = (bf16[256,1408]{1,0:T(8,128)(2,1)S(1)}, bf16[256,1408]{1,0:T(8,128)(2,1)S(1)}, u32[]{:S(2)}, u32[]{:S(2)}) collective-permute-start(bf16[256,1408]{1,0:T(8,128)(2,1)S(1)} %get-tuple-element.159), channel_id=1, source_target_pairs={{0,2},{2,0},{4,6},{6,4},{8,10},{10,8},{12,14},{14,12},{16,18},{18,... | collective-permute-start | bytes 2162696 | tf_op jit(solution)/shard_map/ppermute | solution.py:34
  193.6 18.4 %collective-permute-start.33 = (bf16[256,1408]{1,0:T(8,128)(2,1)S(1)}, bf16[256,1408]{1,0:T(8,128)(2,1)S(1)}, u32[]{:S(2)}, u32[]{:S(2)}) collective-permute-start(bf16[256,1408]{1,0:T(8,128)(2,1)S(1)} %get-tuple-element.157), channel_id=1, source_target_pairs={{0,4},{2,6},{4,0},{6,2},{8,12},{10,14},{12,8},{14,10},{16,20},{18,... | collective-permute-start | bytes 2162696 | tf_op jit(solution)/shard_map/ppermute | solution.py:34
  195.1 23.1 %collective-permute-start.51 = (bf16[256,1408]{1,0:T(8,128)(2,1)}, bf16[256,1408]{1,0:T(8,128)(2,1)}, u32[]{:S(2)}, u32[]{:S(2)}) collective-permute-start(bf16[256,1408]{1,0:T(8,128)(2,1)} %get-tuple-element.206), channel_id=1, source_target_pairs={{0,8},{2,10},{4,12},{6,14},{8,0},{10,2},{12,4},{14,6},{16,24},{18,... | collective-permute-start | bytes 2162696 | tf_op jit(solution)/shard_map/ppermute | solution.py:34
  216.6 34.8 %collective-permute-start.41 = (bf16[512,1408]{1,0:T(8,128)(2,1)}, bf16[512,1408]{1,0:T(8,128)(2,1)S(1)}, u32[]{:S(2)}, u32[]{:S(2)}) collective-permute-start(bf16[512,1408]{1,0:T(8,128)(2,1)} %get-tuple-element.161), channel_id=1, source_target_pairs={{0,2},{2,0},{4,6},{6,4},{8,10},{10,8},{12,14},{14,12},{16,18},{18,... | collective-permute-start | bytes 4325384 | tf_op jit(solution)/shard_map/ppermute | solution.py:34
  217.2 34.7 %collective-permute-start.42 = (bf16[512,1408]{1,0:T(8,128)(2,1)}, bf16[512,1408]{1,0:T(8,128)(2,1)S(1)}, u32[]{:S(2)}, u32[]{:S(2)}) collective-permute-start(bf16[512,1408]{1,0:T(8,128)(2,1)} %get-tuple-element.162), channel_id=1, source_target_pairs={{0,4},{2,6},{4,0},{6,2},{8,12},{10,14},{12,8},{14,10},{16,20},{18,... | collective-permute-start | bytes 4325384 | tf_op jit(solution)/shard_map/ppermute | solution.py:34
  219.5 33.5 %collective-permute-start.52 = (bf16[256,1408]{1,0:T(8,128)(2,1)S(1)}, bf16[256,1408]{1,0:T(8,128)(2,1)S(1)}, u32[]{:S(2)}, u32[]{:S(2)}) collective-permute-start(bf16[256,1408]{1,0:T(8,128)(2,1)S(1)} %add_convert_fusion), channel_id=1, source_target_pairs={{0,24},{2,26},{4,28},{6,30},{8,16},{10,18},{12,20},{14,22},{16,8},... | collective-permute-start | bytes 2162696 | tf_op jit(solution)/shard_map/ppermute | solution.py:34
  223.0 39.2 %collective-permute-start.48 = (bf16[256,1024]{1,0:T(8,128)(2,1)}, bf16[256,1024]{1,0:T(8,128)(2,1)}, u32[]{:S(2)}, u32[]{:S(2)}) collective-permute-start(bf16[256,1024]{1,0:T(8,128)(2,1)} %get-tuple-element.195), channel_id=1, source_target_pairs={{0,2},{2,0},{4,6},{6,4},{8,10},{10,8},{12,14},{14,12},{16,18},{18,... | collective-permute-start | bytes 1572872 | tf_op jit(solution)/shard_map/ppermute | solution.py:34
  223.9 38.2 %collective-permute-start.47 = (bf16[256,1024]{1,0:T(8,128)(2,1)}, bf16[256,1024]{1,0:T(8,128)(2,1)}, u32[]{:S(2)}, u32[]{:S(2)}) collective-permute-start(bf16[256,1024]{1,0:T(8,128)(2,1)} %get-tuple-element.193), channel_id=1, source_target_pairs={{0,4},{2,6},{4,0},{6,2},{8,12},{10,14},{12,8},{14,10},{16,20},{18,... | collective-permute-start | bytes 1572872 | tf_op jit(solution)/shard_map/ppermute | solution.py:34
  251.4 13.2 %collective-permute-start.35 = (bf16[256,1024]{1,0:T(8,128)(2,1)S(1)}, bf16[256,1024]{1,0:T(8,128)(2,1)}, u32[]{:S(2)}, u32[]{:S(2)}) collective-permute-start(bf16[256,1024]{1,0:T(8,128)(2,1)S(1)} %get-tuple-element.168.mine_ref), channel_id=1, source_target_pairs={{0,1},{1,0},{2,3},{3,2},{4,5},{5,4},{6,7},{7,6},{8,9},{9,8},{10,11... | collective-permute-start | bytes 1572872 | tf_op jit(solution)/shard_map/ppermute | solution.py:38
  254.1 21.3 %collective-permute-start.54 = (bf16[64,2816]{1,0:T(8,128)(2,1)}, bf16[64,2816]{1,0:T(8,128)(2,1)}, u32[]{:S(2)}, u32[]{:S(2)}) collective-permute-start(bf16[64,2816]{1,0:T(8,128)(2,1)} %get-tuple-element.210), channel_id=1, source_target_pairs={{0,8},{2,10},{4,12},{6,14},{8,0},{10,2},{12,4},{14,6},{16,24},{18,... | collective-permute-start | bytes 1081352 | tf_op jit(solution)/shard_map/ppermute | solution.py:34
  255.1 24.6 %collective-permute-start.30 = (bf16[256,1024]{1,0:T(8,128)(2,1)}, bf16[256,1024]{1,0:T(8,128)(2,1)}, u32[]{:S(2)}, u32[]{:S(2)}) collective-permute-start(bf16[256,1024]{1,0:T(8,128)(2,1)} %get-tuple-element.147.mine_ref), channel_id=1, source_target_pairs={{0,1},{1,0},{2,3},{3,2},{4,5},{5,4},{6,7},{7,6},{8,9},{9,8},{10,11... | collective-permute-start | bytes 1572872 | tf_op jit(solution)/shard_map/ppermute | solution.py:38
  256.9 26.8 %all-to-all-start.2 = ((bf16[16,8,1024]{2,1,0:T(8,128)(2,1)}), bf16[16,8,1024]{2,1,0:T(8,128)(2,1)}, u32[]{:S(2)}, u32[]{:S(2)}) async-start(bf16[16,8,1024]{2,1,0:T(8,128)(2,1)} %bitcast.7), calls=%async_computation.2 | async-start | bytes 524288 | tf_op jit(solution)/shard_map/all_to_all | solution.py:733
  270.5 28.8 %collective-permute-start.53 = (bf16[64,2816]{1,0:T(8,128)(2,1)}, bf16[64,2816]{1,0:T(8,128)(2,1)}, u32[]{:S(2)}, u32[]{:S(2)}) collective-permute-start(bf16[64,2816]{1,0:T(8,128)(2,1)} %copy-done.49), channel_id=1, source_target_pairs={{0,8},{2,10},{4,12},{6,14},{8,0},{10,2},{12,4},{14,6},{16,24},{18,... | collective-permute-start | bytes 1081352 | tf_op jit(solution)/shard_map/ppermute | solution.py:34
  272.4 29.0 %collective-permute-start.50 = (bf16[512,1024]{1,0:T(8,128)(2,1)}, bf16[512,1024]{1,0:T(8,128)(2,1)}, u32[]{:S(2)}, u32[]{:S(2)}) collective-permute-start(bf16[512,1024]{1,0:T(8,128)(2,1)} %get-tuple-element.199), channel_id=1, source_target_pairs={{0,4},{2,6},{4,0},{6,2},{8,12},{10,14},{12,8},{14,10},{16,20},{18,... | collective-permute-start | bytes 3145736 | tf_op jit(solution)/shard_map/ppermute | solution.py:34
  273.9 31.3 %collective-permute-start.49 = (bf16[512,1024]{1,0:T(8,128)(2,1)}, bf16[512,1024]{1,0:T(8,128)(2,1)}, u32[]{:S(2)}, u32[]{:S(2)}) collective-permute-start(bf16[512,1024]{1,0:T(8,128)(2,1)} %get-tuple-element.197), channel_id=1, source_target_pairs={{0,2},{2,0},{4,6},{6,4},{8,10},{10,8},{12,14},{14,12},{16,18},{18,... | collective-permute-start | bytes 3145736 | tf_op jit(solution)/shard_map/ppermute | solution.py:34
  277.4 22.4 %collective-permute-start.55 = (bf16[64,2816]{1,0:T(8,128)(2,1)}, bf16[64,2816]{1,0:T(8,128)(2,1)}, u32[]{:S(2)}, u32[]{:S(2)}) collective-permute-start(bf16[64,2816]{1,0:T(8,128)(2,1)} %add_convert_fusion.1), channel_id=1, source_target_pairs={{0,24},{2,26},{4,28},{6,30},{8,16},{10,18},{12,20},{14,22},{16,8},... | collective-permute-start | bytes 1081352 | tf_op jit(solution)/shard_map/ppermute | solution.py:34
  279.7 19.0 %collective-permute-start.37 = (f32[26,128]{1,0:T(8,128)S(1)}, f32[26,128]{1,0:T(8,128)S(1)}, u32[]{:S(2)}, u32[]{:S(2)}) collective-permute-start(f32[26,128]{1,0:T(8,128)S(1)} %maximum_bitcast_fusion), channel_id=1, source_target_pairs={{0,2},{2,0},{4,6},{6,4},{8,10},{10,8},{12,14},{14,12},{16,18},{18,... | collective-permute-start | bytes 39944 | tf_op jit(solution)/shard_map/ppermute | solution.py:34
  298.7 20.0 %collective-permute-start.62 = (bf16[256,1408]{1,0:T(8,128)(2,1)}, bf16[256,1408]{1,0:T(8,128)(2,1)S(1)}, u32[]{:S(2)}, u32[]{:S(2)}) collective-permute-start(bf16[256,1408]{1,0:T(8,128)(2,1)} %copy-done.42), channel_id=1, source_target_pairs={{0,8},{2,10},{4,12},{6,14},{8,0},{10,2},{12,4},{14,6},{16,24},{18,... | collective-permute-start | bytes 2162696 | tf_op jit(solution)/shard_map/ppermute | solution.py:34
  299.8 26.2 %collective-permute-start.44 = (bf16[256,1024]{1,0:T(8,128)(2,1)}, bf16[256,1024]{1,0:T(8,128)(2,1)}, u32[]{:S(2)}, u32[]{:S(2)}) collective-permute-start(bf16[256,1024]{1,0:T(8,128)(2,1)} %copy-done.46), channel_id=1, source_target_pairs={{0,2},{2,0},{4,6},{6,4},{8,10},{10,8},{12,14},{14,12},{16,18},{18,... | collective-permute-start | bytes 1572872 | tf_op jit(solution)/shard_map/ppermute | solution.py:34
  301.4 24.6 %collective-permute-start.43 = (bf16[256,1024]{1,0:T(8,128)(2,1)}, bf16[256,1024]{1,0:T(8,128)(2,1)}, u32[]{:S(2)}, u32[]{:S(2)}) collective-permute-start(bf16[256,1024]{1,0:T(8,128)(2,1)} %copy-done.45), channel_id=1, source_target_pairs={{0,4},{2,6},{4,0},{6,2},{8,12},{10,14},{12,8},{14,10},{16,20},{18,... | collective-permute-start | bytes 1572872 | tf_op jit(solution)/shard_map/ppermute | solution.py:34
  309.4 21.1 %collective-permute-start.57 = (bf16[64,2048]{1,0:T(8,128)(2,1)}, bf16[64,2048]{1,0:T(8,128)(2,1)S(1)}, u32[]{:S(2)}, u32[]{:S(2)}) collective-permute-start(bf16[64,2048]{1,0:T(8,128)(2,1)} %get-tuple-element.214), channel_id=1, source_target_pairs={{0,8},{2,10},{4,12},{6,14},{8,0},{10,2},{12,4},{14,6},{16,24},{18,... | collective-permute-start | bytes 786440 | tf_op jit(solution)/shard_map/ppermute | solution.py:34
  310.9 13.4 %collective-permute-start.39 = (f32[26,128]{1,0:T(8,128)S(1)}, f32[26,128]{1,0:T(8,128)S(1)}, u32[]{:S(2)}, u32[]{:S(2)}) collective-permute-start(f32[26,128]{1,0:T(8,128)S(1)} %fusion.8), channel_id=1, source_target_pairs={{0,8},{2,10},{4,12},{6,14},{8,0},{10,2},{12,4},{14,6},{16,24},{18,... | collective-permute-start | bytes 39944 | tf_op jit(solution)/shard_map/ppermute | solution.py:34
  312.3 26.2 %all-to-all-start.3 = ((bf16[16,8,1024]{2,1,0:T(8,128)(2,1)}), bf16[16,8,1024]{2,1,0:T(8,128)(2,1)}, u32[]{:S(2)}, u32[]{:S(2)}) async-start(bf16[16,8,1024]{2,1,0:T(8,128)(2,1)} %broadcast_select_fusion), calls=%async_computation.3 | async-start | bytes 524288 | tf_op jit(solution)/shard_map/all_to_all | solution.py:736
  328.5 22.4 %collective-permute-start.45 = (bf16[512,1024]{1,0:T(8,128)(2,1)}, bf16[512,1024]{1,0:T(8,128)(2,1)S(1)}, u32[]{:S(2)}, u32[]{:S(2)}) collective-permute-start(bf16[512,1024]{1,0:T(8,128)(2,1)} %get-tuple-element.185), channel_id=1, source_target_pairs={{0,2},{2,0},{4,6},{6,4},{8,10},{10,8},{12,14},{14,12},{16,18},{18,... | collective-permute-start | bytes 3145736 | tf_op jit(solution)/shard_map/ppermute | solution.py:34
  329.9 22.1 %collective-permute-start.46 = (bf16[512,1024]{1,0:T(8,128)(2,1)}, bf16[512,1024]{1,0:T(8,128)(2,1)S(1)}, u32[]{:S(2)}, u32[]{:S(2)}) collective-permute-start(bf16[512,1024]{1,0:T(8,128)(2,1)} %get-tuple-element.186), channel_id=1, source_target_pairs={{0,4},{2,6},{4,0},{6,2},{8,12},{10,14},{12,8},{14,10},{16,20},{18,... | collective-permute-start | bytes 3145736 | tf_op jit(solution)/shard_map/ppermute | solution.py:34
  335.1 18.9 %collective-permute-start.63 = (bf16[64,1408]{1,0:T(8,128)(2,1)}, bf16[64,1408]{1,0:T(8,128)(2,1)S(1)}, u32[]{:S(2)}, u32[]{:S(2)}) collective-permute-start(bf16[64,1408]{1,0:T(8,128)(2,1)} %get-tuple-element.222), channel_id=1, source_target_pairs={{0,4},{2,6},{4,0},{6,2},{8,12},{10,14},{12,8},{14,10},{16,20},{18,... | collective-permute-start | bytes 540680 | tf_op jit(solution)/shard_map/ppermute | solution.py:34
  338.4 15.5 %collective-permute-start.65 = (bf16[64,1408]{1,0:T(8,128)(2,1)}, bf16[64,1408]{1,0:T(8,128)(2,1)S(1)}, u32[]{:S(2)}, u32[]{:S(2)}) collective-permute-start(bf16[64,1408]{1,0:T(8,128)(2,1)} %add_convert_fusion.4), channel_id=1, source_target_pairs={{0,2},{2,0},{4,6},{6,4},{8,10},{10,8},{12,14},{14,12},{16,18},{18,... | collective-permute-start | bytes 540680 | tf_op jit(solution)/shard_map/ppermute | solution.py:34
  (109 other events, 918.0 us)
